TPU v7x, 32 devices: a whole 2x2x4 slice. The times are simulated.
32 devices in a mesh: dp: 8 (over z, y), tensor: 4 (over x, core).
Axes of the slice: x: 2, y: 2, z: 4, core: 2. Of those that a mesh axis runs over, the one named last changes fastest.
Arguments:
- tokens: bfloat16 [8192, 1024], P(('dp', 'tensor')), may hold values from -6 to 6
- cotangent: bfloat16 [8192, 1024], P(('dp', 'tensor')), may hold values from -6 to 6
- attn_gain: float32 [1024], replicated, may hold values from 0.1 to 1.9
- q_gain: float32 [128], replicated, may hold values from 0.1 to 1.9
- k_gain: float32 [128], replicated, may hold values from 0.1 to 1.9
- mlp_gain: float32 [1024], replicated, may hold values from 0.1 to 1.9
- w_query: bfloat16 [1024, 2048], P(None, 'tensor'), may hold values from -0.1875 to 0.1875
- key_weight: bfloat16 [1024, 1024], P(None, 'tensor'), may hold values from -0.1875 to 0.1875
- value_weight: bfloat16 [1024, 1024], P(None, 'tensor'), may hold values from -0.1875 to 0.1875
- w_out: bfloat16 [2048, 1024], P('tensor'), may hold values from -0.75 to 0.75
- w_gate: bfloat16 [1024, 3072], P(None, 'tensor'), may hold values from -0.1875 to 0.1875
- w_up: bfloat16 [1024, 3072], P(None, 'tensor'), may hold values from -0.1875 to 0.1875
- w_down: bfloat16 [3072, 1024], P('tensor'), may hold values from -0.109375 to 0.109375
- lengths: int32 [8], P('dp'), may hold values from 512 to 1024, as said below
Outputs:
- layer_out: float32 [8192, 1024], P(('dp', 'tensor'))
- tokens_grad: float32 [8192, 1024], P(('dp', 'tensor'))
- attn_gain_grad: float32 [1024], replicated
- q_gain_grad: float32 [128], replicated
- k_gain_grad: float32 [128], replicated
- mlp_gain_grad: float32 [1024], replicated
- w_query_grad: float32 [1024, 2048], P(None, 'tensor')
- w_key_grad: float32 [1024, 1024], P(None, 'tensor')
- w_value_grad: float32 [1024, 1024], P(None, 'tensor')
- w_out_grad: float32 [2048, 1024], P('tensor')
- w_gate_grad: float32 [1024, 3072], P(None, 'tensor')
- w_up_grad: float32 [1024, 3072], P(None, 'tensor')
- w_down_grad: float32 [3072, 1024], P('tensor')
Inputs may be any that keep to these rules, and one draw needn't show every extreme that they name: Sequence s fills rows 0 to lengths[s] - 1 of the 1024 rows of index s of dp; the other rows are padding. Some sequence has exactly 1024 tokens.
All inputs are finite; a program needn't handle non-finite values.
Results may differ from a plain program's by a relative error of at most 0.014.
Values may be sent and summed in bfloat16 or wider, within the bound.
No kernel may reach another device: no remote copies, remote signals or barrier semaphores. Data moves between devices by JAX's collectives and lax.ppermute only.
A program may use at most 128 MiB of HBM per device.

v0:
```python
import jax
import jax.numpy as jnp
from jax import lax
from jax.sharding import PartitionSpec as P

HEAD_SIZE = 128
QBLOCK = 512


epsilon = 1e-06
rotary_base = 1000000.0
masked_score = -1e30


def rms_norm(values, gain):
    return values * lax.rsqrt(jnp.mean(values * values, axis=-1, keepdims=True) + epsilon) * gain


def rotary(values):
    every_row = values.shape[0]
    half_width = HEAD_SIZE // 2
    frequency = rotary_base ** (-(jnp.arange(half_width, dtype=jnp.float32) * 2.0) / HEAD_SIZE)
    angles = jnp.arange(every_row, dtype=jnp.float32)[:, None] * frequency[None, :]
    cosine = jnp.concatenate([jnp.cos(angles), jnp.cos(angles)], axis=-1)[:, None, :]
    sine_table = jnp.concatenate([jnp.sin(angles), jnp.sin(angles)], axis=-1)[:, None, :]
    first = values[..., :half_width]
    second = values[..., half_width:]
    turned = jnp.concatenate([-second, first], axis=-1)
    return values * cosine + turned * sine_table


def shaped(raw_rows, gain, head_count):
    return rotary(rms_norm(raw_rows.reshape(raw_rows.shape[0], head_count, HEAD_SIZE), gain))


def swiglu(gate_proj, up_proj):
    return gate_proj / (1.0 + jnp.exp(-gate_proj)) * up_proj


def spread(values):
    return lax.all_gather(values, "tensor", axis=0, tiled=True)


def settle(values):
    return lax.psum_scatter(values, "tensor", scatter_dimension=0, tiled=True)


def spread_grad(values):
    return lax.all_gather(values, "tensor", axis=0, tiled=True)


def settle_grad(values):
    return lax.psum_scatter(values, "tensor", scatter_dimension=0, tiled=True)


def body(
    tokens,
    cotangent,
    attn_gain,
    q_gain,
    k_gain,
    mlp_gain,
    w_query,
    key_weight,
    value_weight,
    w_out,
    w_gate,
    w_up,
    w_down,
    lengths,
):
    share_rows = tokens.shape[0]
    every_row = share_rows * lax.axis_size("tensor")
    q_heads = w_query.shape[1] // HEAD_SIZE
    kv_heads = key_weight.shape[1] // HEAD_SIZE
    head_group = q_heads // kv_heads
    length = lengths[0]
    first_row = lax.axis_index("tensor") * share_rows
    live_rows = (first_row + jnp.arange(share_rows, dtype=jnp.int32) < length)[:, None]
    resid = tokens.astype(jnp.float32)
    scaling = HEAD_SIZE ** (-0.5)
    whole_a = spread(rms_norm(resid, attn_gain).astype(jnp.bfloat16))
    raw_q = jnp.dot(whole_a, w_query, preferred_element_type=jnp.float32)
    unrotated_key = jnp.dot(whole_a, key_weight, preferred_element_type=jnp.float32)
    value_heads = (
        jnp.dot(whole_a, value_weight, preferred_element_type=jnp.float32)
        .astype(jnp.bfloat16)
        .reshape(every_row, kv_heads, HEAD_SIZE)
    )
    query_groups = (
        shaped(raw_q, q_gain, q_heads)
        .astype(jnp.bfloat16)
        .reshape(every_row, kv_heads, head_group, HEAD_SIZE)
    )
    heads_of_key = shaped(unrotated_key, k_gain, kv_heads).astype(jnp.bfloat16)
    key_place = jnp.arange(every_row, dtype=jnp.int32)
    blocks = (length + QBLOCK - 1) // QBLOCK

    def scores_of(block_start):
        block_q = lax.dynamic_slice_in_dim(query_groups, block_start, QBLOCK, 0)
        scores = (
            jnp.einsum("qgjd,kgd->gjqk", block_q, heads_of_key, preferred_element_type=jnp.float32)
            * scaling
        )
        places = block_start + jnp.arange(QBLOCK, dtype=jnp.int32)
        allowed = (key_place[None, :] <= places[:, None]) & (key_place[None, :] < length)
        return (block_q, jnp.where(allowed, scores, masked_score))

    def forward_block(block_index, state_carry):
        attended, lse_all = state_carry
        block_start = block_index * QBLOCK
        _, scores = scores_of(block_start)
        row_max = jnp.max(scores, axis=-1, keepdims=True)
        exponent = jnp.exp(scores - row_max)
        row_sum = jnp.sum(exponent, axis=-1, keepdims=True)
        weights = (exponent / row_sum).astype(jnp.bfloat16)
        block_out = jnp.einsum(
            "gjqk,kgd->qgjd", weights, value_heads, preferred_element_type=jnp.float32
        )
        block_out = block_out.reshape(QBLOCK, q_heads * HEAD_SIZE).astype(jnp.bfloat16)
        attended = lax.dynamic_update_slice_in_dim(attended, block_out, block_start, 0)
        lse_all = lax.dynamic_update_slice_in_dim(
            lse_all, (row_max + jnp.log(row_sum))[..., 0], block_start, 2
        )
        return (attended, lse_all)

    attended, lse_all = lax.fori_loop(
        0,
        blocks,
        forward_block,
        (
            jnp.zeros((every_row, q_heads * HEAD_SIZE), jnp.bfloat16),
            jnp.zeros((kv_heads, head_group, every_row), jnp.float32),
        ),
    )
    mixed = resid + settle(jnp.dot(attended, w_out, preferred_element_type=jnp.float32))
    whole_m = spread(rms_norm(mixed, mlp_gain).astype(jnp.bfloat16))
    gate_proj = jnp.dot(whole_m, w_gate, preferred_element_type=jnp.float32)
    up_proj = jnp.dot(whole_m, w_up, preferred_element_type=jnp.float32)
    activated = swiglu(gate_proj, up_proj).astype(jnp.bfloat16)
    layer_out = jnp.where(
        live_rows,
        mixed + settle(jnp.dot(activated, w_down, preferred_element_type=jnp.float32)),
        0.0,
    )
    grad_out = jnp.where(live_rows, cotangent.astype(jnp.float32), 0.0)
    grad_ffn = spread_grad(grad_out.astype(jnp.bfloat16))
    grad_w_down = jnp.einsum("rf,rd->fd", activated, grad_ffn, preferred_element_type=jnp.float32)
    grad_act = jnp.einsum("rd,fd->rf", grad_ffn, w_down, preferred_element_type=jnp.float32)
    _, swiglu_back = jax.vjp(swiglu, gate_proj, up_proj)
    grad_gate, grad_up = swiglu_back(grad_act)
    grad_gate = grad_gate.astype(jnp.bfloat16)
    grad_up = grad_up.astype(jnp.bfloat16)
    grad_w_gate = jnp.einsum("rd,rf->df", whole_m, grad_gate, preferred_element_type=jnp.float32)
    grad_w_up = jnp.einsum("rd,rf->df", whole_m, grad_up, preferred_element_type=jnp.float32)
    grad_normed_m = jnp.einsum(
        "rf,df->rd", grad_gate, w_gate, preferred_element_type=jnp.float32
    ) + jnp.einsum("rf,df->rd", grad_up, w_up, preferred_element_type=jnp.float32)
    _, mlp_norm_back = jax.vjp(rms_norm, mixed, mlp_gain)
    grad_mixed_norm, grad_mlp_gain = mlp_norm_back(settle_grad(grad_normed_m))
    grad_mixed = grad_out + grad_mixed_norm
    grad_branch = spread_grad(grad_mixed.astype(jnp.bfloat16))
    grad_w_out = jnp.einsum("rc,rd->cd", attended, grad_branch, preferred_element_type=jnp.float32)
    grad_groups = (
        jnp.einsum("rd,cd->rc", grad_branch, w_out, preferred_element_type=jnp.float32)
        .astype(jnp.bfloat16)
        .reshape(every_row, kv_heads, head_group, HEAD_SIZE)
    )

    def backward_block(block_index, state_carry):
        grad_query, grad_key, grad_value = state_carry
        block_start = block_index * QBLOCK
        block_q, scores = scores_of(block_start)
        block_lse = lax.dynamic_slice_in_dim(lse_all, block_start, QBLOCK, 2)
        probability = jnp.exp(scores - block_lse[..., None])
        block_grad = lax.dynamic_slice_in_dim(grad_groups, block_start, QBLOCK, 0)
        grad_probs = jnp.einsum(
            "qgjd,kgd->gjqk", block_grad, value_heads, preferred_element_type=jnp.float32
        )
        row_delta = jnp.sum(grad_probs * probability, axis=-1, keepdims=True)
        grad_scores = (probability * (grad_probs - row_delta)).astype(jnp.bfloat16)
        part_query = (
            jnp.einsum(
                "gjqk,kgd->qgjd", grad_scores, heads_of_key, preferred_element_type=jnp.float32
            )
            * scaling
        )
        grad_query = lax.dynamic_update_slice_in_dim(grad_query, part_query, block_start, 0)
        grad_key = (
            grad_key
            + jnp.einsum("gjqk,qgjd->kgd", grad_scores, block_q, preferred_element_type=jnp.float32)
            * scaling
        )
        grad_value = grad_value + jnp.einsum(
            "gjqk,qgjd->kgd",
            probability.astype(jnp.bfloat16),
            block_grad,
            preferred_element_type=jnp.float32,
        )
        return (grad_query, grad_key, grad_value)

    grad_query, grad_key, grad_value = lax.fori_loop(
        0,
        blocks,
        backward_block,
        (
            jnp.zeros((every_row, kv_heads, head_group, HEAD_SIZE), jnp.float32),
            jnp.zeros((every_row, kv_heads, HEAD_SIZE), jnp.float32),
            jnp.zeros((every_row, kv_heads, HEAD_SIZE), jnp.float32),
        ),
    )
    _, query_back = jax.vjp(lambda raw_rows, gain: shaped(raw_rows, gain, q_heads), raw_q, q_gain)
    grad_raw_q, grad_q_gain = query_back(grad_query.reshape(every_row, q_heads, HEAD_SIZE))
    _, key_back = jax.vjp(
        lambda raw_rows, gain: shaped(raw_rows, gain, kv_heads), unrotated_key, k_gain
    )
    grad_raw_k, grad_k_gain = key_back(grad_key)
    grad_raw_q = grad_raw_q.astype(jnp.bfloat16)
    grad_raw_k = grad_raw_k.astype(jnp.bfloat16)
    grad_raw_v = grad_value.reshape(every_row, kv_heads * HEAD_SIZE).astype(jnp.bfloat16)
    grad_w_query = jnp.einsum("rd,rc->dc", whole_a, grad_raw_q, preferred_element_type=jnp.float32)
    grad_w_key = jnp.einsum("rd,rc->dc", whole_a, grad_raw_k, preferred_element_type=jnp.float32)
    grad_w_value = jnp.einsum("rd,rc->dc", whole_a, grad_raw_v, preferred_element_type=jnp.float32)
    grad_normed_a = jnp.einsum("rc,dc->rd", grad_raw_q, w_query, preferred_element_type=jnp.float32)
    grad_normed_a = grad_normed_a + jnp.einsum(
        "rc,dc->rd", grad_raw_k, key_weight, preferred_element_type=jnp.float32
    )
    grad_normed_a = grad_normed_a + jnp.einsum(
        "rc,dc->rd", grad_raw_v, value_weight, preferred_element_type=jnp.float32
    )
    _, attn_norm_back = jax.vjp(rms_norm, resid, attn_gain)
    grad_resid_norm, grad_attn_gain = attn_norm_back(settle_grad(grad_normed_a))
    tokens_grad = grad_mixed + grad_resid_norm
    grad_w_query, grad_w_key, grad_w_value, grad_w_out, grad_w_gate, grad_w_up, grad_w_down = (
        lax.psum(
            (
                grad_w_query,
                grad_w_key,
                grad_w_value,
                grad_w_out,
                grad_w_gate,
                grad_w_up,
                grad_w_down,
            ),
            "dp",
        )
    )
    grad_attn_gain, grad_q_gain, grad_k_gain, grad_mlp_gain = lax.psum(
        (grad_attn_gain, grad_q_gain, grad_k_gain, grad_mlp_gain), ("dp", "tensor")
    )
    return (
        layer_out,
        tokens_grad,
        grad_attn_gain,
        grad_q_gain,
        grad_k_gain,
        grad_mlp_gain,
        grad_w_query,
        grad_w_key,
        grad_w_value,
        grad_w_out,
        grad_w_gate,
        grad_w_up,
        grad_w_down,
    )


def solution(mesh):
    return jax.shard_map(
        body,
        mesh=mesh,
        in_specs=(
            P(("dp", "tensor"), None),
            P(("dp", "tensor"), None),
            P(),
            P(),
            P(),
            P(),
            P(None, "tensor"),
            P(None, "tensor"),
            P(None, "tensor"),
            P("tensor", None),
            P(None, "tensor"),
            P(None, "tensor"),
            P("tensor", None),
            P("dp"),
        ),
        out_specs=(
            P(("dp", "tensor"), None),
            P(("dp", "tensor"), None),
            P(),
            P(),
            P(),
            P(),
            P(None, "tensor"),
            P(None, "tensor"),
            P(None, "tensor"),
            P("tensor", None),
            P(None, "tensor"),
            P(None, "tensor"),
            P("tensor", None),
        ),
        check_vma=False,
    )
```

profile of v0, /device:TPU:0, one launch (start us, length us, event | category | flops | bytes accessed | tf_op | source)
XLA Modules:
  0.0 934.1 jit_solution(8820650561867295150)
XLA Ops:
  8.6 2.0 fusion.56
  14.7 21.4 %all-gather.5.cloned.1.call-done = bf16[1024,1024]{1,0:T(8,128)(2,1)} async-done(((bf16[256,1024]{1,0:T(8,128)(2,1)}), bf16[1024,1024]{1,0:T(8,128)(2,1)}) %all-gather.5.cloned.1.call-update) | async-done | bytes 2097168 | tf_op jit(solution)/shard_map/all_gather | solution.py:41
  36.1 2.4 multiply_reduce_fusion.8
  40.2 4.5 multiply_reduce_fusion.2
  45.9 2.0 multiply_multiply_fusion
  49.0 3.2 copy.31
  52.2 1.9 copy.32
  54.1 2.9 copy.29
  57.0 3.9 fusion.53
  60.9 1.6 convolution_convert_fusion.1
  63.6 19.3 %while.30 = (s32[]{:T(128)}, bf16[1024,512]{0,1:T(8,128)(2,1)}, f32[2,2,1024]{2,1,0:T(2,128)S(1)}, s32[]{:T(128)}, s32[]{:T(128)}, /*index=5*/bf16[1024,2,2,128]...) while((s32[]{:T(128)}, bf16[1024,512]{0,1:T(8,128)(2,1)}, ...), condition=%wide.region_6.7_spmd.clone.clone, body=%wide.region_3.6_spmd.clone.clone.sunk | while | flops 1100217856 | bytes 40966412 | solution.py:127
  64.7 1.8 bitcast_reduce_fusion.2
  66.5 2.4 fusion.153
  68.9 3.1 fusion.154
  74.2 1.8 bitcast_reduce_fusion.2
  76.0 2.4 fusion.153
  78.4 3.1 fusion.154
  82.9 4.8 fusion.74
  87.8 44.6 %reduce-scatter.5.cloned.1.call-done = f32[256,1024]{1,0:T(8,128)} async-done(((f32[1024,1024]{1,0:T(8,128)}), f32[256,1024]{1,0:T(8,128)}) %reduce-scatter.5.cloned.1.call-update) | async-done | bytes 1048592 | tf_op jit(solution)/shard_map/reduce_scatter | solution.py:45
  132.4 1.6 multiply_reduce_fusion.7
  136.0 2.0 fusion.65
  138.1 20.6 %all-gather.7.cloned.1.call-done = bf16[1024,1024]{1,0:T(8,128)(2,1)} async-done(((bf16[256,1024]{1,0:T(8,128)(2,1)}), bf16[1024,1024]{1,0:T(8,128)(2,1)}) %all-gather.7.cloned.1.call-update) | async-done | bytes 2097168 | tf_op jit(solution)/shard_map/all_gather | solution.py:41
  158.7 5.6 fusion.76
  164.3 3.5 fusion.75
  167.8 15.6 %all-gather.9.cloned.1.call-done = bf16[1024,1024]{1,0:T(8,128)(2,1)} async-done(((bf16[256,1024]{1,0:T(8,128)(2,1)}), bf16[1024,1024]{1,0:T(8,128)(2,1)}) %all-gather.9.cloned.1.call-update) | async-done | bytes 2097168 | tf_op jit(solution)/shard_map/all_gather | solution.py:49
  183.4 7.6 multiply_convert_fusion
  191.0 1.8 fusion.78
  193.5 3.9 convolution_add_fusion
  197.5 5.2 fusion.77
  202.8 39.3 %reduce-scatter.9.cloned.1.call-done = f32[256,1024]{1,0:T(8,128)} async-done(((f32[1024,1024]{1,0:T(8,128)}), f32[256,1024]{1,0:T(8,128)}) %reduce-scatter.9.cloned.1.call-update) | async-done | bytes 1048592 | tf_op jit(solution)/shard_map/reduce_scatter | solution.py:53
  242.1 2.1 multiply_reduce_fusion.3
  244.1 44.9 %reduce-scatter.7.cloned.1.call-done = f32[256,1024]{1,0:T(8,128)} async-done(((f32[1024,1024]{1,0:T(8,128)}), f32[256,1024]{1,0:T(8,128)}) %reduce-scatter.7.cloned.1.call-update) | async-done | bytes 1048592 | tf_op jit(solution)/shard_map/reduce_scatter | solution.py:45
  289.0 3.5 fusion.72
  292.5 11.1 %reduce-scatter.11.cloned.1.call-start = ((), (), s32[]{:S(2)}) async-start(), calls=%async_computation.11 | async-start | bytes 5242880 | tf_op jit(solution)/shard_map/reduce_scatter | solution.py:53
  303.6 2.0 copy.37
  305.6 9.6 %all-gather.11.cloned.1.call-done = bf16[1024,1024]{1,0:T(8,128)(2,1)} async-done(((bf16[256,1024]{1,0:T(8,128)(2,1)}), bf16[1024,1024]{1,0:T(8,128)(2,1)}) %all-gather.11.cloned.1.call-update) | async-done | bytes 2097168 | tf_op jit(solution)/shard_map/all_gather | solution.py:49
  315.2 4.1 convolution_convert_fusion
  320.5 1.5 broadcast_in_dim.59
  322.0 31.8 %while.31 = (s32[]{:T(128)}, f32[1024,2,2,128]{3,0,2,1:T(8,128)}, f32[1024,2,128]{0,2,1:T(8,128)S(1)}, f32[1024,2,128]{0,2,1:T(8,128)}, s32[]{:T(128)}, /*index=...) while((s32[]{:T(128)}, f32[1024,2,2,128]{3,0,2,1:T(8,128)}, ...), condition=%wide.region_14.15_spmd.clone.clone, body=%wide.region_12.14_spmd.clone.clone.sunk | while | flops 2717908480 | bytes 105445752 | solution.py:202
  324.6 2.7 fusion.169
  327.4 3.9 fusion.165
  331.3 2.4 fusion.166
  340.5 2.7 fusion.169
  343.3 3.9 fusion.165
  347.2 2.4 fusion.166
  355.1 2.9 copy.38
  368.2 3.4 add_add_fusion
  373.3 5.1 fusion.87
  378.3 3.5 fusion.86
  381.9 3.6 fusion.85
  385.4 1.7 fusion.83
  387.2 1.7 fusion.82
  389.5 2.6 fusion.84
  392.1 2.6 fusion.81
  394.8 21.6 %reduce-scatter.11.cloned.1.call-done = f32[256,1024]{1,0:T(8,128)} async-done(((f32[1024,1024]{1,0:T(8,128)}), f32[256,1024]{1,0:T(8,128)}) %reduce-scatter.11.cloned.1.call-update) | async-done | bytes 1048592 | tf_op jit(solution)/shard_map/reduce_scatter | solution.py:53
  416.4 1.7 fusion.57
  418.0 45.1 %all-reduce.4 = (f32[1024]{0:T(1024)}, f32[128]{0:T(128)}, f32[128]{0:T(128)}, f32[1024]{0:T(1024)}) all-reduce(f32[1024]{0:T(1024)S(1)} %get-tuple-element.257, f32[128]{0:T(128)S(1)} %get-tuple-element.255, f32[128]{0:T(128)S(1)} %get-tuple-element.259, f32[1024]{0:T(1024)S(1)} %copy-done.52), channel_id=1, replica_groups=mesh['dp'=8,'tensor'=4] {'dp','tensor'}, use_global_device_ids=true, to_apply=%region_20.21 | all-reduce | flops 2304 | bytes 18432 | tf_op jit(solution)/shard_map/psum | solution.py:248
  464.5 447.1 %all-reduce.8.cloned.1.call-done = (f32[1024,512]{1,0:T(8,128)}, f32[1024,256]{1,0:T(8,128)}, f32[1024,256]{1,0:T(8,128)}, f32[512,1024]{1,0:T(8,128)}, f32[1024...) async-done(((f32[1024,512]{1,0:T(8,128)}, f32[1024,256]{1,0:T(8,128)}, f32[1024,256]{1,0:T(8,128)}, f32[512,1024]{1,0:T(8,128)}, f32[1024,768]{1,0:T(8,128)}, ...) | async-done | bytes 15728656 | tf_op jit(solution)/shard_map/psum | solution.py:235
  911.6 3.2 copy.81
  919.5 1.7 copy.85
  921.1 1.4 copy-done.29
  922.5 1.7 copy.86
  924.2 1.4 copy-done.28
  925.5 1.7 copy.87
  (240 shorter events, 51.2 us)
Async XLA Ops:
  7.2 176.2 %copy-start = (bf16[768,1024]{1,0:T(8,128)(2,1)S(1)}, bf16[768,1024]{1,0:T(8,128)(2,1)}, u32[]{:S(2)}) copy-start(bf16[768,1024]{1,0:T(8,128)(2,1)} %param.30) | copy-start | bytes 4718596
  7.2 28.9 %all-gather.5.cloned.1.call-start = ((), (), s32[]{:S(2)}) async-start(), calls=%async_computation.4 | async-start | bytes 2621440 | tf_op jit(solution)/shard_map/all_gather | solution.py:41
  8.6 3.8 copy-start.55
  8.6 3.8 copy-start.53
  10.7 121.7 %reduce-scatter.5.cloned.1.call-start = ((), (), s32[]{:S(2)}) async-start(), calls=%async_computation.5 | async-start | bytes 5242880 | tf_op jit(solution)/shard_map/reduce_scatter | solution.py:45
  11.4 24.7 %copy-start.31 = (bf16[1024,256]{1,0:T(8,128)(2,1)S(1)}, bf16[1024,256]{1,0:T(8,128)(2,1)}, u32[]{:S(2)}) copy-start(bf16[1024,256]{1,0:T(8,128)(2,1)} %param.25) | copy-start | bytes 1572868
  12.5 26.8 %copy-start.12 = (f32[1024,128]{0,1:T(8,128)}, f32[1024,128]{0,1:T(8,128)S(1)}, u32[]{:S(2)}) copy-start(f32[1024,128]{0,1:T(8,128)S(1)} %get-tuple-element.338) | copy-start | bytes 1572868
  12.5 26.8 %copy-start.14 = (f32[1024,128]{0,1:T(8,128)}, f32[1024,128]{0,1:T(8,128)S(1)}, u32[]{:S(2)}) copy-start(f32[1024,128]{0,1:T(8,128)S(1)} %get-tuple-element.339) | copy-start | bytes 1572868
  14.7 24.4 %copy-start.59 = (f32[128]{0:T(128)S(1)}, f32[128]{0:T(128)}, u32[]{:S(2)}) copy-start(f32[128]{0:T(128)} %param.22) | copy-start | bytes 1540
  40.2 5.7 copy-start.57
  57.0 3.9 copy-start.5
  57.0 3.9 copy-start.39
  66.5 2.4 copy-start.41
  68.9 3.2 copy-start.19
  76.0 2.4 copy-start.41
  78.4 3.2 copy-start.19
  87.7 47.2 %copy-start.50 = (f32[1024]{0:T(1024)S(1)}, f32[1024]{0:T(1024)}, u32[]{:S(2)}) copy-start(f32[1024]{0:T(1024)} %param.23) | copy-start | bytes 12292
  87.8 70.9 %all-gather.7.cloned.1.call-start = ((), (), s32[]{:S(2)}) async-start(), calls=%async_computation.6 | async-start | bytes 2621440 | tf_op jit(solution)/shard_map/all_gather | solution.py:41
  135.9 47.4 %all-gather.9.cloned.1.call-start = ((), (), s32[]{:S(2)}) async-start(), calls=%async_computation.8 | async-start | bytes 2621440 | tf_op jit(solution)/shard_map/all_gather | solution.py:49
  138.0 104.1 %reduce-scatter.9.cloned.1.call-start = ((), (), s32[]{:S(2)}) async-start(), calls=%async_computation.9 | async-start | bytes 5242880 | tf_op jit(solution)/shard_map/reduce_scatter | solution.py:53
  158.7 5.6 copy-start.61
  158.7 5.6 copy-start.64
  183.4 7.6 copy-start.65
  191.0 1.8 copy-start.69
  191.0 1.9 copy-start.67
  191.0 2.5 copy-start.66
  197.4 91.6 %reduce-scatter.7.cloned.1.call-start = ((), (), s32[]{:S(2)}) async-start(), calls=%async_computation.7 | async-start | bytes 5242880 | tf_op jit(solution)/shard_map/reduce_scatter | solution.py:45
  202.7 39.4 %copy-start.10 = (f32[256,1024]{1,0:T(8,128)S(1)}, f32[256,1024]{1,0:T(8,128)}, u32[]{:S(2)}) copy-start(f32[256,1024]{1,0:T(8,128)} %copy-done.9) | copy-start | bytes 3145732
  202.7 86.3 %copy-start.35 = (bf16[256,1024]{1,0:T(8,128)(2,1)S(1)}, bf16[256,1024]{1,0:T(8,128)(2,1)}, u32[]{:S(2)}) copy-start(bf16[256,1024]{1,0:T(8,128)(2,1)} %param.19) | copy-start | bytes 1572868
  202.7 112.5 %all-gather.11.cloned.1.call-start = ((), (), s32[]{:S(2)}) async-start(), calls=%async_computation.10 | async-start | bytes 2621440 | tf_op jit(solution)/shard_map/all_gather | solution.py:49
  292.5 123.9 %reduce-scatter.11.cloned.1.call-start = ((), (), s32[]{:S(2)}) async-start(), calls=%async_computation.11 | async-start | bytes 5242880 | tf_op jit(solution)/shard_map/reduce_scatter | solution.py:53
  324.6 2.7 copy-start.7
  327.4 3.9 copy-start.25
  333.7 1.6 copy-start.16
  340.5 2.7 copy-start.7
  343.3 3.9 copy-start.25
  349.6 1.6 copy-start.16
  355.1 3.0 copy-start.15
  359.4 1.6 copy-start.8
  361.3 1.6 copy-start.2
  367.6 4.1 copy-start.22
  371.7 1.6 copy-start.33
  371.7 539.9 %all-reduce.8.cloned.1.call-start = ((), (), s32[]{:S(2)}) async-start(), calls=%async_computation.12 | async-start | bytes 31457280 | tf_op jit(solution)/shard_map/psum | solution.py:235
  373.3 5.1 copy-start.62
  373.3 5.1 copy-start.68
  378.3 3.6 copy-start.70
  381.9 3.6 copy-start.6
  387.2 1.8 copy-start.21
  387.2 2.3 copy-start.63
  389.5 2.6 copy-start.23
  394.7 21.6 %copy-start.11 = (bf16[256,1024]{1,0:T(8,128)(2,1)S(1)}, bf16[256,1024]{1,0:T(8,128)(2,1)}, u32[]{:S(2)}) copy-start(bf16[256,1024]{1,0:T(8,128)(2,1)} %param.18) | copy-start | bytes 1572868
  394.7 21.6 %copy-start.51 = (f32[1024]{0:T(1024)S(1)}, f32[1024]{0:T(1024)}, u32[]{:S(2)}) copy-start(f32[1024]{0:T(1024)} %param.20) | copy-start | bytes 12292
  394.7 21.6 %copy-start.54 = (f32[256]{0:T(256)S(1)}, f32[256]{0:T(256)}, u32[]{:S(2)}) copy-start(f32[256]{0:T(256)} %copy-done.53) | copy-start | bytes 3076
  394.7 23.3 %copy-start.52 = (f32[1024]{0:T(1024)S(1)}, f32[1024]{0:T(1024)}, u32[]{:S(2)}) copy-start(f32[1024]{0:T(1024)} %get-tuple-element.253) | copy-start | bytes 12292
  394.7 68.4 %copy-start.56 = (f32[256]{0:T(256)S(1)}, f32[256]{0:T(256)}, u32[]{:S(2)}) copy-start(f32[256]{0:T(256)} %copy-done.55) | copy-start | bytes 3076
  394.7 68.4 %copy-start.27 = (f32[256,1024]{1,0:T(8,128)S(1)}, f32[256,1024]{1,0:T(8,128)}, u32[]{:S(2)}) copy-start(f32[256,1024]{1,0:T(8,128)} %get-tuple-element.313) | copy-start | bytes 3145732
  416.4 46.8 %copy-start.26 = (f32[256,1024]{1,0:T(8,128)S(1)}, f32[256,1024]{1,0:T(8,128)}, u32[]{:S(2)}) copy-start(f32[256,1024]{1,0:T(8,128)} %reduce-scatter.11.cloned.1.call-done) | copy-start | bytes 3145732
  911.6 3.2 copy-start.38
  911.6 4.2 copy-start.37
  914.8 2.0 copy-start.34
  916.8 2.6 copy-start.30
  919.5 3.0 copy-start.29
  922.5 3.0 copy-start.28
  922.5 4.7 copy-start.1
  (25 other events, 28.6 us)
Sparse Core Ops, SparseCore 0:
  10.8 25.2 all-gather.4
  87.9 44.4 reduce-scatter.4
  136.0 22.5 all-gather.6
  160.7 22.5 all-gather.8
  197.5 44.4 reduce-scatter.8
  244.5 44.4 reduce-scatter.6
  292.6 22.5 all-gather.10
  371.8 44.4 reduce-scatter.10
  423.2 488.3 all-reduce.7
where the time goes:
time: 944 us; the launch traced here: 934 us
  waiting for transfers between devices  665 us (70%)
  matrix products  101 us (11%)
  local copies, waits for them, and re-layouts  51.8 us (5%)
  blocking collectives  45.1 us (5%)
  other arithmetic  43.8 us (5%)
  between operations  15.5 us (2%)
  starting transfers between devices  11.6 us (1%)
    psum x1, waiting for transfers between devices, body(): lax.psum((grad_w_query, grad_w_key, grad_w_value, grad_w_out, grad_w_gate...  447 us
    reduce_scatter x2, waiting for transfers between devices, settle(): return lax.psum_scatter(values, 'tensor', scatter_dimension=0, tiled=True)  89.4 us
    reduce_scatter x2, waiting for transfers between devices, settle_grad(): return lax.psum_scatter(values, 'tensor', scatter_dimension=0, tiled=True)  60.9 us
    psum x1, blocking collectives, body(): lax.psum((grad_attn_gain, grad_q_gain, grad_k_gain, grad_mlp_gain), ('dp'...  45.1 us
    all_gather x2, waiting for transfers between devices, spread(): return lax.all_gather(values, 'tensor', axis=0, tiled=True)  42 us
    unnamed x133, local copies, waits for them, and re-layouts  28.5 us
    all_gather x2, waiting for transfers between devices, spread_grad(): return lax.all_gather(values, 'tensor', axis=0, tiled=True)  25.2 us
  transfers between devices with their start and end apart: 9, of which 9 were waited for; matrix products, arithmetic and copies ran while one was open for 5% of the time, Pallas kernels for 0%

commit v1 on v0

--- a/solution.py
+++ b/solution.py
@@ -37,20 +37,82 @@
     return gate_proj / (1.0 + jnp.exp(-gate_proj)) * up_proj
 
 
+def bit_of(axis, bit):
+    return (lax.axis_index(axis) >> bit) & 1
+
+
+def swap(values, axis, bit):
+    size = lax.axis_size(axis)
+    return lax.ppermute(values, axis, [(i, i ^ (1 << bit)) for i in range(size)])
+
+
+def ordered_pair(mine, other, flag):
+    is_first = flag == 0
+    return jnp.concatenate(
+        [jnp.where(is_first, mine, other), jnp.where(is_first, other, mine)], axis=0
+    )
+
+
+def halves(values, flag):
+    rows = values.shape[0] // 2
+    sent = lax.dynamic_slice_in_dim(values, (1 - flag) * rows, rows, 0)
+    kept = lax.dynamic_slice_in_dim(values, flag * rows, rows, 0)
+    return sent, kept
+
+
 def spread(values):
-    return lax.all_gather(values, "tensor", axis=0, tiled=True)
+    core = bit_of("tensor", 0)
+    side = bit_of("tensor", 1)
+    across = swap(values, "tensor", 1)
+    near = swap(values, "tensor", 0)
+    far = swap(across, "tensor", 0)
+    return ordered_pair(
+        ordered_pair(values, near, core), ordered_pair(across, far, core), side
+    )
 
 
 def settle(values):
-    return lax.psum_scatter(values, "tensor", scatter_dimension=0, tiled=True)
-
-
-def spread_grad(values):
-    return lax.all_gather(values, "tensor", axis=0, tiled=True)
-
-
-def settle_grad(values):
-    return lax.psum_scatter(values, "tensor", scatter_dimension=0, tiled=True)
+    core = bit_of("tensor", 0)
+    side = bit_of("tensor", 1)
+    rows = values.shape[0] // 4
+    parts = values.astype(jnp.bfloat16).reshape(2, 2, rows, values.shape[1])
+    sent = lax.dynamic_slice_in_dim(parts, 1 - core, 1, 1)
+    kept = lax.dynamic_slice_in_dim(parts, core, 1, 1)
+    pair = (kept.astype(jnp.float32) + swap(sent, "tensor", 0).astype(jnp.float32))[:, 0]
+    away = lax.dynamic_slice_in_dim(pair, 1 - side, 1, 0)[0].astype(jnp.bfloat16)
+    home = lax.dynamic_slice_in_dim(pair, side, 1, 0)[0]
+    return home + swap(away, "tensor", 1).astype(jnp.float32)
+
+
+def bit_order(first):
+    count = (lax.axis_size("dp") - 1).bit_length()
+    return [(first + i) % count for i in range(count)]
+
+
+def reduced_over_dp(values, first):
+    order = bit_order(first)
+    part = values.astype(jnp.bfloat16)
+    for bit in order:
+        sent, kept = halves(part, bit_of("dp", bit))
+        part = (kept.astype(jnp.float32) + swap(sent, "dp", bit).astype(jnp.float32)).astype(
+            jnp.bfloat16
+        )
+    for bit in reversed(order):
+        part = ordered_pair(part, swap(part, "dp", bit), bit_of("dp", bit))
+    return part.astype(jnp.float32)
+
+
+def reduced_over_all(values):
+    for axis in ("tensor", "dp"):
+        for bit in range((lax.axis_size(axis) - 1).bit_length()):
+            values = values + swap(values, axis, bit)
+    return values
+
+
+def unrolled(count, step, carry):
+    for index in range(count):
+        carry = step(index, carry)
+    return carry
 
 
 def body(
@@ -94,7 +156,6 @@
     )
     heads_of_key = shaped(unrotated_key, k_gain, kv_heads).astype(jnp.bfloat16)
     key_place = jnp.arange(every_row, dtype=jnp.int32)
-    blocks = (length + QBLOCK - 1) // QBLOCK
 
     def scores_of(block_start):
         block_q = lax.dynamic_slice_in_dim(query_groups, block_start, QBLOCK, 0)
@@ -124,9 +185,8 @@
         )
         return (attended, lse_all)
 
-    attended, lse_all = lax.fori_loop(
-        0,
-        blocks,
+    attended, lse_all = unrolled(
+        every_row // QBLOCK,
         forward_block,
         (
             jnp.zeros((every_row, q_heads * HEAD_SIZE), jnp.bfloat16),
@@ -144,7 +204,7 @@
         0.0,
     )
     grad_out = jnp.where(live_rows, cotangent.astype(jnp.float32), 0.0)
-    grad_ffn = spread_grad(grad_out.astype(jnp.bfloat16))
+    grad_ffn = spread(grad_out.astype(jnp.bfloat16))
     grad_w_down = jnp.einsum("rf,rd->fd", activated, grad_ffn, preferred_element_type=jnp.float32)
     grad_act = jnp.einsum("rd,fd->rf", grad_ffn, w_down, preferred_element_type=jnp.float32)
     _, swiglu_back = jax.vjp(swiglu, gate_proj, up_proj)
@@ -157,9 +217,9 @@
         "rf,df->rd", grad_gate, w_gate, preferred_element_type=jnp.float32
     ) + jnp.einsum("rf,df->rd", grad_up, w_up, preferred_element_type=jnp.float32)
     _, mlp_norm_back = jax.vjp(rms_norm, mixed, mlp_gain)
-    grad_mixed_norm, grad_mlp_gain = mlp_norm_back(settle_grad(grad_normed_m))
+    grad_mixed_norm, grad_mlp_gain = mlp_norm_back(settle(grad_normed_m))
     grad_mixed = grad_out + grad_mixed_norm
-    grad_branch = spread_grad(grad_mixed.astype(jnp.bfloat16))
+    grad_branch = spread(grad_mixed.astype(jnp.bfloat16))
     grad_w_out = jnp.einsum("rc,rd->cd", attended, grad_branch, preferred_element_type=jnp.float32)
     grad_groups = (
         jnp.einsum("rd,cd->rc", grad_branch, w_out, preferred_element_type=jnp.float32)
@@ -199,9 +259,8 @@
         )
         return (grad_query, grad_key, grad_value)
 
-    grad_query, grad_key, grad_value = lax.fori_loop(
-        0,
-        blocks,
+    grad_query, grad_key, grad_value = unrolled(
+        every_row // QBLOCK,
         backward_block,
         (
             jnp.zeros((every_row, kv_heads, head_group, HEAD_SIZE), jnp.float32),
@@ -229,24 +288,21 @@
         "rc,dc->rd", grad_raw_v, value_weight, preferred_element_type=jnp.float32
     )
     _, attn_norm_back = jax.vjp(rms_norm, resid, attn_gain)
-    grad_resid_norm, grad_attn_gain = attn_norm_back(settle_grad(grad_normed_a))
+    grad_resid_norm, grad_attn_gain = attn_norm_back(settle(grad_normed_a))
     tokens_grad = grad_mixed + grad_resid_norm
-    grad_w_query, grad_w_key, grad_w_value, grad_w_out, grad_w_gate, grad_w_up, grad_w_down = (
-        lax.psum(
-            (
-                grad_w_query,
-                grad_w_key,
-                grad_w_value,
-                grad_w_out,
-                grad_w_gate,
-                grad_w_up,
-                grad_w_down,
-            ),
-            "dp",
-        )
-    )
-    grad_attn_gain, grad_q_gain, grad_k_gain, grad_mlp_gain = lax.psum(
-        (grad_attn_gain, grad_q_gain, grad_k_gain, grad_mlp_gain), ("dp", "tensor")
+    grad_w_down = reduced_over_dp(grad_w_down, 0)
+    grad_w_gate = reduced_over_dp(grad_w_gate, 1)
+    grad_w_up = reduced_over_dp(grad_w_up, 0)
+    grad_w_out = reduced_over_dp(grad_w_out, 1)
+    grad_w_query = reduced_over_dp(grad_w_query, 0)
+    grad_w_key = reduced_over_dp(grad_w_key, 1)
+    grad_w_value = reduced_over_dp(grad_w_value, 1)
+    gains = reduced_over_all(
+        jnp.concatenate([grad_attn_gain, grad_mlp_gain, grad_q_gain, grad_k_gain])
+    )
+    width = grad_attn_gain.shape[0]
+    grad_attn_gain, grad_mlp_gain, grad_q_gain, grad_k_gain = jnp.split(
+        gains, [width, 2 * width, 2 * width + HEAD_SIZE]
     )
     return (
         layer_out,

time: 944 us -> 412 us (0.44)
  waiting for transfers between devices: 665 us -> 187 us
  starting transfers between devices: 11.6 us -> 64.9 us
  blocking collectives: 45.1 us -> 0 us
  matrix products: 101 us -> 67.1 us
  local copies, waits for them, and re-layouts: 51.8 us -> 23.1 us
  other arithmetic: 43.8 us -> 61.8 us
  between operations: 15.5 us -> 3.47 us
    psum x1 -> x0, waiting for transfers between devices: 447 us -> none  [body(): lax.psum((grad_w_query, grad_w_key, grad_w_value, grad_w_out, grad_w_gate...]
    ppermute x0 -> x67, waiting for transfers between devices: none -> 187 us  [swap(): return lax.ppermute(values, axis, [(i, i ^ 1 << bit) for i in range(size)])]
    reduce_scatter x4 -> x0, waiting for transfers between devices: 150 us -> none  [the longest x2 89.4 us: settle(): return lax.psum_scatter(values, 'tensor', scatter_dimension=0, tiled=True)]
    all_gather x4 -> x0, waiting for transfers between devices: 67.2 us -> none  [the longest x2 42 us: spread(): return lax.all_gather(values, 'tensor', axis=0, tiled=True)]
    ppermute x0 -> x67, starting transfers between devices: none -> 64.9 us  [swap(): return lax.ppermute(values, axis, [(i, i ^ 1 << bit) for i in range(size)])]
    psum x1 -> x0, blocking collectives: 45.1 us -> none  [body(): lax.psum((grad_attn_gain, grad_q_gain, grad_k_gain, grad_mlp_gain), ('dp'...]
    select_n x0 -> x33, other arithmetic: none -> 14 us  [ordered_pair(): jnp.where(is_first, mine, other)]
    reduce_scatter x4 -> x0, starting transfers between devices: 11.2 us -> none  [the longest x2 11.1 us: settle_grad(): return lax.psum_scatter(values, 'tensor', scatter_dimension=0, tiled=True)]
  transfers between devices with their start and end apart: 9 -> 67, of which waited for: 9 -> 31; matrix products, arithmetic and copies ran while one was open for 5% -> 20% of each run, Pallas kernels for 0% -> 0%
where the time goes in v1:
time: 412 us; the launch traced here: 407 us
  waiting for transfers between devices  187 us (45%)
  matrix products  67.1 us (16%)
  starting transfers between devices  64.9 us (16%)
  other arithmetic  61.8 us (15%)
  local copies, waits for them, and re-layouts  23.1 us (6%)
    ppermute x67, waiting for transfers between devices, swap(): return lax.ppermute(values, axis, [(i, i ^ 1 << bit) for i in range(size)])  187 us
    ppermute x67, starting transfers between devices, swap(): return lax.ppermute(values, axis, [(i, i ^ 1 << bit) for i in range(size)])  64.9 us
    unnamed x158, local copies, waits for them, and re-layouts  18.8 us
    select_n x33, other arithmetic, ordered_pair(): jnp.where(is_first, mine, other)  14 us
    dot_general x1, matrix products, body(): gate_proj = jnp.dot(whole_m, w_gate, preferred_element_type=jnp.float32)  11.6 us
    convert_element_type x7, other arithmetic, reduced_over_dp(): return part.astype(jnp.float32)  11.3 us
  transfers between devices with their start and end apart: 67, of which 31 were waited for; matrix products, arithmetic and copies ran while one was open for 20% of the time, Pallas kernels for 0%

profile of v1, /device:TPU:0, one launch (start us, length us, event | category | flops | bytes accessed | tf_op | source)
XLA Modules:
  0.0 407.2 jit_solution(2464493620956632664)
XLA Ops:
  2.1 2.1 fusion.47
  4.1 2.9 collective-permute-start.1
  8.9 10.3 %collective-permute-done.1 = bf16[256,1024]{1,0:T(8,128)(2,1)S(1)} collective-permute-done((bf16[256,1024]{1,0:T(8,128)(2,1)}, bf16[256,1024]{1,0:T(8,128)(2,1)S(1)}, u32[]{:S(2)}, u32[]{:S(2)}) %collective-permute-start.1) | collective-permute-done | bytes 524320 | tf_op jit(solution)/shard_map/ppermute | solution.py:46
  31.2 1.8 fusion.88
  34.1 2.2 copy-done.3
  36.3 1.9 fusion.44
  41.2 2.1 copy-done.2
  49.2 2.0 fusion.58
  52.9 1.9 convert_add_fusion.3
  57.8 8.5 %collective-permute-done.11 = bf16[256,1024]{1,0:T(8,128)(2,1)} collective-permute-done((bf16[256,1024]{1,0:T(8,128)(2,1)}, bf16[256,1024]{1,0:T(8,128)(2,1)}, u32[]{:S(2)}, u32[]{:S(2)}) %collective-permute-start.11) | collective-permute-done | bytes 524320 | tf_op jit(solution)/shard_map/ppermute | solution.py:46
  66.3 10.3 %collective-permute-done.4 = bf16[256,1024]{1,0:T(8,128)(2,1)} collective-permute-done((bf16[256,1024]{1,0:T(8,128)(2,1)}, bf16[256,1024]{1,0:T(8,128)(2,1)}, u32[]{:S(2)}, u32[]{:S(2)}) %collective-permute-start.4) | collective-permute-done | bytes 524320 | tf_op jit(solution)/shard_map/ppermute | solution.py:46
  78.4 1.8 collective-permute-start.6
  82.8 8.7 %collective-permute-done.6 = bf16[256,1024]{1,0:T(8,128)(2,1)S(1)} collective-permute-done((bf16[256,1024]{1,0:T(8,128)(2,1)S(1)}, bf16[256,1024]{1,0:T(8,128)(2,1)S(1)}, u32[]{:S(2)}, u32[]{:S(2)}) %collective-permute-start.6) | collective-permute-done | bytes 524320 | tf_op jit(solution)/shard_map/ppermute | solution.py:46
  94.9 1.8 fusion.76
  96.7 11.6 %fusion.77 = f32[1024,768]{1,0:T(8,128)S(1)} fusion(bf16[1024,768]{1,0:T(8,128)(2,1)S(1)} %copy-done.67, bf16[512,1024]{1,0:T(8,128)(2,1)S(1)} %get-tuple-element.37, bf16[512,1024]{1,0:T(8,128)(2,1)S(1)} %get-tuple-element.36), kind=kOutput, calls=%fused_computation.312 | convolution fusion | flops 1614807040 | bytes 6815744 | tf_op jit(solution)/shard_map/dot_general | solution.py:198
  108.3 4.6 %multiply_convert_fusion = (bf16[1024,768]{1,0:T(8,128)(2,1)S(1)}, bf16[1024,768]{1,0:T(8,128)(2,1)S(1)}, bf16[1024,768]{1,0:T(8,128)(2,1)S(1)}) fusion(f32[1024,768]{1,0:T(8,128)S(1)} %fusion.77, f32[1024,768]{1,0:T(8,128)S(1)} %fusion.76, bf16[768,1024]{1,0:T(8,128)(2,1)S(1)} %copy-done, bf16[512,1024]{1,0:T(8,128)(2,1)S(1)} %get-tuple-element.35, ...), kind=kOutput, calls=%fused_computation.31 | convolution fusion | flops 1628962816 | bytes 14680064 | tf_op jit(solution)/shard_map/rd,fd->rf/dot_general | solution.py:209
  112.9 1.9 convolution_convert_fusion.2
  114.8 1.8 convolution_convert_fusion.1
  116.6 1.9 convolution_convert_fusion.4
  118.5 1.8 fusion.89
  120.4 1.8 collective-permute-start.61
  122.2 1.9 convolution_convert_fusion.3
  124.6 1.9 collective-permute-start.49
  126.7 1.8 add_convert_fusion.1
  129.1 11.7 %collective-permute-done.61 = bf16[384,1024]{1,0:T(8,128)(2,1)S(1)} collective-permute-done((bf16[384,1024]{1,0:T(8,128)(2,1)S(1)}, bf16[384,1024]{1,0:T(8,128)(2,1)S(1)}, u32[]{:S(2)}, u32[]{:S(2)}) %collective-permute-start.61) | collective-permute-done | bytes 786464 | tf_op jit(solution)/shard_map/ppermute | solution.py:46
  141.2 1.9 collective-permute-start.62
  143.1 13.8 %collective-permute-done.55 = bf16[512,768]{1,0:T(8,128)(2,1)S(1)} collective-permute-done((bf16[512,768]{1,0:T(8,128)(2,1)S(1)}, bf16[512,768]{1,0:T(8,128)(2,1)S(1)}, u32[]{:S(2)}, u32[]{:S(2)}) %collective-permute-start.55) | collective-permute-done | bytes 786464 | tf_op jit(solution)/shard_map/ppermute | solution.py:46
  157.2 1.9 collective-permute-start.56
  159.3 2.6 collective-permute-start.50
  165.7 10.0 %collective-permute-done.56 = bf16[256,768]{1,0:T(8,128)(2,1)S(1)} collective-permute-done((bf16[256,768]{1,0:T(8,128)(2,1)S(1)}, bf16[256,768]{1,0:T(8,128)(2,1)S(1)}, u32[]{:S(2)}, u32[]{:S(2)}) %collective-permute-start.56) | collective-permute-done | bytes 393248 | tf_op jit(solution)/shard_map/ppermute | solution.py:46
  176.6 12.6 %collective-permute-done.50 = bf16[256,768]{1,0:T(8,128)(2,1)S(1)} collective-permute-done((bf16[256,768]{1,0:T(8,128)(2,1)S(1)}, bf16[256,768]{1,0:T(8,128)(2,1)S(1)}, u32[]{:S(2)}, u32[]{:S(2)}) %collective-permute-start.50) | collective-permute-done | bytes 393248 | tf_op jit(solution)/shard_map/ppermute | solution.py:46
  189.3 2.0 collective-permute-start.51
  191.3 4.2 %collective-permute-done.63 = bf16[96,1024]{1,0:T(8,128)(2,1)S(1)} collective-permute-done((bf16[96,1024]{1,0:T(8,128)(2,1)S(1)}, bf16[96,1024]{1,0:T(8,128)(2,1)S(1)}, u32[]{:S(2)}, u32[]{:S(2)}) %collective-permute-start.63) | collective-permute-done | bytes 196640 | tf_op jit(solution)/shard_map/ppermute | solution.py:46
  195.7 8.3 %collective-permute-done.57 = bf16[128,768]{1,0:T(8,128)(2,1)S(1)} collective-permute-done((bf16[128,768]{1,0:T(8,128)(2,1)S(1)}, bf16[128,768]{1,0:T(8,128)(2,1)S(1)}, u32[]{:S(2)}, u32[]{:S(2)}) %collective-permute-start.57) | collective-permute-done | bytes 196640 | tf_op jit(solution)/shard_map/ppermute | solution.py:46
  206.1 1.9 fusion.81
  209.6 3.1 collective-permute-start.65
  213.0 2.9 collective-permute-start.53
  215.8 15.2 %collective-permute-done.65 = bf16[192,1024]{1,0:T(8,128)(2,1)S(1)} collective-permute-done((bf16[192,1024]{1,0:T(8,128)(2,1)S(1)}, bf16[192,1024]{1,0:T(8,128)(2,1)S(1)}, u32[]{:S(2)}, u32[]{:S(2)}) %collective-permute-start.65) | collective-permute-done | bytes 393248 | tf_op jit(solution)/shard_map/ppermute | solution.py:46
  232.8 6.3 %collective-permute-done.59 = bf16[256,768]{1,0:T(8,128)(2,1)S(1)} collective-permute-done((bf16[256,768]{1,0:T(8,128)(2,1)S(1)}, bf16[256,768]{1,0:T(8,128)(2,1)S(1)}, u32[]{:S(2)}, u32[]{:S(2)}) %collective-permute-start.59) | collective-permute-done | bytes 393248 | tf_op jit(solution)/shard_map/ppermute | solution.py:46
  244.0 2.2 convolution_convert_fusion.5
  248.6 2.5 fusion.25
  251.1 1.8 fusion.3
  253.3 5.2 %fusion = (f32[2,2,512]{2,1,0:T(2,128)S(1)}, f32[2,1024,512,2]{2,1,3,0:T(8,128)}) fusion(f32[2,2,512,1024]{2,3,1,0:T(8,128)S(1)} %bitcast.199, f32[2,2,512]{2,1,0:T(2,128)S(1)} %log_add_fusion, bf16[1024,2,128,1]{0,2,3,1:T(8,128)(2,1)S(1)} %bitcast.225, bf16[512,2,2,128]{0,3,2,1:T(8,128)(2,1)S(1)} %bitcast.208), kind=kOutput, calls=%fused_computation.2 | convolution fusion | flops 543160320 | bytes 17842176 | tf_op jit(solution)/shard_map/qgjd,kgd->gjqk/dot_general | solution.py:237
  258.4 4.7 %fusion.2 = bf16[2,2,512,1024]{2,3,1,0:T(8,128)(2,1)S(1)} fusion(f32[2,1024,512,2]{2,1,3,0:T(8,128)} %get-tuple-element.126, f32[2,2,512,1024]{2,3,1,0:T(8,128)S(1)} %bitcast.199, f32[2,2,512]{2,1,0:T(2,128)S(1)} %get-tuple-element.125, f32[2,2,512]{2,1,0:T(2,128)S(1)} %log_add_fusion), kind=kLoop, calls=%fused_computation.4 | loop fusion | flops 8388608 | bytes 20987904 | tf_op jit(solution)/shard_map/convert_element_type | solution.py:241
  263.2 2.4 convolution_bitcast_fusion
  267.3 2.6 fusion.5
  294.5 2.3 maximum_convert_fusion.2
  301.3 1.9 maximum_convert_fusion.1
  303.2 1.9 maximum_convert_fusion
  306.0 2.7 collective-permute-done.31
  310.3 7.7 %collective-permute-done.38 = bf16[256,256]{1,0:T(8,128)(2,1)S(1)} collective-permute-done((bf16[256,256]{1,0:T(8,128)(2,1)S(1)}, bf16[256,256]{1,0:T(8,128)(2,1)S(1)}, u32[]{:S(2)}, u32[]{:S(2)}) %collective-permute-start.38) | collective-permute-done | bytes 131104 | tf_op jit(solution)/shard_map/ppermute | solution.py:46
  318.7 1.8 collective-permute-done.32
  323.0 2.0 collective-permute-done.33
  327.5 1.9 collective-permute-start.41
  332.2 14.8 %collective-permute-done.41 = bf16[256,256]{1,0:T(8,128)(2,1)S(1)} collective-permute-done((bf16[256,256]{1,0:T(8,128)(2,1)S(1)}, bf16[256,256]{1,0:T(8,128)(2,1)S(1)}, u32[]{:S(2)}, u32[]{:S(2)}) %collective-permute-start.41) | collective-permute-done | bytes 131104 | tf_op jit(solution)/shard_map/ppermute | solution.py:46
  347.1 2.6 collective-permute-done.35
  350.8 3.0 collective-permute-start.27
  356.2 5.3 %collective-permute-done.27 = bf16[128,512]{1,0:T(8,128)(2,1)S(1)} collective-permute-done((bf16[128,512]{1,0:T(8,128)(2,1)S(1)}, bf16[128,512]{1,0:T(8,128)(2,1)S(1)}, u32[]{:S(2)}, u32[]{:S(2)}) %collective-permute-start.27) | collective-permute-done | bytes 131104 | tf_op jit(solution)/shard_map/ppermute | solution.py:46
  361.5 3.4 collective-permute-start.28
  369.5 5.6 %collective-permute-done.28 = bf16[128,512]{1,0:T(8,128)(2,1)S(1)} collective-permute-done((bf16[128,512]{1,0:T(8,128)(2,1)S(1)}, bf16[128,512]{1,0:T(8,128)(2,1)S(1)}, u32[]{:S(2)}, u32[]{:S(2)}) %collective-permute-start.28) | collective-permute-done | bytes 131104 | tf_op jit(solution)/shard_map/ppermute | solution.py:46
  375.2 6.9 %collective-permute-done.47 = bf16[128,1024]{1,0:T(8,128)(2,1)S(1)} collective-permute-done((bf16[128,1024]{1,0:T(8,128)(2,1)S(1)}, bf16[128,1024]{1,0:T(8,128)(2,1)S(1)}, u32[]{:S(2)}, u32[]{:S(2)}) %collective-permute-start.47) | collective-permute-done | bytes 262176 | tf_op jit(solution)/shard_map/ppermute | solution.py:46
  385.7 2.1 collective-permute-done.21
  392.7 4.9 %collective-permute-done.23 = f32[2304]{0:T(1024)S(1)} collective-permute-done((f32[2304]{0:T(1024)S(1)}, f32[2304]{0:T(1024)S(1)}, u32[]{:S(2)}, u32[]{:S(2)}) %collective-permute-start.23) | collective-permute-done | bytes 9248 | tf_op jit(solution)/shard_map/ppermute | solution.py:46
  399.9 2.3 collective-permute-done.24
  (425 shorter events, 121.4 us)
Async XLA Ops:
  4.1 15.1 %collective-permute-start.1 = (bf16[256,1024]{1,0:T(8,128)(2,1)}, bf16[256,1024]{1,0:T(8,128)(2,1)S(1)}, u32[]{:S(2)}, u32[]{:S(2)}) collective-permute-start(bf16[256,1024]{1,0:T(8,128)(2,1)} %fusion.47), channel_id=1, source_target_pairs={{0,2},{1,3},{2,0},{3,1},{4,6},{5,7},{6,4},{7,5},{8,10},{9,11},{10,... | collective-permute-start | bytes 1572872 | tf_op jit(solution)/shard_map/ppermute | solution.py:46
  7.1 12.7 %collective-permute-start = (bf16[256,1024]{1,0:T(8,128)(2,1)}, bf16[256,1024]{1,0:T(8,128)(2,1)}, u32[]{:S(2)}, u32[]{:S(2)}) collective-permute-start(bf16[256,1024]{1,0:T(8,128)(2,1)} %fusion.47), channel_id=1, source_target_pairs={{0,1},{1,0},{2,3},{3,2},{4,5},{5,4},{6,7},{7,6},{8,9},{9,8},{10,11... | collective-permute-start | bytes 1572872 | tf_op jit(solution)/shard_map/ppermute | solution.py:46
  19.2 2.0 collective-permute-start.2
  48.6 4.3 %collective-permute-start.3 = (bf16[2,1,256,1024]{3,2,1,0:T(8,128)(2,1)}, bf16[2,1,256,1024]{3,2,1,0:T(8,128)(2,1)}, u32[]{:S(2)}, u32[]{:S(2)}) collective-permute-start(bf16[2,1,256,1024]{3,2,1,0:T(8,128)(2,1)} %constant_dynamic-slice_fusion.24), channel_id=1, source_target_pairs={{0,1},{1,0},{2,3},{3,2},{4,5},{5,4},{6,7},{7,6},{8,9},{9,8},{10,11... | collective-permute-start | bytes 3145736 | tf_op jit(solution)/shard_map/ppermute | solution.py:46
  51.2 15.1 %collective-permute-start.11 = (bf16[256,1024]{1,0:T(8,128)(2,1)}, bf16[256,1024]{1,0:T(8,128)(2,1)}, u32[]{:S(2)}, u32[]{:S(2)}) collective-permute-start(bf16[256,1024]{1,0:T(8,128)(2,1)} %fusion.58), channel_id=1, source_target_pairs={{0,2},{1,3},{2,0},{3,1},{4,6},{5,7},{6,4},{7,5},{8,10},{9,11},{10,... | collective-permute-start | bytes 1572872 | tf_op jit(solution)/shard_map/ppermute | solution.py:46
  57.0 19.5 %collective-permute-start.4 = (bf16[256,1024]{1,0:T(8,128)(2,1)}, bf16[256,1024]{1,0:T(8,128)(2,1)}, u32[]{:S(2)}, u32[]{:S(2)}) collective-permute-start(bf16[256,1024]{1,0:T(8,128)(2,1)} %fusion.59), channel_id=1, source_target_pairs={{0,2},{1,3},{2,0},{3,1},{4,6},{5,7},{6,4},{7,5},{8,10},{9,11},{10,... | collective-permute-start | bytes 1572872 | tf_op jit(solution)/shard_map/ppermute | solution.py:46
  57.7 22.5 %collective-permute-start.10 = (bf16[256,1024]{1,0:T(8,128)(2,1)}, bf16[256,1024]{1,0:T(8,128)(2,1)}, u32[]{:S(2)}, u32[]{:S(2)}) collective-permute-start(bf16[256,1024]{1,0:T(8,128)(2,1)} %fusion.58), channel_id=1, source_target_pairs={{0,1},{1,0},{2,3},{3,2},{4,5},{5,4},{6,7},{7,6},{8,9},{9,8},{10,11... | collective-permute-start | bytes 1572872 | tf_op jit(solution)/shard_map/ppermute | solution.py:46
  66.3 15.3 %collective-permute-start.12 = (bf16[256,1024]{1,0:T(8,128)(2,1)}, bf16[256,1024]{1,0:T(8,128)(2,1)S(1)}, u32[]{:S(2)}, u32[]{:S(2)}) collective-permute-start(bf16[256,1024]{1,0:T(8,128)(2,1)} %collective-permute-done.11), channel_id=1, source_target_pairs={{0,1},{1,0},{2,3},{3,2},{4,5},{5,4},{6,7},{7,6},{8,9},{9,8},{10,11... | collective-permute-start | bytes 1572872 | tf_op jit(solution)/shard_map/ppermute | solution.py:46
  78.4 13.1 %collective-permute-start.6 = (bf16[256,1024]{1,0:T(8,128)(2,1)S(1)}, bf16[256,1024]{1,0:T(8,128)(2,1)S(1)}, u32[]{:S(2)}, u32[]{:S(2)}) collective-permute-start(bf16[256,1024]{1,0:T(8,128)(2,1)S(1)} %multiply_convert_fusion.2), channel_id=1, source_target_pairs={{0,2},{1,3},{2,0},{3,1},{4,6},{5,7},{6,4},{7,5},{8,10},{9,11},{10,... | collective-permute-start | bytes 1572872 | tf_op jit(solution)/shard_map/ppermute | solution.py:46
  82.7 9.4 %collective-permute-start.5 = (bf16[256,1024]{1,0:T(8,128)(2,1)S(1)}, bf16[256,1024]{1,0:T(8,128)(2,1)S(1)}, u32[]{:S(2)}, u32[]{:S(2)}) collective-permute-start(bf16[256,1024]{1,0:T(8,128)(2,1)S(1)} %multiply_convert_fusion.2), channel_id=1, source_target_pairs={{0,1},{1,0},{2,3},{3,2},{4,5},{5,4},{6,7},{7,6},{8,9},{9,8},{10,11... | collective-permute-start | bytes 1572872 | tf_op jit(solution)/shard_map/ppermute | solution.py:46
  120.4 20.5 %collective-permute-start.61 = (bf16[384,1024]{1,0:T(8,128)(2,1)S(1)}, bf16[384,1024]{1,0:T(8,128)(2,1)S(1)}, u32[]{:S(2)}, u32[]{:S(2)}) collective-permute-start(bf16[384,1024]{1,0:T(8,128)(2,1)S(1)} %constant_dynamic-slice_fusion.2), channel_id=1, source_target_pairs={{0,4},{4,0},{8,12},{12,8},{16,20},{20,16},{24,28},{28,24},{1,5},{5... | collective-permute-start | bytes 2359304 | tf_op jit(solution)/shard_map/ppermute | solution.py:46
  124.2 32.7 %collective-permute-start.55 = (bf16[512,768]{1,0:T(8,128)(2,1)S(1)}, bf16[512,768]{1,0:T(8,128)(2,1)S(1)}, u32[]{:S(2)}, u32[]{:S(2)}) collective-permute-start(bf16[512,768]{1,0:T(8,128)(2,1)S(1)} %constant_dynamic-slice_fusion.5), channel_id=1, source_target_pairs={{0,4},{4,0},{8,12},{12,8},{16,20},{20,16},{24,28},{28,24},{1,5},{5... | collective-permute-start | bytes 2359304 | tf_op jit(solution)/shard_map/ppermute | solution.py:46
  124.6 34.5 %collective-permute-start.49 = (bf16[512,768]{1,0:T(8,128)(2,1)S(1)}, bf16[512,768]{1,0:T(8,128)(2,1)S(1)}, u32[]{:S(2)}, u32[]{:S(2)}) collective-permute-start(bf16[512,768]{1,0:T(8,128)(2,1)S(1)} %constant_dynamic-slice_fusion.8), channel_id=1, source_target_pairs={{0,8},{4,12},{8,0},{12,4},{16,24},{20,28},{24,16},{28,20},{1,9},{5... | collective-permute-start | bytes 2359304 | tf_op jit(solution)/shard_map/ppermute | solution.py:46
  126.6 35.4 %collective-permute-start.8 = (bf16[2,1,256,1024]{3,2,1,0:T(8,128)(2,1)S(1)}, bf16[2,1,256,1024]{3,2,1,0:T(8,128)(2,1)S(1)}, u32[]{:S(2)}, u32[]{:S(2)}) collective-permute-start(bf16[2,1,256,1024]{3,2,1,0:T(8,128)(2,1)S(1)} %constant_dynamic-slice_fusion.23), channel_id=1, source_target_pairs={{0,1},{1,0},{2,3},{3,2},{4,5},{5,4},{6,7},{7,6},{8,9},{9,8},{10,11... | collective-permute-start | bytes 3145736 | tf_op jit(solution)/shard_map/ppermute | solution.py:46
  128.6 35.4 %collective-permute-start.13 = (bf16[2,1,256,1024]{3,2,1,0:T(8,128)(2,1)S(1)}, bf16[2,1,256,1024]{3,2,1,0:T(8,128)(2,1)S(1)}, u32[]{:S(2)}, u32[]{:S(2)}) collective-permute-start(bf16[2,1,256,1024]{3,2,1,0:T(8,128)(2,1)S(1)} %constant_dynamic-slice_fusion.22), channel_id=1, source_target_pairs={{0,1},{1,0},{2,3},{3,2},{4,5},{5,4},{6,7},{7,6},{8,9},{9,8},{10,11... | collective-permute-start | bytes 3145736 | tf_op jit(solution)/shard_map/ppermute | solution.py:46
  141.2 23.9 %collective-permute-start.62 = (bf16[192,1024]{1,0:T(8,128)(2,1)S(1)}, bf16[192,1024]{1,0:T(8,128)(2,1)S(1)}, u32[]{:S(2)}, u32[]{:S(2)}) collective-permute-start(bf16[192,1024]{1,0:T(8,128)(2,1)S(1)} %constant_dynamic-slice_fusion.1), channel_id=1, source_target_pairs={{0,8},{4,12},{8,0},{12,4},{16,24},{20,28},{24,16},{28,20},{1,9},{5... | collective-permute-start | bytes 1179656 | tf_op jit(solution)/shard_map/ppermute | solution.py:46
  157.2 18.5 %collective-permute-start.56 = (bf16[256,768]{1,0:T(8,128)(2,1)S(1)}, bf16[256,768]{1,0:T(8,128)(2,1)S(1)}, u32[]{:S(2)}, u32[]{:S(2)}) collective-permute-start(bf16[256,768]{1,0:T(8,128)(2,1)S(1)} %constant_dynamic-slice_fusion.4), channel_id=1, source_target_pairs={{0,8},{4,12},{8,0},{12,4},{16,24},{20,28},{24,16},{28,20},{1,9},{5... | collective-permute-start | bytes 1179656 | tf_op jit(solution)/shard_map/ppermute | solution.py:46
  159.3 29.9 %collective-permute-start.50 = (bf16[256,768]{1,0:T(8,128)(2,1)S(1)}, bf16[256,768]{1,0:T(8,128)(2,1)S(1)}, u32[]{:S(2)}, u32[]{:S(2)}) collective-permute-start(bf16[256,768]{1,0:T(8,128)(2,1)S(1)} %constant_dynamic-slice_fusion.7), channel_id=1, source_target_pairs={{0,16},{4,20},{8,24},{12,28},{16,0},{20,4},{24,8},{28,12},{1,17},{... | collective-permute-start | bytes 1179656 | tf_op jit(solution)/shard_map/ppermute | solution.py:46
  162.5 43.7 %collective-permute-start.9 = (bf16[256,1024]{1,0:T(8,128)(2,1)S(1)}, bf16[256,1024]{1,0:T(8,128)(2,1)S(1)}, u32[]{:S(2)}, u32[]{:S(2)}) collective-permute-start(bf16[256,1024]{1,0:T(8,128)(2,1)S(1)} %fusion.60), channel_id=1, source_target_pairs={{0,2},{1,3},{2,0},{3,1},{4,6},{5,7},{6,4},{7,5},{8,10},{9,11},{10,... | collective-permute-start | bytes 1572872 | tf_op jit(solution)/shard_map/ppermute | solution.py:46
  164.5 41.2 %collective-permute-start.14 = (bf16[256,1024]{1,0:T(8,128)(2,1)S(1)}, bf16[256,1024]{1,0:T(8,128)(2,1)S(1)}, u32[]{:S(2)}, u32[]{:S(2)}) collective-permute-start(bf16[256,1024]{1,0:T(8,128)(2,1)S(1)} %fusion.61), channel_id=1, source_target_pairs={{0,2},{1,3},{2,0},{3,1},{4,6},{5,7},{6,4},{7,5},{8,10},{9,11},{10,... | collective-permute-start | bytes 1572872 | tf_op jit(solution)/shard_map/ppermute | solution.py:46
  165.3 30.2 %collective-permute-start.63 = (bf16[96,1024]{1,0:T(8,128)(2,1)S(1)}, bf16[96,1024]{1,0:T(8,128)(2,1)S(1)}, u32[]{:S(2)}, u32[]{:S(2)}) collective-permute-start(bf16[96,1024]{1,0:T(8,128)(2,1)S(1)} %constant_dynamic-slice_fusion), channel_id=1, source_target_pairs={{0,16},{4,20},{8,24},{12,28},{16,0},{20,4},{24,8},{28,12},{1,17},{... | collective-permute-start | bytes 589832 | tf_op jit(solution)/shard_map/ppermute | solution.py:46
  175.8 28.1 %collective-permute-start.57 = (bf16[128,768]{1,0:T(8,128)(2,1)S(1)}, bf16[128,768]{1,0:T(8,128)(2,1)S(1)}, u32[]{:S(2)}, u32[]{:S(2)}) collective-permute-start(bf16[128,768]{1,0:T(8,128)(2,1)S(1)} %constant_dynamic-slice_fusion.3), channel_id=1, source_target_pairs={{0,16},{4,20},{8,24},{12,28},{16,0},{20,4},{24,8},{28,12},{1,17},{... | collective-permute-start | bytes 589832 | tf_op jit(solution)/shard_map/ppermute | solution.py:46
  189.3 14.7 %collective-permute-start.51 = (bf16[128,768]{1,0:T(8,128)(2,1)S(1)}, bf16[128,768]{1,0:T(8,128)(2,1)S(1)}, u32[]{:S(2)}, u32[]{:S(2)}) collective-permute-start(bf16[128,768]{1,0:T(8,128)(2,1)S(1)} %constant_dynamic-slice_fusion.6), channel_id=1, source_target_pairs={{0,4},{4,0},{8,12},{12,8},{16,20},{20,16},{24,28},{28,24},{1,5},{5... | collective-permute-start | bytes 589832 | tf_op jit(solution)/shard_map/ppermute | solution.py:46
  195.6 14.0 %collective-permute-start.64 = (bf16[96,1024]{1,0:T(8,128)(2,1)S(1)}, bf16[96,1024]{1,0:T(8,128)(2,1)S(1)}, u32[]{:S(2)}, u32[]{:S(2)}) collective-permute-start(bf16[96,1024]{1,0:T(8,128)(2,1)S(1)} %add_convert_fusion.15), channel_id=1, source_target_pairs={{0,16},{4,20},{8,24},{12,28},{16,0},{20,4},{24,8},{28,12},{1,17},{... | collective-permute-start | bytes 589832 | tf_op jit(solution)/shard_map/ppermute | solution.py:46
  204.0 8.7 %collective-permute-start.58 = (bf16[128,768]{1,0:T(8,128)(2,1)S(1)}, bf16[128,768]{1,0:T(8,128)(2,1)S(1)}, u32[]{:S(2)}, u32[]{:S(2)}) collective-permute-start(bf16[128,768]{1,0:T(8,128)(2,1)S(1)} %add_convert_fusion.16), channel_id=1, source_target_pairs={{0,16},{4,20},{8,24},{12,28},{16,0},{20,4},{24,8},{28,12},{1,17},{... | collective-permute-start | bytes 589832 | tf_op jit(solution)/shard_map/ppermute | solution.py:46
  204.2 8.7 %collective-permute-start.52 = (bf16[128,768]{1,0:T(8,128)(2,1)S(1)}, bf16[128,768]{1,0:T(8,128)(2,1)S(1)}, u32[]{:S(2)}, u32[]{:S(2)}) collective-permute-start(bf16[128,768]{1,0:T(8,128)(2,1)S(1)} %add_convert_fusion.17), channel_id=1, source_target_pairs={{0,4},{4,0},{8,12},{12,8},{16,20},{20,16},{24,28},{28,24},{1,5},{5... | collective-permute-start | bytes 589832 | tf_op jit(solution)/shard_map/ppermute | solution.py:46
  208.0 33.9 %collective-permute-start.15 = (bf16[256,1024]{1,0:T(8,128)(2,1)S(1)}, bf16[256,1024]{1,0:T(8,128)(2,1)S(1)}, u32[]{:S(2)}, u32[]{:S(2)}) collective-permute-start(bf16[256,1024]{1,0:T(8,128)(2,1)S(1)} %get-tuple-element.23), channel_id=1, source_target_pairs={{0,1},{1,0},{2,3},{3,2},{4,5},{5,4},{6,7},{7,6},{8,9},{9,8},{10,11... | collective-permute-start | bytes 1572872 | tf_op jit(solution)/shard_map/ppermute | solution.py:46
  208.0 32.7 %collective-permute-start.16 = (bf16[256,1024]{1,0:T(8,128)(2,1)S(1)}, bf16[256,1024]{1,0:T(8,128)(2,1)S(1)}, u32[]{:S(2)}, u32[]{:S(2)}) collective-permute-start(bf16[256,1024]{1,0:T(8,128)(2,1)S(1)} %get-tuple-element.23), channel_id=1, source_target_pairs={{0,2},{1,3},{2,0},{3,1},{4,6},{5,7},{6,4},{7,5},{8,10},{9,11},{10,... | collective-permute-start | bytes 1572872 | tf_op jit(solution)/shard_map/ppermute | solution.py:46
  209.6 21.4 %collective-permute-start.65 = (bf16[192,1024]{1,0:T(8,128)(2,1)S(1)}, bf16[192,1024]{1,0:T(8,128)(2,1)S(1)}, u32[]{:S(2)}, u32[]{:S(2)}) collective-permute-start(bf16[192,1024]{1,0:T(8,128)(2,1)S(1)} %pad_maximum_fusion.29), channel_id=1, source_target_pairs={{0,8},{4,12},{8,0},{12,4},{16,24},{20,28},{24,16},{28,20},{1,9},{5... | collective-permute-start | bytes 1179656 | tf_op jit(solution)/shard_map/ppermute | solution.py:46
  212.8 26.3 %collective-permute-start.59 = (bf16[256,768]{1,0:T(8,128)(2,1)S(1)}, bf16[256,768]{1,0:T(8,128)(2,1)S(1)}, u32[]{:S(2)}, u32[]{:S(2)}) collective-permute-start(bf16[256,768]{1,0:T(8,128)(2,1)S(1)} %pad_maximum_fusion.28), channel_id=1, source_target_pairs={{0,8},{4,12},{8,0},{12,4},{16,24},{20,28},{24,16},{28,20},{1,9},{5... | collective-permute-start | bytes 1179656 | tf_op jit(solution)/shard_map/ppermute | solution.py:46
  213.0 27.8 %collective-permute-start.53 = (bf16[256,768]{1,0:T(8,128)(2,1)S(1)}, bf16[256,768]{1,0:T(8,128)(2,1)S(1)}, u32[]{:S(2)}, u32[]{:S(2)}) collective-permute-start(bf16[256,768]{1,0:T(8,128)(2,1)S(1)} %pad_maximum_fusion.27), channel_id=1, source_target_pairs={{0,16},{4,20},{8,24},{12,28},{16,0},{20,4},{24,8},{28,12},{1,17},{... | collective-permute-start | bytes 1179656 | tf_op jit(solution)/shard_map/ppermute | solution.py:46
  232.3 59.2 %collective-permute-start.66 = (bf16[384,1024]{1,0:T(8,128)(2,1)}, bf16[384,1024]{1,0:T(8,128)(2,1)}, u32[]{:S(2)}, u32[]{:S(2)}) collective-permute-start(bf16[384,1024]{1,0:T(8,128)(2,1)} %pad_maximum_fusion.20), channel_id=1, source_target_pairs={{0,4},{4,0},{8,12},{12,8},{16,20},{20,16},{24,28},{28,24},{1,5},{5... | collective-permute-start | bytes 2359304 | tf_op jit(solution)/shard_map/ppermute | solution.py:46
  240.3 56.5 %collective-permute-start.60 = (bf16[512,768]{1,0:T(8,128)(2,1)}, bf16[512,768]{1,0:T(8,128)(2,1)}, u32[]{:S(2)}, u32[]{:S(2)}) collective-permute-start(bf16[512,768]{1,0:T(8,128)(2,1)} %pad_maximum_fusion.19), channel_id=1, source_target_pairs={{0,4},{4,0},{8,12},{12,8},{16,20},{20,16},{24,28},{28,24},{1,5},{5... | collective-permute-start | bytes 2359304 | tf_op jit(solution)/shard_map/ppermute | solution.py:46
  242.0 57.8 %collective-permute-start.54 = (bf16[512,768]{1,0:T(8,128)(2,1)}, bf16[512,768]{1,0:T(8,128)(2,1)}, u32[]{:S(2)}, u32[]{:S(2)}) collective-permute-start(bf16[512,768]{1,0:T(8,128)(2,1)} %pad_maximum_fusion.18), channel_id=1, source_target_pairs={{0,8},{4,12},{8,0},{12,4},{16,24},{20,28},{24,16},{28,20},{1,9},{5... | collective-permute-start | bytes 2359304 | tf_op jit(solution)/shard_map/ppermute | solution.py:46
  281.9 23.2 %collective-permute-start.37 = (bf16[512,256]{1,0:T(8,128)(2,1)S(1)}, bf16[512,256]{1,0:T(8,128)(2,1)S(1)}, u32[]{:S(2)}, u32[]{:S(2)}) collective-permute-start(bf16[512,256]{1,0:T(8,128)(2,1)S(1)} %constant_dynamic-slice_fusion.14), channel_id=1, source_target_pairs={{0,8},{4,12},{8,0},{12,4},{16,24},{20,28},{24,16},{28,20},{1,9},{5... | collective-permute-start | bytes 786440 | tf_op jit(solution)/shard_map/ppermute | solution.py:46
  289.3 36.8 %collective-permute-start.43 = (bf16[256,1024]{1,0:T(8,128)(2,1)S(1)}, bf16[256,1024]{1,0:T(8,128)(2,1)S(1)}, u32[]{:S(2)}, u32[]{:S(2)}) collective-permute-start(bf16[256,1024]{1,0:T(8,128)(2,1)S(1)} %constant_dynamic-slice_fusion.11), channel_id=1, source_target_pairs={{0,8},{4,12},{8,0},{12,4},{16,24},{20,28},{24,16},{28,20},{1,9},{5... | collective-permute-start | bytes 1572872 | tf_op jit(solution)/shard_map/ppermute | solution.py:46
  291.4 17.3 %collective-permute-start.31 = (bf16[512,256]{1,0:T(8,128)(2,1)S(1)}, bf16[512,256]{1,0:T(8,128)(2,1)S(1)}, u32[]{:S(2)}, u32[]{:S(2)}) collective-permute-start(bf16[512,256]{1,0:T(8,128)(2,1)S(1)} %constant_dynamic-slice_fusion.17), channel_id=1, source_target_pairs={{0,8},{4,12},{8,0},{12,4},{16,24},{20,28},{24,16},{28,20},{1,9},{5... | collective-permute-start | bytes 786440 | tf_op jit(solution)/shard_map/ppermute | solution.py:46
  296.8 33.8 %collective-permute-start.25 = (bf16[512,512]{1,0:T(8,128)(2,1)S(1)}, bf16[512,512]{1,0:T(8,128)(2,1)S(1)}, u32[]{:S(2)}, u32[]{:S(2)}) collective-permute-start(bf16[512,512]{1,0:T(8,128)(2,1)S(1)} %constant_dynamic-slice_fusion.20), channel_id=1, source_target_pairs={{0,4},{4,0},{8,12},{12,8},{16,20},{20,16},{24,28},{28,24},{1,5},{5... | collective-permute-start | bytes 1572872 | tf_op jit(solution)/shard_map/ppermute | solution.py:46
  299.8 67.5 %collective-permute-start.18 = (bf16[2,1,256,1024]{3,2,1,0:T(8,128)(2,1)S(1)}, bf16[2,1,256,1024]{3,2,1,0:T(8,128)(2,1)S(1)}, u32[]{:S(2)}, u32[]{:S(2)}) collective-permute-start(bf16[2,1,256,1024]{3,2,1,0:T(8,128)(2,1)S(1)} %constant_dynamic-slice_fusion.21), channel_id=1, source_target_pairs={{0,1},{1,0},{2,3},{3,2},{4,5},{5,4},{6,7},{7,6},{8,9},{9,8},{10,11... | collective-permute-start | bytes 3145736 | tf_op jit(solution)/shard_map/ppermute | solution.py:46
  305.2 12.8 %collective-permute-start.38 = (bf16[256,256]{1,0:T(8,128)(2,1)S(1)}, bf16[256,256]{1,0:T(8,128)(2,1)S(1)}, u32[]{:S(2)}, u32[]{:S(2)}) collective-permute-start(bf16[256,256]{1,0:T(8,128)(2,1)S(1)} %constant_dynamic-slice_fusion.13), channel_id=1, source_target_pairs={{0,16},{4,20},{8,24},{12,28},{16,0},{20,4},{24,8},{28,12},{1,17},{... | collective-permute-start | bytes 393224 | tf_op jit(solution)/shard_map/ppermute | solution.py:46
  308.9 11.6 %collective-permute-start.32 = (bf16[256,256]{1,0:T(8,128)(2,1)S(1)}, bf16[256,256]{1,0:T(8,128)(2,1)S(1)}, u32[]{:S(2)}, u32[]{:S(2)}) collective-permute-start(bf16[256,256]{1,0:T(8,128)(2,1)S(1)} %constant_dynamic-slice_fusion.16), channel_id=1, source_target_pairs={{0,16},{4,20},{8,24},{12,28},{16,0},{20,4},{24,8},{28,12},{1,17},{... | collective-permute-start | bytes 393224 | tf_op jit(solution)/shard_map/ppermute | solution.py:46
  318.1 4.3 %collective-permute-start.39 = (bf16[128,256]{1,0:T(8,128)(2,1)S(1)}, bf16[128,256]{1,0:T(8,128)(2,1)S(1)}, u32[]{:S(2)}, u32[]{:S(2)}) collective-permute-start(bf16[128,256]{1,0:T(8,128)(2,1)S(1)} %constant_dynamic-slice_fusion.12), channel_id=1, source_target_pairs={{0,4},{4,0},{8,12},{12,8},{16,20},{20,16},{24,28},{28,24},{1,5},{5... | collective-permute-start | bytes 196616 | tf_op jit(solution)/shard_map/ppermute | solution.py:46
  320.6 4.5 %collective-permute-start.33 = (bf16[128,256]{1,0:T(8,128)(2,1)S(1)}, bf16[128,256]{1,0:T(8,128)(2,1)S(1)}, u32[]{:S(2)}, u32[]{:S(2)}) collective-permute-start(bf16[128,256]{1,0:T(8,128)(2,1)S(1)} %constant_dynamic-slice_fusion.15), channel_id=1, source_target_pairs={{0,4},{4,0},{8,12},{12,8},{16,20},{20,16},{24,28},{28,24},{1,5},{5... | collective-permute-start | bytes 196616 | tf_op jit(solution)/shard_map/ppermute | solution.py:46
  322.5 5.0 %collective-permute-start.40 = (bf16[128,256]{1,0:T(8,128)(2,1)S(1)}, bf16[128,256]{1,0:T(8,128)(2,1)S(1)}, u32[]{:S(2)}, u32[]{:S(2)}) collective-permute-start(bf16[128,256]{1,0:T(8,128)(2,1)S(1)} %add_convert_fusion.22), channel_id=1, source_target_pairs={{0,4},{4,0},{8,12},{12,8},{16,20},{20,16},{24,28},{28,24},{1,5},{5... | collective-permute-start | bytes 196616 | tf_op jit(solution)/shard_map/ppermute | solution.py:46
  325.1 4.3 %collective-permute-start.34 = (bf16[128,256]{1,0:T(8,128)(2,1)S(1)}, bf16[128,256]{1,0:T(8,128)(2,1)S(1)}, u32[]{:S(2)}, u32[]{:S(2)}) collective-permute-start(bf16[128,256]{1,0:T(8,128)(2,1)S(1)} %add_convert_fusion.23), channel_id=1, source_target_pairs={{0,4},{4,0},{8,12},{12,8},{16,20},{20,16},{24,28},{28,24},{1,5},{5... | collective-permute-start | bytes 196616 | tf_op jit(solution)/shard_map/ppermute | solution.py:46
  326.3 23.5 %collective-permute-start.44 = (bf16[128,1024]{1,0:T(8,128)(2,1)S(1)}, bf16[128,1024]{1,0:T(8,128)(2,1)S(1)}, u32[]{:S(2)}, u32[]{:S(2)}) collective-permute-start(bf16[128,1024]{1,0:T(8,128)(2,1)S(1)} %constant_dynamic-slice_fusion.10), channel_id=1, source_target_pairs={{0,16},{4,20},{8,24},{12,28},{16,0},{20,4},{24,8},{28,12},{1,17},{... | collective-permute-start | bytes 786440 | tf_op jit(solution)/shard_map/ppermute | solution.py:46
  327.5 19.5 %collective-permute-start.41 = (bf16[256,256]{1,0:T(8,128)(2,1)S(1)}, bf16[256,256]{1,0:T(8,128)(2,1)S(1)}, u32[]{:S(2)}, u32[]{:S(2)}) collective-permute-start(bf16[256,256]{1,0:T(8,128)(2,1)S(1)} %pad_maximum_fusion.35), channel_id=1, source_target_pairs={{0,16},{4,20},{8,24},{12,28},{16,0},{20,4},{24,8},{28,12},{1,17},{... | collective-permute-start | bytes 393224 | tf_op jit(solution)/shard_map/ppermute | solution.py:46
  329.5 20.2 %collective-permute-start.35 = (bf16[256,256]{1,0:T(8,128)(2,1)S(1)}, bf16[256,256]{1,0:T(8,128)(2,1)S(1)}, u32[]{:S(2)}, u32[]{:S(2)}) collective-permute-start(bf16[256,256]{1,0:T(8,128)(2,1)S(1)} %pad_maximum_fusion.34), channel_id=1, source_target_pairs={{0,16},{4,20},{8,24},{12,28},{16,0},{20,4},{24,8},{28,12},{1,17},{... | collective-permute-start | bytes 393224 | tf_op jit(solution)/shard_map/ppermute | solution.py:46
  330.8 19.9 %collective-permute-start.26 = (bf16[256,512]{1,0:T(8,128)(2,1)S(1)}, bf16[256,512]{1,0:T(8,128)(2,1)S(1)}, u32[]{:S(2)}, u32[]{:S(2)}) collective-permute-start(bf16[256,512]{1,0:T(8,128)(2,1)S(1)} %constant_dynamic-slice_fusion.19), channel_id=1, source_target_pairs={{0,8},{4,12},{8,0},{12,4},{16,24},{20,28},{24,16},{28,20},{1,9},{5... | collective-permute-start | bytes 786440 | tf_op jit(solution)/shard_map/ppermute | solution.py:46
  347.1 17.9 %collective-permute-start.42 = (bf16[512,256]{1,0:T(8,128)(2,1)S(1)}, bf16[512,256]{1,0:T(8,128)(2,1)S(1)}, u32[]{:S(2)}, u32[]{:S(2)}) collective-permute-start(bf16[512,256]{1,0:T(8,128)(2,1)S(1)} %pad_maximum_fusion.32), channel_id=1, source_target_pairs={{0,8},{4,12},{8,0},{12,4},{16,24},{20,28},{24,16},{28,20},{1,9},{5... | collective-permute-start | bytes 786440 | tf_op jit(solution)/shard_map/ppermute | solution.py:46
  349.8 16.4 %collective-permute-start.36 = (bf16[512,256]{1,0:T(8,128)(2,1)S(1)}, bf16[512,256]{1,0:T(8,128)(2,1)S(1)}, u32[]{:S(2)}, u32[]{:S(2)}) collective-permute-start(bf16[512,256]{1,0:T(8,128)(2,1)S(1)} %pad_maximum_fusion.31), channel_id=1, source_target_pairs={{0,8},{4,12},{8,0},{12,4},{16,24},{20,28},{24,16},{28,20},{1,9},{5... | collective-permute-start | bytes 786440 | tf_op jit(solution)/shard_map/ppermute | solution.py:46
  350.0 5.5 %collective-permute-start.45 = (bf16[64,1024]{1,0:T(8,128)(2,1)S(1)}, bf16[64,1024]{1,0:T(8,128)(2,1)S(1)}, u32[]{:S(2)}, u32[]{:S(2)}) collective-permute-start(bf16[64,1024]{1,0:T(8,128)(2,1)S(1)} %constant_dynamic-slice_fusion.9), channel_id=1, source_target_pairs={{0,4},{4,0},{8,12},{12,8},{16,20},{20,16},{24,28},{28,24},{1,5},{5... | collective-permute-start | bytes 393224 | tf_op jit(solution)/shard_map/ppermute | solution.py:46
  350.8 10.7 %collective-permute-start.27 = (bf16[128,512]{1,0:T(8,128)(2,1)S(1)}, bf16[128,512]{1,0:T(8,128)(2,1)S(1)}, u32[]{:S(2)}, u32[]{:S(2)}) collective-permute-start(bf16[128,512]{1,0:T(8,128)(2,1)S(1)} %constant_dynamic-slice_fusion.18), channel_id=1, source_target_pairs={{0,16},{4,20},{8,24},{12,28},{16,0},{20,4},{24,8},{28,12},{1,17},{... | collective-permute-start | bytes 393224 | tf_op jit(solution)/shard_map/ppermute | solution.py:46
  355.5 13.9 %collective-permute-start.46 = (bf16[64,1024]{1,0:T(8,128)(2,1)S(1)}, bf16[64,1024]{1,0:T(8,128)(2,1)S(1)}, u32[]{:S(2)}, u32[]{:S(2)}) collective-permute-start(bf16[64,1024]{1,0:T(8,128)(2,1)S(1)} %add_convert_fusion.18), channel_id=1, source_target_pairs={{0,4},{4,0},{8,12},{12,8},{16,20},{20,16},{24,28},{28,24},{1,5},{5... | collective-permute-start | bytes 393224 | tf_op jit(solution)/shard_map/ppermute | solution.py:46
  361.5 13.6 %collective-permute-start.28 = (bf16[128,512]{1,0:T(8,128)(2,1)S(1)}, bf16[128,512]{1,0:T(8,128)(2,1)S(1)}, u32[]{:S(2)}, u32[]{:S(2)}) collective-permute-start(bf16[128,512]{1,0:T(8,128)(2,1)S(1)} %add_convert_fusion.21), channel_id=1, source_target_pairs={{0,16},{4,20},{8,24},{12,28},{16,0},{20,4},{24,8},{28,12},{1,17},{... | collective-permute-start | bytes 393224 | tf_op jit(solution)/shard_map/ppermute | solution.py:46
  367.8 14.5 %collective-permute-start.19 = (bf16[256,1024]{1,0:T(8,128)(2,1)S(1)}, bf16[256,1024]{1,0:T(8,128)(2,1)S(1)}, u32[]{:S(2)}, u32[]{:S(2)}) collective-permute-start(bf16[256,1024]{1,0:T(8,128)(2,1)S(1)} %fusion.62), channel_id=1, source_target_pairs={{0,2},{1,3},{2,0},{3,1},{4,6},{5,7},{6,4},{7,5},{8,10},{9,11},{10,... | collective-permute-start | bytes 1572872 | tf_op jit(solution)/shard_map/ppermute | solution.py:46
  369.4 12.7 %collective-permute-start.47 = (bf16[128,1024]{1,0:T(8,128)(2,1)S(1)}, bf16[128,1024]{1,0:T(8,128)(2,1)S(1)}, u32[]{:S(2)}, u32[]{:S(2)}) collective-permute-start(bf16[128,1024]{1,0:T(8,128)(2,1)S(1)} %pad_maximum_fusion.33), channel_id=1, source_target_pairs={{0,16},{4,20},{8,24},{12,28},{16,0},{20,4},{24,8},{28,12},{1,17},{... | collective-permute-start | bytes 786440 | tf_op jit(solution)/shard_map/ppermute | solution.py:46
  375.2 10.4 %collective-permute-start.29 = (bf16[256,512]{1,0:T(8,128)(2,1)S(1)}, bf16[256,512]{1,0:T(8,128)(2,1)S(1)}, u32[]{:S(2)}, u32[]{:S(2)}) collective-permute-start(bf16[256,512]{1,0:T(8,128)(2,1)S(1)} %pad_maximum_fusion.30), channel_id=1, source_target_pairs={{0,8},{4,12},{8,0},{12,4},{16,24},{20,28},{24,16},{28,20},{1,9},{5... | collective-permute-start | bytes 786440 | tf_op jit(solution)/shard_map/ppermute | solution.py:46
  382.9 20.4 %collective-permute-start.48 = (bf16[256,1024]{1,0:T(8,128)(2,1)S(1)}, bf16[256,1024]{1,0:T(8,128)(2,1)S(1)}, u32[]{:S(2)}, u32[]{:S(2)}) collective-permute-start(bf16[256,1024]{1,0:T(8,128)(2,1)S(1)} %pad_maximum_fusion.26), channel_id=1, source_target_pairs={{0,8},{4,12},{8,0},{12,4},{16,24},{20,28},{24,16},{28,20},{1,9},{5... | collective-permute-start | bytes 1572872 | tf_op jit(solution)/shard_map/ppermute | solution.py:46
  384.1 3.7 collective-permute-start.21
  387.8 3.8 collective-permute-start.22
  388.4 16.7 %collective-permute-start.30 = (bf16[512,512]{1,0:T(8,128)(2,1)S(1)}, bf16[512,512]{1,0:T(8,128)(2,1)S(1)}, u32[]{:S(2)}, u32[]{:S(2)}) collective-permute-start(bf16[512,512]{1,0:T(8,128)(2,1)S(1)} %pad_maximum_fusion.25), channel_id=1, source_target_pairs={{0,4},{4,0},{8,12},{12,8},{16,20},{20,16},{24,28},{28,24},{1,5},{5... | collective-permute-start | bytes 1572872 | tf_op jit(solution)/shard_map/ppermute | solution.py:46
  391.6 6.0 %collective-permute-start.23 = (f32[2304]{0:T(1024)S(1)}, f32[2304]{0:T(1024)S(1)}, u32[]{:S(2)}, u32[]{:S(2)}) collective-permute-start(f32[2304]{0:T(1024)S(1)} %add.375), channel_id=1, source_target_pairs={{0,8},{4,12},{8,0},{12,4},{16,24},{20,28},{24,16},{28,20},{1,9},{5... | collective-permute-start | bytes 27656 | tf_op jit(solution)/shard_map/ppermute | solution.py:46
  397.6 4.6 %collective-permute-start.24 = (f32[2304]{0:T(1024)S(1)}, f32[2304]{0:T(1024)S(1)}, u32[]{:S(2)}, u32[]{:S(2)}) collective-permute-start(f32[2304]{0:T(1024)S(1)} %add.376), channel_id=1, source_target_pairs={{0,16},{4,20},{8,24},{12,28},{16,0},{20,4},{24,8},{28,12},{1,17},{... | collective-permute-start | bytes 27656 | tf_op jit(solution)/shard_map/ppermute | solution.py:46
  (82 other events, 492.0 us)

commit v2 on v0

v2 whole, which is shorter than its diff:
```python
import jax
import jax.numpy as jnp
from jax import lax
from jax.experimental import pallas as pl
from jax.experimental.pallas import tpu as pltpu
from jax.sharding import PartitionSpec as P

HEAD_SIZE = 128
BLOCK_ROWS = 256
epsilon = 1e-06
rotary_base = 1000000.0
masked_score = -1e30


def rotary_tables(every_row):
    half_width = HEAD_SIZE // 2
    frequency = rotary_base ** (-(jnp.arange(half_width, dtype=jnp.float32) * 2.0) / HEAD_SIZE)
    angles = jnp.arange(every_row, dtype=jnp.float32)[:, None] * frequency[None, :]
    cosine = jnp.cos(angles)
    sine = jnp.sin(angles)
    return (
        jnp.concatenate([cosine, cosine], axis=-1),
        jnp.concatenate([-sine, sine], axis=-1),
    )


def turned(values):
    return pltpu.roll(values, HEAD_SIZE // 2, 1)


def shaped(raw, gain, cosine, sine):
    normed = raw * lax.rsqrt(jnp.mean(raw * raw, axis=-1, keepdims=True) + epsilon) * gain
    return normed * cosine + turned(normed) * sine


def shaped_back(grad, raw, gain, cosine, sine):
    factor = lax.rsqrt(jnp.mean(raw * raw, axis=-1, keepdims=True) + epsilon)
    unit = raw * factor
    grad_normed = grad * cosine - turned(grad) * sine
    grad_gain = jnp.sum(grad_normed * unit, axis=0, keepdims=True)
    scaled = grad_normed * gain
    grad_raw = factor * (scaled - unit * jnp.mean(scaled * unit, axis=-1, keepdims=True))
    return grad_raw, grad_gain


def dot(left, right, left_dim, right_dim):
    return lax.dot_general(
        left, right, (((left_dim,), (right_dim,)), ((), ())), preferred_element_type=jnp.float32
    )


def heads_kernel(
    rows_ref, wq_ref, wk_ref, wv_ref, q_gain_ref, k_gain_ref, cos_ref, sin_ref,
    raw_q_ref, raw_k_ref, query_ref, key_ref, value_ref,
):
    rows = rows_ref[...]
    cosine = cos_ref[...]
    sine = sin_ref[...]
    value_ref[...] = dot(rows, wv_ref[...], 1, 0).astype(jnp.bfloat16)
    for weight_ref, gain_ref, raw_ref, out_ref in (
        (wq_ref, q_gain_ref, raw_q_ref, query_ref),
        (wk_ref, k_gain_ref, raw_k_ref, key_ref),
    ):
        raw = dot(rows, weight_ref[...], 1, 0)
        raw_ref[...] = raw
        for head in range(raw.shape[1] // HEAD_SIZE):
            cut = slice(head * HEAD_SIZE, (head + 1) * HEAD_SIZE)
            out_ref[:, cut] = shaped(raw[:, cut], gain_ref[...], cosine, sine).astype(jnp.bfloat16)


def project_heads(rows, w_query, key_weight, value_weight, q_gain, k_gain, cosine, sine):
    every_row, width = rows.shape
    block = BLOCK_ROWS
    q_cols, k_cols = w_query.shape[1], key_weight.shape[1]

    def by_row(cols):
        return pl.BlockSpec((block, cols), lambda i: (i, 0))

    def whole(shape):
        return pl.BlockSpec(shape, lambda i: (0, 0))

    return pl.pallas_call(
        heads_kernel,
        grid=(every_row // block,),
        in_specs=[
            by_row(width),
            whole(w_query.shape),
            whole(key_weight.shape),
            whole(value_weight.shape),
            whole((1, HEAD_SIZE)),
            whole((1, HEAD_SIZE)),
            by_row(HEAD_SIZE),
            by_row(HEAD_SIZE),
        ],
        out_specs=[by_row(q_cols), by_row(k_cols), by_row(q_cols), by_row(k_cols), by_row(k_cols)],
        out_shape=[
            jax.ShapeDtypeStruct((every_row, q_cols), jnp.float32),
            jax.ShapeDtypeStruct((every_row, k_cols), jnp.float32),
            jax.ShapeDtypeStruct((every_row, q_cols), jnp.bfloat16),
            jax.ShapeDtypeStruct((every_row, k_cols), jnp.bfloat16),
            jax.ShapeDtypeStruct((every_row, k_cols), jnp.bfloat16),
        ],
        name="project_heads",
    )(
        rows, w_query, key_weight, value_weight,
        q_gain.reshape(1, HEAD_SIZE), k_gain.reshape(1, HEAD_SIZE), cosine, sine,
    )


def masked_exponents(query, key, first_row, length):
    scores = dot(query, key, 1, 1) * HEAD_SIZE ** (-0.5)
    row = first_row + lax.broadcasted_iota(jnp.int32, scores.shape, 0)
    place = lax.broadcasted_iota(jnp.int32, scores.shape, 1)
    allowed = (place <= row) & (place < length)
    scores = jnp.where(allowed, scores, masked_score)
    exponents = jnp.exp(scores - jnp.max(scores, axis=-1, keepdims=True))
    return exponents, 1.0 / jnp.sum(exponents, axis=-1, keepdims=True)


def attend_kernel(length_ref, query_ref, key_ref, value_ref, out_ref):
    length = length_ref[0]
    every_row = key_ref.shape[0]
    for first_row in range(0, every_row, BLOCK_ROWS):
        last = first_row + BLOCK_ROWS
        exponents, inverse = masked_exponents(
            query_ref[first_row:last, :], key_ref[:last, :], first_row, length
        )
        weights = (exponents * inverse).astype(jnp.bfloat16)
        out_ref[first_row:last, :] = dot(weights, value_ref[:last, :], 1, 0).astype(jnp.bfloat16)


def attend(lengths, query, key, value):
    every_row, q_cols = query.shape
    group = q_cols // key.shape[1]

    def head_spec(share):
        return pl.BlockSpec((every_row, HEAD_SIZE), lambda h, lengths: (0, h // share))

    return pl.pallas_call(
        attend_kernel,
        grid_spec=pltpu.PrefetchScalarGridSpec(
            num_scalar_prefetch=1,
            grid=(q_cols // HEAD_SIZE,),
            in_specs=[head_spec(1), head_spec(group), head_spec(group)],
            out_specs=head_spec(1),
        ),
        out_shape=jax.ShapeDtypeStruct((every_row, q_cols), jnp.bfloat16),
        name="attend",
    )(lengths, query, key, value)


def attend_back_kernel(
    length_ref, query_ref, key_ref, value_ref, grad_ref, raw_q_ref, raw_k_ref,
    q_gain_ref, k_gain_ref, cos_ref, sin_ref,
    out_ref, gain_q_ref, gain_k_ref,
    key_acc, value_acc,
):
    length = length_ref[0]
    every_row = key_ref.shape[0]
    group = query_ref.shape[1] // HEAD_SIZE
    scaling = HEAD_SIZE ** (-0.5)
    key_acc[...] = jnp.zeros_like(key_acc)
    value_acc[...] = jnp.zeros_like(value_acc)
    gain_q = jnp.zeros((1, HEAD_SIZE), jnp.float32)
    for head in range(group):
        cut = slice(head * HEAD_SIZE, (head + 1) * HEAD_SIZE)
        for first_row in range(0, every_row, BLOCK_ROWS):
            last = first_row + BLOCK_ROWS
            query = query_ref[first_row:last, cut]
            grad = grad_ref[first_row:last, cut]
            exponents, inverse = masked_exponents(query, key_ref[:last, :], first_row, length)
            probs = exponents * inverse
            grad_probs = dot(grad, value_ref[:last, :], 1, 1)
            delta = jnp.sum(grad_probs * probs, axis=-1, keepdims=True)
            grad_scores = (probs * (grad_probs - delta)).astype(jnp.bfloat16)
            grad_query = dot(grad_scores, key_ref[:last, :], 1, 0) * scaling
            key_acc[:last, :] += dot(grad_scores, query, 0, 0)
            value_acc[:last, :] += dot(probs.astype(jnp.bfloat16), grad, 0, 0)
            grad_raw, grad_gain = shaped_back(
                grad_query, raw_q_ref[first_row:last, cut], q_gain_ref[...],
                cos_ref[first_row:last, :], sin_ref[first_row:last, :],
            )
            out_ref[first_row:last, cut] = grad_raw.astype(jnp.bfloat16)
            gain_q += grad_gain
    gain_q_ref[...] = gain_q
    grad_raw, grad_gain = shaped_back(
        key_acc[...] * scaling, raw_k_ref[...], k_gain_ref[...], cos_ref[...], sin_ref[...]
    )
    key_col = group * HEAD_SIZE
    value_col = key_col + HEAD_SIZE
    out_ref[:, key_col:value_col] = grad_raw.astype(jnp.bfloat16)
    out_ref[:, value_col:] = value_acc[...].astype(jnp.bfloat16)
    gain_k_ref[...] = grad_gain


def attend_back(
    kv_head, lengths, query, key, value, grad, raw_q, raw_k, q_gain, k_gain, cosine, sine
):
    every_row, q_cols = query.shape
    group_cols = q_cols // key.shape[1] * HEAD_SIZE

    def cut(cols):
        return pl.BlockSpec((every_row, cols), lambda i, lengths: (0, kv_head))

    def whole(rows, cols):
        return pl.BlockSpec((rows, cols), lambda i, lengths: (0, 0))

    return pl.pallas_call(
        attend_back_kernel,
        grid_spec=pltpu.PrefetchScalarGridSpec(
            num_scalar_prefetch=1,
            grid=(1,),
            in_specs=[
                cut(group_cols), cut(HEAD_SIZE), cut(HEAD_SIZE), cut(group_cols),
                cut(group_cols), cut(HEAD_SIZE),
                whole(1, HEAD_SIZE), whole(1, HEAD_SIZE),
                whole(every_row, HEAD_SIZE), whole(every_row, HEAD_SIZE),
            ],
            out_specs=[
                whole(every_row, group_cols + 2 * HEAD_SIZE),
                whole(1, HEAD_SIZE), whole(1, HEAD_SIZE),
            ],
            scratch_shapes=[
                pltpu.VMEM((every_row, HEAD_SIZE), jnp.float32),
                pltpu.VMEM((every_row, HEAD_SIZE), jnp.float32),
            ],
        ),
        out_shape=[
            jax.ShapeDtypeStruct((every_row, group_cols + 2 * HEAD_SIZE), jnp.bfloat16),
            jax.ShapeDtypeStruct((1, HEAD_SIZE), jnp.float32),
            jax.ShapeDtypeStruct((1, HEAD_SIZE), jnp.float32),
        ],
        name="attend_back",
    )(
        lengths, query, key, value, grad, raw_q, raw_k,
        q_gain.reshape(1, HEAD_SIZE), k_gain.reshape(1, HEAD_SIZE), cosine, sine,
    )


def rms_norm(values, gain):
    return values * lax.rsqrt(jnp.mean(values * values, axis=-1, keepdims=True) + epsilon) * gain


def swiglu(gate_proj, up_proj):
    return gate_proj / (1.0 + jnp.exp(-gate_proj)) * up_proj


def matmul(left, right, left_dim, right_dim):
    return dot(left, right, left_dim, right_dim).astype(jnp.bfloat16)


def bit_of(axis, bit):
    return (lax.axis_index(axis) >> bit) & 1


def swap(values, axis, bit):
    size = lax.axis_size(axis)
    return lax.ppermute(values, axis, [(i, i ^ (1 << bit)) for i in range(size)])


def bits(axis):
    return list(range((lax.axis_size(axis) - 1).bit_length()))


def ordered_pair(mine, other, flag):
    is_first = flag == 0
    return jnp.concatenate(
        [jnp.where(is_first, mine, other), jnp.where(is_first, other, mine)], axis=0
    )


def halves(values, flag):
    rows = values.shape[0] // 2
    sent = lax.dynamic_slice_in_dim(values, (1 - flag) * rows, rows, 0)
    kept = lax.dynamic_slice_in_dim(values, flag * rows, rows, 0)
    return sent, kept


def after(values, done):
    return lax.optimization_barrier((values, done))[0]


class Flight:
    def __init__(self, received, arrival):
        self.received = received
        self.arrival = arrival


class Order:
    def __init__(self):
        self.clock = 0.0
        self.token = None
        self.free = {}
        self.sums = []

    def gate(self, values):
        return values if self.token is None else after(values, self.token)

    def step(self, us, function, *inputs):
        out = function(*self.gate(inputs))
        self.token = out
        self.clock += us
        return out

    def send(self, values, axis, bit):
        size = values.size * values.dtype.itemsize
        if axis == "tensor" and bit == 0:
            us = size / 400e3
        else:
            us = 2 * size / 87e3 * (2 if axis == "dp" and bit > 1 else 1)
        values = self.gate(values)
        received = swap(values, axis, bit)
        self.token = values
        self.clock += 1.6
        start = max(self.clock, self.free.get((axis, bit), 0.0))
        self.free[axis, bit] = start + us
        return Flight(received, start + us + 1.0)

    def fill(self, until):
        while True:
            waiting = [one for one in self.sums if one.flight is not None]
            if not waiting:
                break
            one = min(waiting, key=lambda one: one.flight.arrival)
            if one.flight.arrival > max(self.clock, until - 3.0):
                break
            self.clock = max(self.clock, one.flight.arrival)
            one.advance()

    def land(self, flight):
        self.fill(flight.arrival)
        self.clock = max(self.clock, flight.arrival)
        received = self.gate(flight.received)
        self.token = received
        return received

    def finish(self):
        self.fill(float("inf"))


class DpSum:
    def __init__(self, order, values, first):
        count = len(bits("dp"))
        self.order = order
        self.turns = [(first + i) % count for i in range(count)]
        self.stage = 0
        self.part = values
        order.sums.append(self)
        self.launch()

    def launch(self):
        count = len(self.turns)
        if self.stage < count:
            bit = self.turns[self.stage]
            sent, self.kept = halves(self.part, bit_of("dp", bit))
        elif self.stage < 2 * count:
            bit = self.turns[2 * count - 1 - self.stage]
            sent = self.part
        else:
            self.flight = None
            return
        self.order.clock += 1.0
        self.flight = self.order.send(sent, "dp", bit)

    def advance(self):
        count = len(self.turns)
        received = self.order.gate(self.flight.received)
        if self.stage < count:
            self.part = (self.kept.astype(jnp.float32) + received.astype(jnp.float32)).astype(
                jnp.bfloat16
            )
        else:
            bit = self.turns[2 * count - 1 - self.stage]
            self.part = ordered_pair(self.part, received, bit_of("dp", bit))
        self.order.token = self.part
        self.stage += 1
        self.launch()


class GainSum:
    def __init__(self, order, values):
        self.order = order
        self.part = values
        self.turns = [(axis, bit) for axis in ("tensor", "dp") for bit in bits(axis)]
        order.sums.append(self)
        self.launch()

    def launch(self):
        self.flight = self.order.send(self.part, *self.turns.pop(0)) if self.turns else None

    def advance(self):
        self.part = self.part + self.order.gate(self.flight.received)
        self.order.token = self.part
        self.launch()


class Spread:
    def __init__(self, order, values):
        self.order = order
        self.values = values
        self.across = order.send(values, "tensor", 1)
        self.near = order.send(values, "tensor", 0)

    def land(self):
        core = bit_of("tensor", 0)
        side = bit_of("tensor", 1)
        across = self.order.land(self.across)
        far = self.order.send(across, "tensor", 0)
        near = self.order.gate(self.near.received)
        return self.order.step(
            4.0,
            lambda values, near, across, far: ordered_pair(
                ordered_pair(values, near, core), ordered_pair(across, far, core), side
            ),
            self.values, near, across, far.received,
        )


class Settle:
    def __init__(self, order, values):
        self.order = order
        core = bit_of("tensor", 0)
        rows = values.shape[0] // 4
        parts = values.reshape(2, 2, rows, values.shape[1])
        sent = lax.dynamic_slice_in_dim(parts, 1 - core, 1, 1)
        self.kept = lax.dynamic_slice_in_dim(parts, core, 1, 1)
        self.flight = order.send(sent, "tensor", 0)

    def cross(self):
        side = bit_of("tensor", 1)
        received = self.order.land(self.flight)
        pair = (self.kept.astype(jnp.float32) + received.astype(jnp.float32))[:, 0]
        away = lax.dynamic_slice_in_dim(pair, 1 - side, 1, 0)[0].astype(jnp.bfloat16)
        self.home = lax.dynamic_slice_in_dim(pair, side, 1, 0)[0]
        self.order.clock += 2.0
        self.flight = self.order.send(away, "tensor", 1)

    def land(self):
        return self.home + self.order.land(self.flight).astype(jnp.float32)


def body(
    tokens,
    cotangent,
    attn_gain,
    q_gain,
    k_gain,
    mlp_gain,
    w_query,
    key_weight,
    value_weight,
    w_out,
    w_gate,
    w_up,
    w_down,
    lengths,
):
    share_rows = tokens.shape[0]
    every_row = share_rows * lax.axis_size("tensor")
    kv_heads = key_weight.shape[1] // HEAD_SIZE
    group_cols = w_query.shape[1] // kv_heads
    length = lengths[0]
    first_row = lax.axis_index("tensor") * share_rows
    live_rows = (first_row + jnp.arange(share_rows, dtype=jnp.int32) < length)[:, None]
    order = Order()

    resid = tokens.astype(jnp.float32)
    gather_a = Spread(order, rms_norm(resid, attn_gain).astype(jnp.bfloat16))
    cosine, sine = rotary_tables(every_row)
    grad_out = jnp.where(live_rows, cotangent.astype(jnp.float32), 0.0)
    head_weights = [
        jnp.concatenate(
            [
                w_query[:, head * group_cols : (head + 1) * group_cols],
                key_weight[:, head * HEAD_SIZE : (head + 1) * HEAD_SIZE],
                value_weight[:, head * HEAD_SIZE : (head + 1) * HEAD_SIZE],
            ],
            axis=1,
        )
        for head in range(kv_heads)
    ]
    whole_a = gather_a.land()
    gather_ffn = Spread(order, grad_out.astype(jnp.bfloat16))
    raw_q, raw_k, query, key, value = order.step(
        7.5,
        lambda rows: project_heads(
            rows, w_query, key_weight, value_weight, q_gain, k_gain, cosine, sine
        ),
        whole_a,
    )
    attended = order.step(
        11.0, lambda query, key, value: attend(lengths, query, key, value), query, key, value
    )
    branch_out = order.step(1.5, lambda rows: matmul(rows, w_out, 1, 0), attended)
    settle_mixed = Settle(order, branch_out)
    settle_mixed.cross()
    whole_ffn = gather_ffn.land()
    grad_act = order.step(2.0, lambda rows: matmul(rows, w_down, 1, 1), whole_ffn)
    mixed = resid + settle_mixed.land()

    order.clock += 2.0
    whole_m = Spread(order, rms_norm(mixed, mlp_gain).astype(jnp.bfloat16)).land()

    def hidden(rows, grad_act):
        gate_proj = dot(rows, w_gate, 1, 0)
        up_proj = dot(rows, w_up, 1, 0)
        activated, swiglu_back = jax.vjp(swiglu, gate_proj, up_proj)
        grad_gate, grad_up = swiglu_back(grad_act.astype(jnp.float32))
        return (
            activated.astype(jnp.bfloat16),
            grad_gate.astype(jnp.bfloat16),
            grad_up.astype(jnp.bfloat16),
        )

    activated, grad_gate, grad_up = order.step(7.5, hidden, whole_m, grad_act)
    grad_w_down = DpSum(
        order, order.step(2.0, lambda a, b: matmul(a, b, 0, 0), activated, whole_ffn), 0
    )
    grad_normed_m = order.step(
        4.0,
        lambda a, b: (dot(a, w_gate, 1, 1) + dot(b, w_up, 1, 1)).astype(jnp.bfloat16),
        grad_gate, grad_up,
    )
    settle_m = Settle(order, grad_normed_m)
    settle_m.cross()
    grad_w_gate = DpSum(
        order, order.step(2.0, lambda a, b: matmul(a, b, 0, 0), whole_m, grad_gate), 0
    )
    up_grad = order.step(2.0, lambda a, b: matmul(a, b, 0, 0), whole_m, grad_up)
    layer_branch = order.step(2.0, lambda rows: matmul(rows, w_down, 1, 0), activated)
    _, mlp_norm_back = jax.vjp(rms_norm, mixed, mlp_gain)
    grad_mixed_norm, grad_mlp_gain = mlp_norm_back(settle_m.land())
    grad_mixed = grad_out + grad_mixed_norm
    order.clock += 2.0
    gather_branch = Spread(order, grad_mixed.astype(jnp.bfloat16))
    grad_w_up = DpSum(order, up_grad, 1)
    settle_out = Settle(order, layer_branch)
    grad_branch = gather_branch.land()

    grad_attended = order.step(2.0, lambda rows: matmul(rows, w_out, 1, 1), grad_branch)
    settle_out.cross()
    order.fill(order.clock)
    grad_w_out = DpSum(
        order, order.step(2.0, lambda a, b: matmul(a, b, 0, 0), attended, grad_branch), 0
    )
    heads = []
    for head in range(kv_heads):
        out, head_q_gain, head_k_gain = order.step(
            12.5,
            lambda grad: attend_back(
                head, lengths, query, key, value, grad, raw_q, raw_k,
                q_gain, k_gain, cosine, sine,
            ),
            grad_attended,
        )
        grad_weights = DpSum(
            order, order.step(2.0, lambda a, b: matmul(a, b, 0, 0), whole_a, out), head % 2
        )
        heads.append((out, grad_weights, head_q_gain[0], head_k_gain[0]))
        order.fill(order.clock)
    grad_normed_a = order.step(
        3.0,
        lambda outs: sum(
            dot(out, weights, 1, 1) for out, weights in zip(outs, head_weights)
        ).astype(jnp.bfloat16),
        [one[0] for one in heads],
    )
    settle_a = Settle(order, grad_normed_a)
    settle_a.cross()
    layer_out = jnp.where(live_rows, mixed + settle_out.land(), 0.0)
    _, attn_norm_back = jax.vjp(rms_norm, resid, attn_gain)
    grad_resid_norm, grad_attn_gain = attn_norm_back(settle_a.land())
    tokens_grad = grad_mixed + grad_resid_norm
    gains = GainSum(
        order,
        jnp.concatenate(
            [
                grad_attn_gain,
                grad_mlp_gain,
                sum(one[2] for one in heads),
                sum(one[3] for one in heads),
            ]
        ),
    )
    order.finish()

    width = attn_gain.shape[0]
    grad_attn_gain, grad_mlp_gain, grad_q_gain, grad_k_gain = jnp.split(
        gains.part, [width, 2 * width, 2 * width + HEAD_SIZE]
    )
    by_head = [one[1].part.astype(jnp.float32) for one in heads]
    value_col = group_cols + HEAD_SIZE
    return (
        layer_out,
        tokens_grad,
        grad_attn_gain,
        grad_q_gain,
        grad_k_gain,
        grad_mlp_gain,
        jnp.concatenate([one[:, :group_cols] for one in by_head], axis=1),
        jnp.concatenate([one[:, group_cols:value_col] for one in by_head], axis=1),
        jnp.concatenate([one[:, value_col:] for one in by_head], axis=1),
        grad_w_out.part.astype(jnp.float32),
        grad_w_gate.part.astype(jnp.float32),
        grad_w_up.part.astype(jnp.float32),
        grad_w_down.part.astype(jnp.float32),
    )


def solution(mesh):
    return jax.shard_map(
        body,
        mesh=mesh,
        in_specs=(
            P(("dp", "tensor"), None),
            P(("dp", "tensor"), None),
            P(),
            P(),
            P(),
            P(),
            P(None, "tensor"),
            P(None, "tensor"),
            P(None, "tensor"),
            P("tensor", None),
            P(None, "tensor"),
            P(None, "tensor"),
            P("tensor", None),
            P("dp"),
        ),
        out_specs=(
            P(("dp", "tensor"), None),
            P(("dp", "tensor"), None),
            P(),
            P(),
            P(),
            P(),
            P(None, "tensor"),
            P(None, "tensor"),
            P(None, "tensor"),
            P("tensor", None),
            P(None, "tensor"),
            P(None, "tensor"),
            P("tensor", None),
        ),
        check_vma=False,
    )
```

time: 944 us -> 390 us (0.41)
  waiting for transfers between devices: 665 us -> 145 us
  matrix products: 101 us -> 35.3 us
  starting transfers between devices: 11.6 us -> 73 us
  blocking collectives: 45.1 us -> 0 us
  Pallas kernels: 0 us -> 43.8 us
  local copies, waits for them, and re-layouts: 51.8 us -> 29.4 us
  between operations: 15.5 us -> 3.3 us
  other arithmetic: 43.8 us -> 53.9 us
    psum x1 -> x0, waiting for transfers between devices: 447 us -> none  [body(): lax.psum((grad_w_query, grad_w_key, grad_w_value, grad_w_out, grad_w_gate...]
    reduce_scatter x4 -> x0, waiting for transfers between devices: 150 us -> none  [the longest x2 89.4 us: settle(): return lax.psum_scatter(values, 'tensor', scatter_dimension=0, tiled=True)]
    ppermute x0 -> x61, waiting for transfers between devices: none -> 145 us  [swap(): return lax.ppermute(values, axis, [(i, i ^ 1 << bit) for i in range(size)])]
    ppermute x0 -> x61, starting transfers between devices: none -> 73 us  [swap(): return lax.ppermute(values, axis, [(i, i ^ 1 << bit) for i in range(size)])]
    all_gather x4 -> x0, waiting for transfers between devices: 67.2 us -> none  [the longest x2 42 us: spread(): return lax.all_gather(values, 'tensor', axis=0, tiled=True)]
    dot_general x35 -> x16, matrix products: 101 us -> 35.3 us  [dot(): lax.dot_general(left, right, (((left_dim,), (right_dim,)), ((), ())), pre...]
    psum x1 -> x0, blocking collectives: 45.1 us -> none  [body(): lax.psum((grad_attn_gain, grad_q_gain, grad_k_gain, grad_mlp_gain), ('dp'...]
    pallas_call x0 -> x4, Pallas kernels: none -> 43.8 us  [the longest x2 25.5 us: attend_back(): pl.pallas_call(attend_back_kernel, grid_spec=pltpu.PrefetchScalarGridSpec...]
  transfers between devices with their start and end apart: 9 -> 61, of which waited for: 9 -> 23; matrix products, arithmetic and copies ran while one was open for 5% -> 19% of each run, Pallas kernels for 0% -> 7%
where the time goes in v2:
time: 390 us; the launch traced here: 384 us
  waiting for transfers between devices  145 us (37%)
  starting transfers between devices  73 us (19%)
  other arithmetic  53.9 us (14%)
  Pallas kernels  43.8 us (11%)
  matrix products  35.3 us (9%)
  local copies, waits for them, and re-layouts  29.4 us (8%)
    ppermute x61, waiting for transfers between devices, swap(): return lax.ppermute(values, axis, [(i, i ^ 1 << bit) for i in range(size)])  145 us
    ppermute x61, starting transfers between devices, swap(): return lax.ppermute(values, axis, [(i, i ^ 1 << bit) for i in range(size)])  73 us
    dot_general x16, matrix products, dot(): lax.dot_general(left, right, (((left_dim,), (right_dim,)), ((), ())), pre...  35.3 us
    pallas_call x2, Pallas kernels, attend_back(): pl.pallas_call(attend_back_kernel, grid_spec=pltpu.PrefetchScalarGridSpec...  25.5 us
    unnamed x130, local copies, waits for them, and re-layouts  13.8 us
    select_n x29, other arithmetic, ordered_pair(): jnp.where(is_first, mine, other)  12.5 us
    pallas_call x1, Pallas kernels, attend(): pl.pallas_call(attend_kernel, grid_spec=pltpu.PrefetchScalarGridSpec(num_...  11 us
    convert_element_type x18, other arithmetic, advance(): (self.kept.astype(jnp.float32) + received.astype(jnp.float32)).astype(jnp...  7.95 us
  transfers between devices with their start and end apart: 61, of which 23 were waited for; matrix products, arithmetic and copies ran while one was open for 19% of the time, Pallas kernels for 7%

profile of v2, /device:TPU:0, one launch (start us, length us, event | category | flops | bytes accessed | tf_op | source)
XLA Modules:
  0.0 384.0 jit_solution(4606758229556713027)
XLA Ops:
  3.3 3.0 collective-permute-start.1
  6.3 12.0 %collective-permute-done.1 = bf16[256,1024]{1,0:T(8,128)(2,1)} collective-permute-done((bf16[256,1024]{1,0:T(8,128)(2,1)S(1)}, bf16[256,1024]{1,0:T(8,128)(2,1)}, u32[]{:S(2)}, u32[]{:S(2)}) %collective-permute-start.1) | collective-permute-done | bytes 524320 | tf_op jit(solution)/shard_map/ppermute | solution.py:258
  18.3 2.7 fusion.29
  21.7 2.7 pad_maximum_fusion.23
  28.1 7.3 %project_heads.1 = (f32[1024,512]{1,0:T(8,128)}, f32[1024,256]{1,0:T(8,128)}, bf16[1024,512]{1,0:T(8,128)(2,1)}, bf16[1024,256]{1,0:T(8,128)(2,1)}, bf16[1024,256]{1,0:T(8,128)(2,1)}) custom-call(bf16[1024,1024]{1,0:T(8,128)(2,1)} %pad_maximum_fusion.rows_ref, bf16[1024,512]{1,0:T(8,128)(2,1)} %wq_ref.1, bf16[1024,256]{1,0:T(8,128)(2,1)} %wk_ref.1, ...), custom_call_target="tpu_custom_call" | custom-call | tf_op jit(solution)/shard_map/project_heads/pallas_call | solution.py:82
  35.4 11.0 %attend.1 = bf16[1024,512]{1,0:T(8,128)(2,1)} custom-call(s32[1]{0:T(128)} %copy.27.length_ref, bf16[1024,512]{1,0:T(8,128)(2,1)} %get-tuple-element.201.query_ref, bf16[1024,256]{1,0:T(8,128)(2,1)} %get-tuple-element.202.key_ref, bf16[1024,256]{1,0:T(8,128)(2,1)} %get-tuple-element.203.value_ref), custom_call_target="tpu_custom_call" | custom-call | tf_op jit(solution)/shard_map/attend/pallas_call | solution.py:139
  46.4 2.8 convolution_convert_fusion
  52.1 1.8 collective-permute-start.6
  54.7 1.9 convert_add_fusion.3
  58.8 7.1 %collective-permute-done.6 = bf16[256,1024]{1,0:T(8,128)(2,1)S(1)} collective-permute-done((bf16[256,1024]{1,0:T(8,128)(2,1)S(1)}, bf16[256,1024]{1,0:T(8,128)(2,1)S(1)}, u32[]{:S(2)}, u32[]{:S(2)}) %collective-permute-start.6) | collective-permute-done | bytes 524320 | tf_op jit(solution)/shard_map/ppermute | solution.py:258
  65.9 1.7 collective-permute-start.4
  71.2 3.0 convolution_convert_fusion.5
  74.2 6.3 %collective-permute-done.4 = bf16[256,1024]{1,0:T(8,128)(2,1)S(1)} collective-permute-done((bf16[256,1024]{1,0:T(8,128)(2,1)}, bf16[256,1024]{1,0:T(8,128)(2,1)S(1)}, u32[]{:S(2)}, u32[]{:S(2)}) %collective-permute-start.4) | collective-permute-done | bytes 524320 | tf_op jit(solution)/shard_map/ppermute | solution.py:258
  83.5 12.1 %collective-permute-done.9 = bf16[256,1024]{1,0:T(8,128)(2,1)} collective-permute-done((bf16[256,1024]{1,0:T(8,128)(2,1)}, bf16[256,1024]{1,0:T(8,128)(2,1)}, u32[]{:S(2)}, u32[]{:S(2)}) %collective-permute-start.9) | collective-permute-done | bytes 524320 | tf_op jit(solution)/shard_map/ppermute | solution.py:258
  95.6 2.2 collective-permute-done.10
  102.5 1.8 fusion.48
  104.6 4.0 %add_convert_fusion.2 = (bf16[1024,768]{1,0:T(8,128)(2,1)S(1)}, bf16[1024,768]{1,0:T(8,128)(2,1)S(1)}, bf16[1024,768]{1,0:T(8,128)(2,1)S(1)}) fusion(f32[1024,768]{1,0:T(8,128)S(1)} %fusion.48, bf16[1024,768]{1,0:T(8,128)(2,1)S(1)} %copy-done.64, bf16[1024,1024]{1,0:T(8,128)(2,1)S(1)} %pad_maximum_fusion.2, bf16[1024,768]{1,0:T(8,128)(2,1)S(1)} %copy-done), kind=kOutput, calls=%fused_computation.5 | convolution fusion | flops 1625554944 | bytes 13107200 | tf_op jit(solution)/shard_map/dot_general | solution.py:47
  108.7 1.8 convolution_convert_fusion.4
  112.6 1.8 fusion.49
  114.5 1.8 add_convert_fusion.1
  118.8 1.8 collective-permute-start.13
  123.2 1.8 collective-permute-start.12
  125.1 1.9 convolution_convert_fusion.3
  128.7 1.9 convolution_convert_fusion.2
  130.6 1.8 convolution_convert_fusion.1
  132.4 7.0 %collective-permute-done.13 = bf16[384,1024]{1,0:T(8,128)(2,1)S(1)} collective-permute-done((bf16[384,1024]{1,0:T(8,128)(2,1)}, bf16[384,1024]{1,0:T(8,128)(2,1)S(1)}, u32[]{:S(2)}, u32[]{:S(2)}) %collective-permute-start.13) | collective-permute-done | bytes 786464 | tf_op jit(solution)/shard_map/ppermute | solution.py:258
  139.7 1.9 collective-permute-start.15
  144.7 5.2 %collective-permute-done.15 = bf16[192,1024]{1,0:T(8,128)(2,1)S(1)} collective-permute-done((bf16[192,1024]{1,0:T(8,128)(2,1)S(1)}, bf16[192,1024]{1,0:T(8,128)(2,1)S(1)}, u32[]{:S(2)}, u32[]{:S(2)}) %collective-permute-start.15) | collective-permute-done | bytes 393248 | tf_op jit(solution)/shard_map/ppermute | solution.py:258
  150.1 5.6 %collective-permute-done.19 = bf16[512,768]{1,0:T(8,128)(2,1)S(1)} collective-permute-done((bf16[512,768]{1,0:T(8,128)(2,1)S(1)}, bf16[512,768]{1,0:T(8,128)(2,1)S(1)}, u32[]{:S(2)}, u32[]{:S(2)}) %collective-permute-start.19) | collective-permute-done | bytes 786464 | tf_op jit(solution)/shard_map/ppermute | solution.py:258
  159.6 2.8 collective-permute-start.16
  166.4 2.3 convolution_convert_fusion.9.grad_ref
  168.7 3.1 collective-permute-done.16
  175.0 15.1 %collective-permute-done.22 = bf16[512,768]{1,0:T(8,128)(2,1)S(1)} collective-permute-done((bf16[512,768]{1,0:T(8,128)(2,1)S(1)}, bf16[512,768]{1,0:T(8,128)(2,1)S(1)}, u32[]{:S(2)}, u32[]{:S(2)}) %collective-permute-start.22) | collective-permute-done | bytes 786464 | tf_op jit(solution)/shard_map/ppermute | solution.py:258
  196.5 12.9 %attend_back.2 = (bf16[1024,512]{1,0:T(8,128)(2,1)}, f32[1,128]{1,0:T(1,128)}, f32[1,128]{1,0:T(1,128)}) custom-call(s32[1]{0:T(128)} %copy.27.length_ref, bf16[1024,512]{1,0:T(8,128)(2,1)} %get-tuple-element.201.query_ref, bf16[1024,256]{1,0:T(8,128)(2,1)} %get-tuple-element.202.key_ref, bf16[1024,256]{1,0:T(8,128)(2,1)} %get-tuple-element.203.value_ref, ...), custom_call_target="tpu_custom_call" | custom-call | tf_op jit(solution)/shard_map/attend_back/pallas_call | solution.py:208
  209.3 3.2 convolution_convert_fusion.7
  216.5 2.3 collective-permute-start.25
  222.8 1.9 collective-permute-start.32
  227.2 12.7 %attend_back.3 = (bf16[1024,512]{1,0:T(8,128)(2,1)}, f32[1,128]{1,0:T(1,128)}, f32[1,128]{1,0:T(1,128)}) custom-call(s32[1]{0:T(128)} %copy.27.length_ref, bf16[1024,512]{1,0:T(8,128)(2,1)} %get-tuple-element.201.query_ref, bf16[1024,256]{1,0:T(8,128)(2,1)} %get-tuple-element.202.key_ref, bf16[1024,256]{1,0:T(8,128)(2,1)} %get-tuple-element.203.value_ref, ...), custom_call_target="tpu_custom_call" | custom-call | tf_op jit(solution)/shard_map/attend_back/pallas_call | solution.py:208
  239.9 3.3 convolution_convert_fusion.6
  247.4 2.0 collective-permute-start.29
  250.9 4.1 %collective-permute-start.31 = (bf16[128,768]{1,0:T(8,128)(2,1)S(1)}, bf16[128,768]{1,0:T(8,128)(2,1)S(1)}, u32[]{:S(2)}, u32[]{:S(2)}) collective-permute-start(bf16[128,768]{1,0:T(8,128)(2,1)S(1)} %add_convert_fusion.16), channel_id=1, source_target_pairs={{0,16},{4,20},{8,24},{12,28},{16,0},{20,4},{24,8},{28,12},{1,17},{... | collective-permute-start | bytes 589832 | tf_op jit(solution)/shard_map/ppermute | solution.py:258
  255.0 1.8 collective-permute-start.40
  257.9 3.1 collective-permute-done.31
  261.1 2.5 collective-permute-start.37
  263.7 3.5 collective-permute-start.41
  270.6 2.5 collective-permute-start.38
  274.1 2.1 fusion.39
  276.1 2.4 collective-permute-start.36
  279.1 9.2 %collective-permute-done.38 = bf16[256,768]{1,0:T(8,128)(2,1)S(1)} collective-permute-done((bf16[256,768]{1,0:T(8,128)(2,1)S(1)}, bf16[256,768]{1,0:T(8,128)(2,1)S(1)}, u32[]{:S(2)}, u32[]{:S(2)}) %collective-permute-start.38) | collective-permute-done | bytes 393248 | tf_op jit(solution)/shard_map/ppermute | solution.py:258
  290.5 7.0 %collective-permute-done.36 = bf16[256,512]{1,0:T(8,128)(2,1)S(1)} collective-permute-done((bf16[256,512]{1,0:T(8,128)(2,1)S(1)}, bf16[256,512]{1,0:T(8,128)(2,1)S(1)}, u32[]{:S(2)}, u32[]{:S(2)}) %collective-permute-start.36) | collective-permute-done | bytes 262176 | tf_op jit(solution)/shard_map/ppermute | solution.py:258
  297.7 3.0 collective-permute-start.53
  300.7 2.2 fusion.21
  303.5 8.1 %collective-permute-done.44 = bf16[64,1024]{1,0:T(8,128)(2,1)S(1)} collective-permute-done((bf16[64,1024]{1,0:T(8,128)(2,1)S(1)}, bf16[64,1024]{1,0:T(8,128)(2,1)S(1)}, u32[]{:S(2)}, u32[]{:S(2)}) %collective-permute-start.44) | collective-permute-done | bytes 131104 | tf_op jit(solution)/shard_map/ppermute | solution.py:258
  315.5 11.8 %collective-permute-done.48 = bf16[128,1024]{1,0:T(8,128)(2,1)S(1)} collective-permute-done((bf16[128,1024]{1,0:T(8,128)(2,1)S(1)}, bf16[128,1024]{1,0:T(8,128)(2,1)S(1)}, u32[]{:S(2)}, u32[]{:S(2)}) %collective-permute-start.48) | collective-permute-done | bytes 262176 | tf_op jit(solution)/shard_map/ppermute | solution.py:258
  327.5 2.1 collective-permute-start.56
  329.6 4.1 %collective-permute-done.46 = f32[2304]{0:T(1024)S(1)} collective-permute-done((f32[2304]{0:T(1024)S(1)}, f32[2304]{0:T(1024)S(1)}, u32[]{:S(2)}, u32[]{:S(2)}) %collective-permute-start.46) | collective-permute-done | bytes 9248 | tf_op jit(solution)/shard_map/ppermute | solution.py:258
  333.7 3.8 collective-permute-start.50
  338.1 1.9 fusion.38
  342.2 13.6 %collective-permute-done.52 = f32[2304]{0:T(1024)S(1)} collective-permute-done((f32[2304]{0:T(1024)S(1)}, f32[2304]{0:T(1024)S(1)}, u32[]{:S(2)}, u32[]{:S(2)}) %collective-permute-start.52) | collective-permute-done | bytes 9248 | tf_op jit(solution)/shard_map/ppermute | solution.py:258
  355.8 3.5 collective-permute-start.57
  360.5 6.4 %collective-permute-done.57 = bf16[256,512]{1,0:T(8,128)(2,1)S(1)} collective-permute-done((bf16[256,512]{1,0:T(8,128)(2,1)S(1)}, bf16[256,512]{1,0:T(8,128)(2,1)S(1)}, u32[]{:S(2)}, u32[]{:S(2)}) %collective-permute-start.57) | collective-permute-done | bytes 262176 | tf_op jit(solution)/shard_map/ppermute | solution.py:258
  367.2 1.9 collective-permute-start.59
  371.3 1.9 fusion.37
  373.2 3.1 collective-permute-done.60
  (345 shorter events, 95.8 us)
Async XLA Ops:
  0.6 103.6 %copy-start = (bf16[1024,768]{1,0:T(8,128)(2,1)S(1)}, bf16[1024,768]{1,0:T(8,128)(2,1)}, u32[]{:S(2)}) copy-start(bf16[1024,768]{1,0:T(8,128)(2,1)} %param.24) | copy-start | bytes 4718596
  3.3 15.0 %collective-permute-start.1 = (bf16[256,1024]{1,0:T(8,128)(2,1)S(1)}, bf16[256,1024]{1,0:T(8,128)(2,1)}, u32[]{:S(2)}, u32[]{:S(2)}) collective-permute-start(bf16[256,1024]{1,0:T(8,128)(2,1)S(1)} %fusion.3), channel_id=1, source_target_pairs={{0,2},{1,3},{2,0},{3,1},{4,6},{5,7},{6,4},{7,5},{8,10},{9,11},{10,... | collective-permute-start | bytes 1572872 | tf_op jit(solution)/shard_map/ppermute | solution.py:258
  6.3 18.2 %collective-permute-start = (bf16[256,1024]{1,0:T(8,128)(2,1)S(1)}, bf16[256,1024]{1,0:T(8,128)(2,1)}, u32[]{:S(2)}, u32[]{:S(2)}) collective-permute-start(bf16[256,1024]{1,0:T(8,128)(2,1)S(1)} %fusion.3), channel_id=1, source_target_pairs={{0,1},{1,0},{2,3},{3,2},{4,5},{5,4},{6,7},{7,6},{8,9},{9,8},{10,11... | collective-permute-start | bytes 1572872 | tf_op jit(solution)/shard_map/ppermute | solution.py:258
  18.3 6.2 %collective-permute-start.2 = (bf16[256,1024]{1,0:T(8,128)(2,1)}, bf16[256,1024]{1,0:T(8,128)(2,1)}, u32[]{:S(2)}, u32[]{:S(2)}) collective-permute-start(bf16[256,1024]{1,0:T(8,128)(2,1)} %collective-permute-done.1), channel_id=1, source_target_pairs={{0,1},{1,0},{2,3},{3,2},{4,5},{5,4},{6,7},{7,6},{8,9},{9,8},{10,11... | collective-permute-start | bytes 1572872 | tf_op jit(solution)/shard_map/ppermute | solution.py:258
  51.6 3.1 collective-permute-start.3
  52.1 13.9 %collective-permute-start.6 = (bf16[256,1024]{1,0:T(8,128)(2,1)S(1)}, bf16[256,1024]{1,0:T(8,128)(2,1)S(1)}, u32[]{:S(2)}, u32[]{:S(2)}) collective-permute-start(bf16[256,1024]{1,0:T(8,128)(2,1)S(1)} %fusion.22), channel_id=1, source_target_pairs={{0,2},{1,3},{2,0},{3,1},{4,6},{5,7},{6,4},{7,5},{8,10},{9,11},{10,... | collective-permute-start | bytes 1572872 | tf_op jit(solution)/shard_map/ppermute | solution.py:258
  53.9 13.8 %collective-permute-start.5 = (bf16[256,1024]{1,0:T(8,128)(2,1)S(1)}, bf16[256,1024]{1,0:T(8,128)(2,1)S(1)}, u32[]{:S(2)}, u32[]{:S(2)}) collective-permute-start(bf16[256,1024]{1,0:T(8,128)(2,1)S(1)} %fusion.22), channel_id=1, source_target_pairs={{0,1},{1,0},{2,3},{3,2},{4,5},{5,4},{6,7},{7,6},{8,9},{9,8},{10,11... | collective-permute-start | bytes 1572872 | tf_op jit(solution)/shard_map/ppermute | solution.py:258
  65.9 2.0 collective-permute-start.7
  65.9 14.5 %collective-permute-start.4 = (bf16[256,1024]{1,0:T(8,128)(2,1)}, bf16[256,1024]{1,0:T(8,128)(2,1)S(1)}, u32[]{:S(2)}, u32[]{:S(2)}) collective-permute-start(bf16[256,1024]{1,0:T(8,128)(2,1)} %fusion.23), channel_id=1, source_target_pairs={{0,2},{1,3},{2,0},{3,1},{4,6},{5,7},{6,4},{7,5},{8,10},{9,11},{10,... | collective-permute-start | bytes 1572872 | tf_op jit(solution)/shard_map/ppermute | solution.py:258
  81.8 13.9 %collective-permute-start.9 = (bf16[256,1024]{1,0:T(8,128)(2,1)}, bf16[256,1024]{1,0:T(8,128)(2,1)}, u32[]{:S(2)}, u32[]{:S(2)}) collective-permute-start(bf16[256,1024]{1,0:T(8,128)(2,1)} %multiply_convert_fusion.1), channel_id=1, source_target_pairs={{0,2},{1,3},{2,0},{3,1},{4,6},{5,7},{6,4},{7,5},{8,10},{9,11},{10,... | collective-permute-start | bytes 1572872 | tf_op jit(solution)/shard_map/ppermute | solution.py:258
  83.5 12.1 %collective-permute-start.8 = (bf16[256,1024]{1,0:T(8,128)(2,1)}, bf16[256,1024]{1,0:T(8,128)(2,1)}, u32[]{:S(2)}, u32[]{:S(2)}) collective-permute-start(bf16[256,1024]{1,0:T(8,128)(2,1)} %multiply_convert_fusion.1), channel_id=1, source_target_pairs={{0,1},{1,0},{2,3},{3,2},{4,5},{5,4},{6,7},{7,6},{8,9},{9,8},{10,11... | collective-permute-start | bytes 1572872 | tf_op jit(solution)/shard_map/ppermute | solution.py:258
  95.6 2.3 collective-permute-start.10
  118.7 2.9 collective-permute-start.11
  118.8 20.6 %collective-permute-start.13 = (bf16[384,1024]{1,0:T(8,128)(2,1)}, bf16[384,1024]{1,0:T(8,128)(2,1)S(1)}, u32[]{:S(2)}, u32[]{:S(2)}) collective-permute-start(bf16[384,1024]{1,0:T(8,128)(2,1)} %constant_dynamic-slice_fusion.20), channel_id=1, source_target_pairs={{0,4},{4,0},{8,12},{12,8},{16,20},{20,16},{24,28},{28,24},{1,5},{5... | collective-permute-start | bytes 2359304 | tf_op jit(solution)/shard_map/ppermute | solution.py:258
  123.2 18.6 %collective-permute-start.12 = (bf16[256,1024]{1,0:T(8,128)(2,1)S(1)}, bf16[256,1024]{1,0:T(8,128)(2,1)S(1)}, u32[]{:S(2)}, u32[]{:S(2)}) collective-permute-start(bf16[256,1024]{1,0:T(8,128)(2,1)S(1)} %fusion.24), channel_id=1, source_target_pairs={{0,2},{1,3},{2,0},{3,1},{4,6},{5,7},{6,4},{7,5},{8,10},{9,11},{10,... | collective-permute-start | bytes 1572872 | tf_op jit(solution)/shard_map/ppermute | solution.py:258
  127.1 28.6 %collective-permute-start.19 = (bf16[512,768]{1,0:T(8,128)(2,1)S(1)}, bf16[512,768]{1,0:T(8,128)(2,1)S(1)}, u32[]{:S(2)}, u32[]{:S(2)}) collective-permute-start(bf16[512,768]{1,0:T(8,128)(2,1)S(1)} %constant_dynamic-slice_fusion.18), channel_id=1, source_target_pairs={{0,4},{4,0},{8,12},{12,8},{16,20},{20,16},{24,28},{28,24},{1,5},{5... | collective-permute-start | bytes 2359304 | tf_op jit(solution)/shard_map/ppermute | solution.py:258
  139.7 10.2 %collective-permute-start.15 = (bf16[192,1024]{1,0:T(8,128)(2,1)S(1)}, bf16[192,1024]{1,0:T(8,128)(2,1)S(1)}, u32[]{:S(2)}, u32[]{:S(2)}) collective-permute-start(bf16[192,1024]{1,0:T(8,128)(2,1)S(1)} %constant_dynamic-slice_fusion.15), channel_id=1, source_target_pairs={{0,8},{4,12},{8,0},{12,4},{16,24},{20,28},{24,16},{28,20},{1,9},{5... | collective-permute-start | bytes 1179656 | tf_op jit(solution)/shard_map/ppermute | solution.py:258
  143.2 13.6 %collective-permute-start.18 = (bf16[256,1024]{1,0:T(8,128)(2,1)S(1)}, bf16[256,1024]{1,0:T(8,128)(2,1)S(1)}, u32[]{:S(2)}, u32[]{:S(2)}) collective-permute-start(bf16[256,1024]{1,0:T(8,128)(2,1)S(1)} %get-tuple-element.256), channel_id=1, source_target_pairs={{0,2},{1,3},{2,0},{3,1},{4,6},{5,7},{6,4},{7,5},{8,10},{9,11},{10,... | collective-permute-start | bytes 1572872 | tf_op jit(solution)/shard_map/ppermute | solution.py:258
  144.7 19.3 %collective-permute-start.17 = (bf16[256,1024]{1,0:T(8,128)(2,1)S(1)}, bf16[256,1024]{1,0:T(8,128)(2,1)S(1)}, u32[]{:S(2)}, u32[]{:S(2)}) collective-permute-start(bf16[256,1024]{1,0:T(8,128)(2,1)S(1)} %get-tuple-element.256), channel_id=1, source_target_pairs={{0,1},{1,0},{2,3},{3,2},{4,5},{5,4},{6,7},{7,6},{8,9},{9,8},{10,11... | collective-permute-start | bytes 1572872 | tf_op jit(solution)/shard_map/ppermute | solution.py:258
  156.8 7.7 %collective-permute-start.20 = (bf16[256,1024]{1,0:T(8,128)(2,1)S(1)}, bf16[256,1024]{1,0:T(8,128)(2,1)S(1)}, u32[]{:S(2)}, u32[]{:S(2)}) collective-permute-start(bf16[256,1024]{1,0:T(8,128)(2,1)S(1)} %collective-permute-done.18), channel_id=1, source_target_pairs={{0,1},{1,0},{2,3},{3,2},{4,5},{5,4},{6,7},{7,6},{8,9},{9,8},{10,11... | collective-permute-start | bytes 1572872 | tf_op jit(solution)/shard_map/ppermute | solution.py:258
  159.1 12.9 %collective-permute-start.14 = (bf16[2,1,256,1024]{3,2,1,0:T(8,128)(2,1)S(1)}, bf16[2,1,256,1024]{3,2,1,0:T(8,128)(2,1)S(1)}, u32[]{:S(2)}, u32[]{:S(2)}) collective-permute-start(bf16[2,1,256,1024]{3,2,1,0:T(8,128)(2,1)S(1)} %constant_dynamic-slice_fusion.17), channel_id=1, source_target_pairs={{0,1},{1,0},{2,3},{3,2},{4,5},{5,4},{6,7},{7,6},{8,9},{9,8},{10,11... | collective-permute-start | bytes 3145736 | tf_op jit(solution)/shard_map/ppermute | solution.py:258
  159.6 12.2 %collective-permute-start.16 = (bf16[96,1024]{1,0:T(8,128)(2,1)S(1)}, bf16[96,1024]{1,0:T(8,128)(2,1)S(1)}, u32[]{:S(2)}, u32[]{:S(2)}) collective-permute-start(bf16[96,1024]{1,0:T(8,128)(2,1)S(1)} %constant_dynamic-slice_fusion.14), channel_id=1, source_target_pairs={{0,16},{4,20},{8,24},{12,28},{16,0},{20,4},{24,8},{28,12},{1,17},{... | collective-permute-start | bytes 589832 | tf_op jit(solution)/shard_map/ppermute | solution.py:258
  162.4 27.7 %collective-permute-start.22 = (bf16[512,768]{1,0:T(8,128)(2,1)S(1)}, bf16[512,768]{1,0:T(8,128)(2,1)S(1)}, u32[]{:S(2)}, u32[]{:S(2)}) collective-permute-start(bf16[512,768]{1,0:T(8,128)(2,1)S(1)} %constant_dynamic-slice_fusion.16), channel_id=1, source_target_pairs={{0,8},{4,12},{8,0},{12,4},{16,24},{20,28},{24,16},{28,20},{1,9},{5... | collective-permute-start | bytes 2359304 | tf_op jit(solution)/shard_map/ppermute | solution.py:258
  164.0 49.5 %collective-permute-start.24 = (bf16[256,768]{1,0:T(8,128)(2,1)}, bf16[256,768]{1,0:T(8,128)(2,1)}, u32[]{:S(2)}, u32[]{:S(2)}) collective-permute-start(bf16[256,768]{1,0:T(8,128)(2,1)} %constant_dynamic-slice_fusion.13), channel_id=1, source_target_pairs={{0,8},{4,12},{8,0},{12,4},{16,24},{20,28},{24,16},{28,20},{1,9},{5... | collective-permute-start | bytes 1179656 | tf_op jit(solution)/shard_map/ppermute | solution.py:258
  171.9 43.9 %collective-permute-start.28 = (bf16[96,1024]{1,0:T(8,128)(2,1)S(1)}, bf16[96,1024]{1,0:T(8,128)(2,1)S(1)}, u32[]{:S(2)}, u32[]{:S(2)}) collective-permute-start(bf16[96,1024]{1,0:T(8,128)(2,1)S(1)} %add_convert_fusion.17), channel_id=1, source_target_pairs={{0,16},{4,20},{8,24},{12,28},{16,0},{20,4},{24,8},{28,12},{1,17},{... | collective-permute-start | bytes 589832 | tf_op jit(solution)/shard_map/ppermute | solution.py:258
  172.5 18.6 %copy-start.6 = (f32[2,1,256,1024]{3,2,1,0:T(8,128)}, f32[2,1,256,1024]{3,2,1,0:T(8,128)S(1)}, u32[]{:S(2)}) copy-start(f32[2,1,256,1024]{3,2,1,0:T(8,128)S(1)} %convert_add_fusion.1) | copy-start | bytes 6291460
  172.5 19.4 %copy-start.9 = (bf16[1024,512]{1,0:T(8,128)(2,1)S(1)}, bf16[1024,512]{1,0:T(8,128)(2,1)}, u32[]{:S(2)}) copy-start(bf16[1024,512]{1,0:T(8,128)(2,1)} %attend.1) | copy-start | bytes 3145732
  173.4 124.3 %collective-permute-start.21 = (bf16[256,1024]{1,0:T(8,128)(2,1)}, bf16[256,1024]{1,0:T(8,128)(2,1)}, u32[]{:S(2)}, u32[]{:S(2)}) collective-permute-start(bf16[256,1024]{1,0:T(8,128)(2,1)} %fusion.25), channel_id=1, source_target_pairs={{0,2},{1,3},{2,0},{3,1},{4,6},{5,7},{6,4},{7,5},{8,10},{9,11},{10,... | collective-permute-start | bytes 1572872 | tf_op jit(solution)/shard_map/ppermute | solution.py:258
  191.3 31.5 %collective-permute-start.26 = (bf16[256,768]{1,0:T(8,128)(2,1)}, bf16[256,768]{1,0:T(8,128)(2,1)}, u32[]{:S(2)}, u32[]{:S(2)}) collective-permute-start(bf16[256,768]{1,0:T(8,128)(2,1)} %constant_dynamic-slice_fusion.12), channel_id=1, source_target_pairs={{0,16},{4,20},{8,24},{12,28},{16,0},{20,4},{24,8},{28,12},{1,17},{... | collective-permute-start | bytes 1179656 | tf_op jit(solution)/shard_map/ppermute | solution.py:258
  195.0 25.6 %collective-permute-start.27 = (bf16[256,1024]{1,0:T(8,128)(2,1)}, bf16[256,1024]{1,0:T(8,128)(2,1)}, u32[]{:S(2)}, u32[]{:S(2)}) collective-permute-start(bf16[256,1024]{1,0:T(8,128)(2,1)} %constant_dynamic-slice_fusion.11), channel_id=1, source_target_pairs={{0,4},{4,0},{8,12},{12,8},{16,20},{20,16},{24,28},{28,24},{1,5},{5... | collective-permute-start | bytes 1572872 | tf_op jit(solution)/shard_map/ppermute | solution.py:258
  213.4 31.1 %collective-permute-start.23 = (bf16[512,512]{1,0:T(8,128)(2,1)}, bf16[512,512]{1,0:T(8,128)(2,1)}, u32[]{:S(2)}, u32[]{:S(2)}) collective-permute-start(bf16[512,512]{1,0:T(8,128)(2,1)} %constant_dynamic-slice_fusion.10), channel_id=1, source_target_pairs={{0,4},{4,0},{8,12},{12,8},{16,20},{20,16},{24,28},{28,24},{1,5},{5... | collective-permute-start | bytes 1572872 | tf_op jit(solution)/shard_map/ppermute | solution.py:258
  216.5 26.8 %collective-permute-start.25 = (bf16[128,768]{1,0:T(8,128)(2,1)}, bf16[128,768]{1,0:T(8,128)(2,1)}, u32[]{:S(2)}, u32[]{:S(2)}) collective-permute-start(bf16[128,768]{1,0:T(8,128)(2,1)} %constant_dynamic-slice_fusion.9), channel_id=1, source_target_pairs={{0,16},{4,20},{8,24},{12,28},{16,0},{20,4},{24,8},{28,12},{1,17},{... | collective-permute-start | bytes 589832 | tf_op jit(solution)/shard_map/ppermute | solution.py:258
  220.6 26.8 %collective-permute-start.34 = (bf16[192,1024]{1,0:T(8,128)(2,1)}, bf16[192,1024]{1,0:T(8,128)(2,1)}, u32[]{:S(2)}, u32[]{:S(2)}) collective-permute-start(bf16[192,1024]{1,0:T(8,128)(2,1)} %pad_maximum_fusion.28), channel_id=1, source_target_pairs={{0,8},{4,12},{8,0},{12,4},{16,24},{20,28},{24,16},{28,20},{1,9},{5... | collective-permute-start | bytes 1179656 | tf_op jit(solution)/shard_map/ppermute | solution.py:258
  222.8 32.2 %collective-permute-start.32 = (bf16[128,1024]{1,0:T(8,128)(2,1)}, bf16[128,1024]{1,0:T(8,128)(2,1)}, u32[]{:S(2)}, u32[]{:S(2)}) collective-permute-start(bf16[128,1024]{1,0:T(8,128)(2,1)} %constant_dynamic-slice_fusion.8), channel_id=1, source_target_pairs={{0,8},{4,12},{8,0},{12,4},{16,24},{20,28},{24,16},{28,20},{1,9},{5... | collective-permute-start | bytes 786440 | tf_op jit(solution)/shard_map/ppermute | solution.py:258
  243.3 20.4 %collective-permute-start.30 = (bf16[512,512]{1,0:T(8,128)(2,1)S(1)}, bf16[512,512]{1,0:T(8,128)(2,1)S(1)}, u32[]{:S(2)}, u32[]{:S(2)}) collective-permute-start(bf16[512,512]{1,0:T(8,128)(2,1)S(1)} %constant_dynamic-slice_fusion.6), channel_id=1, source_target_pairs={{0,8},{4,12},{8,0},{12,4},{16,24},{20,28},{24,16},{28,20},{1,9},{5... | collective-permute-start | bytes 1572872 | tf_op jit(solution)/shard_map/ppermute | solution.py:258
  244.5 6.4 %collective-permute-start.33 = (bf16[128,768]{1,0:T(8,128)(2,1)S(1)}, bf16[128,768]{1,0:T(8,128)(2,1)S(1)}, u32[]{:S(2)}, u32[]{:S(2)}) collective-permute-start(bf16[128,768]{1,0:T(8,128)(2,1)S(1)} %copy-done.45), channel_id=1, source_target_pairs={{0,4},{4,0},{8,12},{12,8},{16,20},{20,16},{24,28},{28,24},{1,5},{5... | collective-permute-start | bytes 589832 | tf_op jit(solution)/shard_map/ppermute | solution.py:258
  247.4 22.9 %collective-permute-start.29 = (bf16[256,512]{1,0:T(8,128)(2,1)S(1)}, bf16[256,512]{1,0:T(8,128)(2,1)S(1)}, u32[]{:S(2)}, u32[]{:S(2)}) collective-permute-start(bf16[256,512]{1,0:T(8,128)(2,1)S(1)} %constant_dynamic-slice_fusion.5), channel_id=1, source_target_pairs={{0,8},{4,12},{8,0},{12,4},{16,24},{20,28},{24,16},{28,20},{1,9},{5... | collective-permute-start | bytes 786440 | tf_op jit(solution)/shard_map/ppermute | solution.py:258
  250.9 10.2 %collective-permute-start.31 = (bf16[128,768]{1,0:T(8,128)(2,1)S(1)}, bf16[128,768]{1,0:T(8,128)(2,1)S(1)}, u32[]{:S(2)}, u32[]{:S(2)}) collective-permute-start(bf16[128,768]{1,0:T(8,128)(2,1)S(1)} %add_convert_fusion.16), channel_id=1, source_target_pairs={{0,16},{4,20},{8,24},{12,28},{16,0},{20,4},{24,8},{28,12},{1,17},{... | collective-permute-start | bytes 589832 | tf_op jit(solution)/shard_map/ppermute | solution.py:258
  255.0 18.1 %collective-permute-start.40 = (bf16[384,1024]{1,0:T(8,128)(2,1)S(1)}, bf16[384,1024]{1,0:T(8,128)(2,1)S(1)}, u32[]{:S(2)}, u32[]{:S(2)}) collective-permute-start(bf16[384,1024]{1,0:T(8,128)(2,1)S(1)} %pad_maximum_fusion.20), channel_id=1, source_target_pairs={{0,4},{4,0},{8,12},{12,8},{16,20},{20,16},{24,28},{28,24},{1,5},{5... | collective-permute-start | bytes 2359304 | tf_op jit(solution)/shard_map/ppermute | solution.py:258
  261.1 27.8 %collective-permute-start.37 = (bf16[128,768]{1,0:T(8,128)(2,1)S(1)}, bf16[128,768]{1,0:T(8,128)(2,1)S(1)}, u32[]{:S(2)}, u32[]{:S(2)}) collective-permute-start(bf16[128,768]{1,0:T(8,128)(2,1)S(1)} %add_convert_fusion.15), channel_id=1, source_target_pairs={{0,4},{4,0},{8,12},{12,8},{16,20},{20,16},{24,28},{28,24},{1,5},{5... | collective-permute-start | bytes 589832 | tf_op jit(solution)/shard_map/ppermute | solution.py:258
  263.7 6.9 %collective-permute-start.41 = (bf16[64,1024]{1,0:T(8,128)(2,1)S(1)}, bf16[64,1024]{1,0:T(8,128)(2,1)S(1)}, u32[]{:S(2)}, u32[]{:S(2)}) collective-permute-start(bf16[64,1024]{1,0:T(8,128)(2,1)S(1)} %constant_dynamic-slice_fusion.4), channel_id=1, source_target_pairs={{0,16},{4,20},{8,24},{12,28},{16,0},{20,4},{24,8},{28,12},{1,17},{... | collective-permute-start | bytes 393224 | tf_op jit(solution)/shard_map/ppermute | solution.py:258
  270.4 5.8 %collective-permute-start.39 = (bf16[2,1,256,1024]{3,2,1,0:T(8,128)(2,1)S(1)}, bf16[2,1,256,1024]{3,2,1,0:T(8,128)(2,1)S(1)}, u32[]{:S(2)}, u32[]{:S(2)}) collective-permute-start(bf16[2,1,256,1024]{3,2,1,0:T(8,128)(2,1)S(1)} %constant_dynamic-slice_fusion.2), channel_id=1, source_target_pairs={{0,1},{1,0},{2,3},{3,2},{4,5},{5,4},{6,7},{7,6},{8,9},{9,8},{10,11... | collective-permute-start | bytes 3145736 | tf_op jit(solution)/shard_map/ppermute | solution.py:258
  270.6 17.7 %collective-permute-start.38 = (bf16[256,768]{1,0:T(8,128)(2,1)S(1)}, bf16[256,768]{1,0:T(8,128)(2,1)S(1)}, u32[]{:S(2)}, u32[]{:S(2)}) collective-permute-start(bf16[256,768]{1,0:T(8,128)(2,1)S(1)} %pad_maximum_fusion.29), channel_id=1, source_target_pairs={{0,8},{4,12},{8,0},{12,4},{16,24},{20,28},{24,16},{28,20},{1,9},{5... | collective-permute-start | bytes 1179656 | tf_op jit(solution)/shard_map/ppermute | solution.py:258
  273.1 24.5 %collective-permute-start.35 = (bf16[128,512]{1,0:T(8,128)(2,1)S(1)}, bf16[128,512]{1,0:T(8,128)(2,1)S(1)}, u32[]{:S(2)}, u32[]{:S(2)}) collective-permute-start(bf16[128,512]{1,0:T(8,128)(2,1)S(1)} %constant_dynamic-slice_fusion.1), channel_id=1, source_target_pairs={{0,16},{4,20},{8,24},{12,28},{16,0},{20,4},{24,8},{28,12},{1,17},{... | collective-permute-start | bytes 393224 | tf_op jit(solution)/shard_map/ppermute | solution.py:258
  276.1 21.3 %collective-permute-start.36 = (bf16[256,512]{1,0:T(8,128)(2,1)S(1)}, bf16[256,512]{1,0:T(8,128)(2,1)S(1)}, u32[]{:S(2)}, u32[]{:S(2)}) collective-permute-start(bf16[256,512]{1,0:T(8,128)(2,1)S(1)} %constant_dynamic-slice_fusion.3), channel_id=1, source_target_pairs={{0,16},{4,20},{8,24},{12,28},{16,0},{20,4},{24,8},{28,12},{1,17},{... | collective-permute-start | bytes 786440 | tf_op jit(solution)/shard_map/ppermute | solution.py:258
  288.2 23.3 %collective-permute-start.44 = (bf16[64,1024]{1,0:T(8,128)(2,1)S(1)}, bf16[64,1024]{1,0:T(8,128)(2,1)S(1)}, u32[]{:S(2)}, u32[]{:S(2)}) collective-permute-start(bf16[64,1024]{1,0:T(8,128)(2,1)S(1)} %add_convert_fusion.20), channel_id=1, source_target_pairs={{0,16},{4,20},{8,24},{12,28},{16,0},{20,4},{24,8},{28,12},{1,17},{... | collective-permute-start | bytes 393224 | tf_op jit(solution)/shard_map/ppermute | solution.py:258
  288.9 14.0 %collective-permute-start.42 = (bf16[256,1024]{1,0:T(8,128)(2,1)S(1)}, bf16[256,1024]{1,0:T(8,128)(2,1)S(1)}, u32[]{:S(2)}, u32[]{:S(2)}) collective-permute-start(bf16[256,1024]{1,0:T(8,128)(2,1)S(1)} %fusion.26), channel_id=1, source_target_pairs={{0,2},{1,3},{2,0},{3,1},{4,6},{5,7},{6,4},{7,5},{8,10},{9,11},{10,... | collective-permute-start | bytes 1572872 | tf_op jit(solution)/shard_map/ppermute | solution.py:258
  297.5 36.2 %collective-permute-start.51 = (bf16[256,768]{1,0:T(8,128)(2,1)S(1)}, bf16[256,768]{1,0:T(8,128)(2,1)S(1)}, u32[]{:S(2)}, u32[]{:S(2)}) collective-permute-start(bf16[256,768]{1,0:T(8,128)(2,1)S(1)} %pad_maximum_fusion.30), channel_id=1, source_target_pairs={{0,16},{4,20},{8,24},{12,28},{16,0},{20,4},{24,8},{28,12},{1,17},{... | collective-permute-start | bytes 1179656 | tf_op jit(solution)/shard_map/ppermute | solution.py:258
  297.6 29.9 %collective-permute-start.47 = (bf16[128,512]{1,0:T(8,128)(2,1)S(1)}, bf16[128,512]{1,0:T(8,128)(2,1)S(1)}, u32[]{:S(2)}, u32[]{:S(2)}) collective-permute-start(bf16[128,512]{1,0:T(8,128)(2,1)S(1)} %constant_dynamic-slice_fusion), channel_id=1, source_target_pairs={{0,4},{4,0},{8,12},{12,8},{16,20},{20,16},{24,28},{28,24},{1,5},{5... | collective-permute-start | bytes 393224 | tf_op jit(solution)/shard_map/ppermute | solution.py:258
  297.7 43.0 %collective-permute-start.53 = (bf16[128,512]{1,0:T(8,128)(2,1)S(1)}, bf16[128,512]{1,0:T(8,128)(2,1)S(1)}, u32[]{:S(2)}, u32[]{:S(2)}) collective-permute-start(bf16[128,512]{1,0:T(8,128)(2,1)S(1)} %add_convert_fusion.19), channel_id=1, source_target_pairs={{0,16},{4,20},{8,24},{12,28},{16,0},{20,4},{24,8},{28,12},{1,17},{... | collective-permute-start | bytes 393224 | tf_op jit(solution)/shard_map/ppermute | solution.py:258
  303.4 8.3 %collective-permute-start.43 = (f32[2304]{0:T(1024)S(1)}, f32[2304]{0:T(1024)S(1)}, u32[]{:S(2)}, u32[]{:S(2)}) collective-permute-start(f32[2304]{0:T(1024)S(1)} %pad_maximum_fusion.34), channel_id=1, source_target_pairs={{0,1},{1,0},{2,3},{3,2},{4,5},{5,4},{6,7},{7,6},{8,9},{9,8},{10,11... | collective-permute-start | bytes 27656 | tf_op jit(solution)/shard_map/ppermute | solution.py:258
  311.6 15.7 %collective-permute-start.48 = (bf16[128,1024]{1,0:T(8,128)(2,1)S(1)}, bf16[128,1024]{1,0:T(8,128)(2,1)S(1)}, u32[]{:S(2)}, u32[]{:S(2)}) collective-permute-start(bf16[128,1024]{1,0:T(8,128)(2,1)S(1)} %pad_maximum_fusion.31), channel_id=1, source_target_pairs={{0,8},{4,12},{8,0},{12,4},{16,24},{20,28},{24,16},{28,20},{1,9},{5... | collective-permute-start | bytes 786440 | tf_op jit(solution)/shard_map/ppermute | solution.py:258
  311.7 3.8 collective-permute-start.45
  315.5 22.3 %collective-permute-start.49 = (bf16[512,768]{1,0:T(8,128)(2,1)S(1)}, bf16[512,768]{1,0:T(8,128)(2,1)S(1)}, u32[]{:S(2)}, u32[]{:S(2)}) collective-permute-start(bf16[512,768]{1,0:T(8,128)(2,1)S(1)} %pad_maximum_fusion.21), channel_id=1, source_target_pairs={{0,4},{4,0},{8,12},{12,8},{16,20},{20,16},{24,28},{28,24},{1,5},{5... | collective-permute-start | bytes 2359304 | tf_op jit(solution)/shard_map/ppermute | solution.py:258
  327.3 6.4 %collective-permute-start.46 = (f32[2304]{0:T(1024)S(1)}, f32[2304]{0:T(1024)S(1)}, u32[]{:S(2)}, u32[]{:S(2)}) collective-permute-start(f32[2304]{0:T(1024)S(1)} %add.337), channel_id=1, source_target_pairs={{0,4},{4,0},{8,12},{12,8},{16,20},{20,16},{24,28},{28,24},{1,5},{5... | collective-permute-start | bytes 27656 | tf_op jit(solution)/shard_map/ppermute | solution.py:258
  327.5 41.6 %collective-permute-start.56 = (bf16[256,1024]{1,0:T(8,128)(2,1)S(1)}, bf16[256,1024]{1,0:T(8,128)(2,1)S(1)}, u32[]{:S(2)}, u32[]{:S(2)}) collective-permute-start(bf16[256,1024]{1,0:T(8,128)(2,1)S(1)} %pad_maximum_fusion.25), channel_id=1, source_target_pairs={{0,4},{4,0},{8,12},{12,8},{16,20},{20,16},{24,28},{28,24},{1,5},{5... | collective-permute-start | bytes 1572872 | tf_op jit(solution)/shard_map/ppermute | solution.py:258
  333.7 22.1 %collective-permute-start.55 = (bf16[128,512]{1,0:T(8,128)(2,1)S(1)}, bf16[128,512]{1,0:T(8,128)(2,1)S(1)}, u32[]{:S(2)}, u32[]{:S(2)}) collective-permute-start(bf16[128,512]{1,0:T(8,128)(2,1)S(1)} %add_convert_fusion.18), channel_id=1, source_target_pairs={{0,4},{4,0},{8,12},{12,8},{16,20},{20,16},{24,28},{28,24},{1,5},{5... | collective-permute-start | bytes 393224 | tf_op jit(solution)/shard_map/ppermute | solution.py:258
  333.7 6.3 %collective-permute-start.50 = (f32[2304]{0:T(1024)S(1)}, f32[2304]{0:T(1024)S(1)}, u32[]{:S(2)}, u32[]{:S(2)}) collective-permute-start(f32[2304]{0:T(1024)S(1)} %add.339), channel_id=1, source_target_pairs={{0,8},{4,12},{8,0},{12,4},{16,24},{20,28},{24,16},{28,20},{1,9},{5... | collective-permute-start | bytes 27656 | tf_op jit(solution)/shard_map/ppermute | solution.py:258
  338.1 32.9 %collective-permute-start.58 = (bf16[512,768]{1,0:T(8,128)(2,1)S(1)}, bf16[512,768]{1,0:T(8,128)(2,1)S(1)}, u32[]{:S(2)}, u32[]{:S(2)}) collective-permute-start(bf16[512,768]{1,0:T(8,128)(2,1)S(1)} %pad_maximum_fusion.22), channel_id=1, source_target_pairs={{0,8},{4,12},{8,0},{12,4},{16,24},{20,28},{24,16},{28,20},{1,9},{5... | collective-permute-start | bytes 2359304 | tf_op jit(solution)/shard_map/ppermute | solution.py:258
  340.0 15.7 %collective-permute-start.52 = (f32[2304]{0:T(1024)S(1)}, f32[2304]{0:T(1024)S(1)}, u32[]{:S(2)}, u32[]{:S(2)}) collective-permute-start(f32[2304]{0:T(1024)S(1)} %add.340), channel_id=1, source_target_pairs={{0,16},{4,20},{8,24},{12,28},{16,0},{20,4},{24,8},{28,12},{1,17},{... | collective-permute-start | bytes 27656 | tf_op jit(solution)/shard_map/ppermute | solution.py:258
  340.8 26.3 %collective-permute-start.54 = (bf16[256,512]{1,0:T(8,128)(2,1)S(1)}, bf16[256,512]{1,0:T(8,128)(2,1)S(1)}, u32[]{:S(2)}, u32[]{:S(2)}) collective-permute-start(bf16[256,512]{1,0:T(8,128)(2,1)S(1)} %pad_maximum_fusion.32), channel_id=1, source_target_pairs={{0,8},{4,12},{8,0},{12,4},{16,24},{20,28},{24,16},{28,20},{1,9},{5... | collective-permute-start | bytes 786440 | tf_op jit(solution)/shard_map/ppermute | solution.py:258
  355.8 11.0 %collective-permute-start.57 = (bf16[256,512]{1,0:T(8,128)(2,1)S(1)}, bf16[256,512]{1,0:T(8,128)(2,1)S(1)}, u32[]{:S(2)}, u32[]{:S(2)}) collective-permute-start(bf16[256,512]{1,0:T(8,128)(2,1)S(1)} %pad_maximum_fusion.33), channel_id=1, source_target_pairs={{0,16},{4,20},{8,24},{12,28},{16,0},{20,4},{24,8},{28,12},{1,17},{... | collective-permute-start | bytes 786440 | tf_op jit(solution)/shard_map/ppermute | solution.py:258
  367.0 9.2 %collective-permute-start.60 = (bf16[512,512]{1,0:T(8,128)(2,1)S(1)}, bf16[512,512]{1,0:T(8,128)(2,1)S(1)}, u32[]{:S(2)}, u32[]{:S(2)}) collective-permute-start(bf16[512,512]{1,0:T(8,128)(2,1)S(1)} %pad_maximum_fusion.26), channel_id=1, source_target_pairs={{0,8},{4,12},{8,0},{12,4},{16,24},{20,28},{24,16},{28,20},{1,9},{5... | collective-permute-start | bytes 1572872 | tf_op jit(solution)/shard_map/ppermute | solution.py:258
  367.2 10.8 %collective-permute-start.59 = (bf16[512,512]{1,0:T(8,128)(2,1)S(1)}, bf16[512,512]{1,0:T(8,128)(2,1)S(1)}, u32[]{:S(2)}, u32[]{:S(2)}) collective-permute-start(bf16[512,512]{1,0:T(8,128)(2,1)S(1)} %pad_maximum_fusion.27), channel_id=1, source_target_pairs={{0,4},{4,0},{8,12},{12,8},{16,20},{20,16},{24,28},{28,24},{1,5},{5... | collective-permute-start | bytes 1572872 | tf_op jit(solution)/shard_map/ppermute | solution.py:258
  (63 other events, 310.5 us)

commit v3 on v2

--- a/solution.py
+++ b/solution.py
@@ -9,7 +9,6 @@
 BLOCK_ROWS = 256
 epsilon = 1e-06
 rotary_base = 1000000.0
-masked_score = -1e30
 
 
 def rotary_tables(every_row):
@@ -50,9 +49,15 @@
 
 
 def heads_kernel(
-    rows_ref, wq_ref, wk_ref, wv_ref, q_gain_ref, k_gain_ref, cos_ref, sin_ref,
-    raw_q_ref, raw_k_ref, query_ref, key_ref, value_ref,
+    place_ref, mine_ref, near_ref, across_ref, far_ref, wq_ref, wk_ref, wv_ref, q_gain_ref, k_gain_ref, cos_ref, sin_ref,
+    rows_ref, raw_q_ref, raw_k_ref, query_ref, key_ref, value_ref,
 ):
+    for k, piece_ref in enumerate((mine_ref, near_ref, across_ref, far_ref)):
+
+        @pl.when(pl.program_id(0) == k)
+        def _():
+            rows_ref[...] = piece_ref[...]
+
     rows = rows_ref[...]
     cosine = cos_ref[...]
     sine = sin_ref[...]
@@ -68,65 +73,79 @@
             out_ref[:, cut] = shaped(raw[:, cut], gain_ref[...], cosine, sine).astype(jnp.bfloat16)
 
 
-def project_heads(rows, w_query, key_weight, value_weight, q_gain, k_gain, cosine, sine):
-    every_row, width = rows.shape
-    block = BLOCK_ROWS
+def project_heads(places, pieces, w_query, key_weight, value_weight, q_gain, k_gain, cosine, sine):
+    block, width = pieces[0].shape
+    every_row = block * len(pieces)
     q_cols, k_cols = w_query.shape[1], key_weight.shape[1]
 
     def by_row(cols):
-        return pl.BlockSpec((block, cols), lambda i: (i, 0))
+        return pl.BlockSpec((block, cols), lambda i, places: (places[i], 0))
 
     def whole(shape):
-        return pl.BlockSpec(shape, lambda i: (0, 0))
-
+        return pl.BlockSpec(shape, lambda i, places: (0, 0))
+
+    outs = [
+        (width, jnp.bfloat16), (q_cols, jnp.float32), (k_cols, jnp.float32),
+        (q_cols, jnp.bfloat16), (k_cols, jnp.bfloat16), (k_cols, jnp.bfloat16),
+    ]
     return pl.pallas_call(
         heads_kernel,
-        grid=(every_row // block,),
-        in_specs=[
-            by_row(width),
-            whole(w_query.shape),
-            whole(key_weight.shape),
-            whole(value_weight.shape),
-            whole((1, HEAD_SIZE)),
-            whole((1, HEAD_SIZE)),
-            by_row(HEAD_SIZE),
-            by_row(HEAD_SIZE),
-        ],
-        out_specs=[by_row(q_cols), by_row(k_cols), by_row(q_cols), by_row(k_cols), by_row(k_cols)],
-        out_shape=[
-            jax.ShapeDtypeStruct((every_row, q_cols), jnp.float32),
-            jax.ShapeDtypeStruct((every_row, k_cols), jnp.float32),
-            jax.ShapeDtypeStruct((every_row, q_cols), jnp.bfloat16),
-            jax.ShapeDtypeStruct((every_row, k_cols), jnp.bfloat16),
-            jax.ShapeDtypeStruct((every_row, k_cols), jnp.bfloat16),
-        ],
+        grid_spec=pltpu.PrefetchScalarGridSpec(
+            num_scalar_prefetch=1,
+            grid=(len(pieces),),
+            in_specs=[whole(one.shape) for one in pieces]
+            + [
+                whole(w_query.shape),
+                whole(key_weight.shape),
+                whole(value_weight.shape),
+                whole((1, HEAD_SIZE)),
+                whole((1, HEAD_SIZE)),
+                by_row(HEAD_SIZE),
+                by_row(HEAD_SIZE),
+            ],
+            out_specs=[by_row(cols) for cols, _ in outs],
+        ),
+        out_shape=[jax.ShapeDtypeStruct((every_row, cols), kind) for cols, kind in outs],
         name="project_heads",
     )(
-        rows, w_query, key_weight, value_weight,
+        places, *pieces, w_query, key_weight, value_weight,
         q_gain.reshape(1, HEAD_SIZE), k_gain.reshape(1, HEAD_SIZE), cosine, sine,
     )
 
 
-def masked_exponents(query, key, first_row, length):
-    scores = dot(query, key, 1, 1) * HEAD_SIZE ** (-0.5)
-    row = first_row + lax.broadcasted_iota(jnp.int32, scores.shape, 0)
-    place = lax.broadcasted_iota(jnp.int32, scores.shape, 1)
-    allowed = (place <= row) & (place < length)
-    scores = jnp.where(allowed, scores, masked_score)
-    exponents = jnp.exp(scores - jnp.max(scores, axis=-1, keepdims=True))
-    return exponents, 1.0 / jnp.sum(exponents, axis=-1, keepdims=True)
+def live_lanes(length, every_row):
+    row = lax.broadcasted_iota(jnp.int32, (every_row, HEAD_SIZE), 0)
+    return jnp.where(row < length, 1.0, 0.0)
+
+
+def exponents(query, key, diagonal):
+    raised = jnp.exp2(dot(query, key, 1, 1) * (HEAD_SIZE ** (-0.5) * 1.4426950408889634))
+    if diagonal:
+        row = lax.broadcasted_iota(jnp.int32, raised.shape, 0)
+        place = lax.broadcasted_iota(jnp.int32, raised.shape, 1)
+        raised = jnp.where(place <= row, raised, 0.0)
+    return raised
+
+
+def spans(first_row):
+    whole = [(slice(0, first_row), False)] if first_row else []
+    return whole + [(slice(first_row, first_row + BLOCK_ROWS), True)]
 
 
 def attend_kernel(length_ref, query_ref, key_ref, value_ref, out_ref):
-    length = length_ref[0]
     every_row = key_ref.shape[0]
+    live = live_lanes(length_ref[0], every_row)
+    values = jnp.concatenate(
+        [(value_ref[...].astype(jnp.float32) * live).astype(jnp.bfloat16), live.astype(jnp.bfloat16)],
+        axis=1,
+    )
     for first_row in range(0, every_row, BLOCK_ROWS):
-        last = first_row + BLOCK_ROWS
-        exponents, inverse = masked_exponents(
-            query_ref[first_row:last, :], key_ref[:last, :], first_row, length
-        )
-        weights = (exponents * inverse).astype(jnp.bfloat16)
-        out_ref[first_row:last, :] = dot(weights, value_ref[:last, :], 1, 0).astype(jnp.bfloat16)
+        rows = slice(first_row, first_row + BLOCK_ROWS)
+        total = 0.0
+        for span, diagonal in spans(first_row):
+            raised = exponents(query_ref[rows, :], key_ref[span, :], diagonal)
+            total = total + dot(raised.astype(jnp.bfloat16), values[span], 1, 0)
+        out_ref[rows, :] = (total[:, :HEAD_SIZE] / total[:, HEAD_SIZE:]).astype(jnp.bfloat16)
 
 
 def attend(lengths, query, key, value):
@@ -150,51 +169,66 @@
 
 
 def attend_back_kernel(
-    length_ref, query_ref, key_ref, value_ref, grad_ref, raw_q_ref, raw_k_ref,
+    length_ref, query_ref, key_ref, value_ref, attended_ref, grad_ref, raw_q_ref, raw_k_ref,
     q_gain_ref, k_gain_ref, cos_ref, sin_ref,
     out_ref, gain_q_ref, gain_k_ref,
     key_acc, value_acc,
 ):
-    length = length_ref[0]
     every_row = key_ref.shape[0]
     group = query_ref.shape[1] // HEAD_SIZE
     scaling = HEAD_SIZE ** (-0.5)
+    live = live_lanes(length_ref[0], every_row)
+    ones = live.astype(jnp.bfloat16)
+    keys = (key_ref[...].astype(jnp.float32) * live).astype(jnp.bfloat16)
     key_acc[...] = jnp.zeros_like(key_acc)
     value_acc[...] = jnp.zeros_like(value_acc)
     gain_q = jnp.zeros((1, HEAD_SIZE), jnp.float32)
     for head in range(group):
         cut = slice(head * HEAD_SIZE, (head + 1) * HEAD_SIZE)
         for first_row in range(0, every_row, BLOCK_ROWS):
-            last = first_row + BLOCK_ROWS
-            query = query_ref[first_row:last, cut]
-            grad = grad_ref[first_row:last, cut]
-            exponents, inverse = masked_exponents(query, key_ref[:last, :], first_row, length)
-            probs = exponents * inverse
-            grad_probs = dot(grad, value_ref[:last, :], 1, 1)
-            delta = jnp.sum(grad_probs * probs, axis=-1, keepdims=True)
-            grad_scores = (probs * (grad_probs - delta)).astype(jnp.bfloat16)
-            grad_query = dot(grad_scores, key_ref[:last, :], 1, 0) * scaling
-            key_acc[:last, :] += dot(grad_scores, query, 0, 0)
-            value_acc[:last, :] += dot(probs.astype(jnp.bfloat16), grad, 0, 0)
+            rows = slice(first_row, first_row + BLOCK_ROWS)
+            query = query_ref[rows, cut]
+            grad = grad_ref[rows, cut]
+            grad_wide = grad.astype(jnp.float32)
+            delta = jnp.sum(
+                grad_wide * attended_ref[rows, cut].astype(jnp.float32), axis=-1, keepdims=True
+            )
+            sums = 0.0
+            grad_query = 0.0
+            parts = []
+            for span, diagonal in spans(first_row):
+                raised = exponents(query, key_ref[span, :], diagonal)
+                grad_scores = raised * (dot(grad, value_ref[span, :], 1, 1) - delta)
+                raised = raised.astype(jnp.bfloat16)
+                grad_scores = grad_scores.astype(jnp.bfloat16)
+                sums = sums + dot(raised, ones[span], 1, 0)
+                grad_query = grad_query + dot(grad_scores, keys[span], 1, 0)
+                parts.append((span, raised, grad_scores))
+            inverse = 1.0 / sums
+            query_share = (query.astype(jnp.float32) * inverse).astype(jnp.bfloat16)
+            grad_share = (grad_wide * inverse).astype(jnp.bfloat16)
+            for span, raised, grad_scores in parts:
+                key_acc[span, :] += dot(grad_scores, query_share, 0, 0)
+                value_acc[span, :] += dot(raised, grad_share, 0, 0)
             grad_raw, grad_gain = shaped_back(
-                grad_query, raw_q_ref[first_row:last, cut], q_gain_ref[...],
-                cos_ref[first_row:last, :], sin_ref[first_row:last, :],
+                grad_query * (inverse * scaling), raw_q_ref[rows, cut], q_gain_ref[...],
+                cos_ref[rows, :], sin_ref[rows, :],
             )
-            out_ref[first_row:last, cut] = grad_raw.astype(jnp.bfloat16)
+            out_ref[rows, cut] = grad_raw.astype(jnp.bfloat16)
             gain_q += grad_gain
     gain_q_ref[...] = gain_q
     grad_raw, grad_gain = shaped_back(
-        key_acc[...] * scaling, raw_k_ref[...], k_gain_ref[...], cos_ref[...], sin_ref[...]
+        key_acc[...] * (live * scaling), raw_k_ref[...], k_gain_ref[...], cos_ref[...], sin_ref[...]
     )
     key_col = group * HEAD_SIZE
     value_col = key_col + HEAD_SIZE
     out_ref[:, key_col:value_col] = grad_raw.astype(jnp.bfloat16)
-    out_ref[:, value_col:] = value_acc[...].astype(jnp.bfloat16)
+    out_ref[:, value_col:] = (value_acc[...] * live).astype(jnp.bfloat16)
     gain_k_ref[...] = grad_gain
 
 
 def attend_back(
-    kv_head, lengths, query, key, value, grad, raw_q, raw_k, q_gain, k_gain, cosine, sine
+    kv_head, lengths, query, key, value, attended, grad, raw_q, raw_k, q_gain, k_gain, cosine, sine
 ):
     every_row, q_cols = query.shape
     group_cols = q_cols // key.shape[1] * HEAD_SIZE
@@ -212,7 +246,7 @@
             grid=(1,),
             in_specs=[
                 cut(group_cols), cut(HEAD_SIZE), cut(HEAD_SIZE), cut(group_cols),
-                cut(group_cols), cut(HEAD_SIZE),
+                cut(group_cols), cut(group_cols), cut(HEAD_SIZE),
                 whole(1, HEAD_SIZE), whole(1, HEAD_SIZE),
                 whole(every_row, HEAD_SIZE), whole(every_row, HEAD_SIZE),
             ],
@@ -232,9 +266,37 @@
         ],
         name="attend_back",
     )(
-        lengths, query, key, value, grad, raw_q, raw_k,
+        lengths, query, key, value, attended, grad, raw_q, raw_k,
         q_gain.reshape(1, HEAD_SIZE), k_gain.reshape(1, HEAD_SIZE), cosine, sine,
     )
+
+
+def rows_at(block, rows):
+    return pl.ds(pl.multiple_of(block * rows, rows), rows)
+
+
+def join_kernel(place_ref, *refs):
+    for k, piece_ref in enumerate(refs[:-1]):
+        rows = piece_ref.shape[0]
+        refs[-1][rows_at(place_ref[k], rows), :] = piece_ref[...].astype(refs[-1].dtype)
+
+
+def in_vmem(count):
+    return [pl.BlockSpec(memory_space=pltpu.VMEM)] * count
+
+
+def join(places, pieces, dtype=jnp.bfloat16):
+    rows, width = pieces[0].shape
+    count = len(pieces)
+    if rows % 16:
+        return jnp.stack(pieces)[jnp.argsort(places)].reshape(count * rows, width).astype(dtype)
+    return pl.pallas_call(
+        join_kernel,
+        in_specs=[pl.BlockSpec(memory_space=pltpu.SMEM)] + in_vmem(count),
+        out_specs=in_vmem(1)[0],
+        out_shape=jax.ShapeDtypeStruct((count * rows, width), dtype),
+        name="join",
+    )(places, *pieces)
 
 
 def rms_norm(values, gain):
@@ -340,40 +402,54 @@
 
 class DpSum:
     def __init__(self, order, values, first):
-        count = len(bits("dp"))
+        turns = bits("dp")
         self.order = order
-        self.turns = [(first + i) % count for i in range(count)]
+        self.turns = turns[first:] + turns[:first]
         self.stage = 0
-        self.part = values
+        self.rows = values.shape[0]
+        self.terms = [(values, 0)]
         order.sums.append(self)
         self.launch()
+
+    def total(self, start):
+        parts = [
+            lax.dynamic_slice_in_dim(values, first + start, self.rows, 0).astype(jnp.float32)
+            for values, first in self.terms
+        ]
+        return sum(parts[1:], parts[0]).astype(jnp.bfloat16)
 
     def launch(self):
         count = len(self.turns)
         if self.stage < count:
             bit = self.turns[self.stage]
-            sent, self.kept = halves(self.part, bit_of("dp", bit))
-        elif self.stage < 2 * count:
+            self.rows //= 2
+            flag = bit_of("dp", bit)
+            sent = self.total((1 - flag) * self.rows)
+            self.terms = [(values, first + flag * self.rows) for values, first in self.terms]
+        else:
             bit = self.turns[2 * count - 1 - self.stage]
+            if self.stage == count:
+                self.part = self.total(0)
             sent = self.part
-        else:
-            self.flight = None
-            return
-        self.order.clock += 1.0
+        self.order.clock += 0.8
         self.flight = self.order.send(sent, "dp", bit)
 
     def advance(self):
         count = len(self.turns)
         received = self.order.gate(self.flight.received)
-        if self.stage < count:
-            self.part = (self.kept.astype(jnp.float32) + received.astype(jnp.float32)).astype(
-                jnp.bfloat16
-            )
+        self.order.token = received
+        self.stage += 1
+        if self.stage <= count:
+            self.terms = self.terms + [(received, 0)]
         else:
-            bit = self.turns[2 * count - 1 - self.stage]
-            self.part = ordered_pair(self.part, received, bit_of("dp", bit))
-        self.order.token = self.part
-        self.stage += 1
+            self.flag = bit_of("dp", self.turns[2 * count - self.stage])
+            self.last = (self.part, received)
+            self.part = ordered_pair(*self.last, self.flag)
+            self.order.token = self.part
+            self.order.clock += 1.0
+            if self.stage == 2 * count:
+                self.flight = None
+                return
         self.launch()
 
 
@@ -387,6 +463,8 @@
 
     def launch(self):
         self.flight = self.order.send(self.part, *self.turns.pop(0)) if self.turns else None
+        if self.flight is not None:
+            self.flight.arrival += 12.0
 
     def advance(self):
         self.part = self.part + self.order.gate(self.flight.received)
@@ -401,19 +479,14 @@
         self.across = order.send(values, "tensor", 1)
         self.near = order.send(values, "tensor", 0)
 
-    def land(self):
-        core = bit_of("tensor", 0)
-        side = bit_of("tensor", 1)
+    def pieces(self):
         across = self.order.land(self.across)
         far = self.order.send(across, "tensor", 0)
         near = self.order.gate(self.near.received)
-        return self.order.step(
-            4.0,
-            lambda values, near, across, far: ordered_pair(
-                ordered_pair(values, near, core), ordered_pair(across, far, core), side
-            ),
-            self.values, near, across, far.received,
-        )
+        return [self.values, near, across, far.received]
+
+    def land(self, places):
+        return self.order.step(2.0, lambda *pieces: join(places, pieces), *self.pieces())
 
 
 class Settle:
@@ -437,6 +510,26 @@
 
     def land(self):
         return self.home + self.order.land(self.flight).astype(jnp.float32)
+
+
+class SettlePieces:
+    def __init__(self, order, us, function, near_far, mine_across):
+        self.order = order
+        self.flight = order.send(order.step(us, function, near_far), "tensor", 0)
+        self.kept = order.step(us, function, mine_across)
+
+    def cross(self):
+        self.near = self.order.land(self.flight)
+        rows = self.near.shape[0] // 2
+        self.order.clock += 1.0
+        away = self.kept[rows:].astype(jnp.float32) + self.near[rows:].astype(jnp.float32)
+        self.flight = self.order.send(away.astype(jnp.bfloat16), "tensor", 1)
+
+    def land(self):
+        received = self.order.land(self.flight).astype(jnp.float32)
+        kept, near = after((self.kept, self.near), received)
+        rows = near.shape[0] // 2
+        return kept[:rows].astype(jnp.float32) + near[:rows].astype(jnp.float32) + received
 
 
 def body(
@@ -464,6 +557,11 @@
     live_rows = (first_row + jnp.arange(share_rows, dtype=jnp.int32) < length)[:, None]
     order = Order()
 
+    core = bit_of("tensor", 0)
+    side = bit_of("tensor", 1)
+    turn = jnp.arange(4, dtype=jnp.int32)
+    places = (side ^ (turn >> 1)) * 2 + (core ^ (turn & 1))
+
     resid = tokens.astype(jnp.float32)
     gather_a = Spread(order, rms_norm(resid, attn_gain).astype(jnp.bfloat16))
     cosine, sine = rotary_tables(every_row)
@@ -479,27 +577,27 @@
         )
         for head in range(kv_heads)
     ]
-    whole_a = gather_a.land()
+    pieces_a = gather_a.pieces()
     gather_ffn = Spread(order, grad_out.astype(jnp.bfloat16))
-    raw_q, raw_k, query, key, value = order.step(
+    whole_a, raw_q, raw_k, query, key, value = order.step(
         7.5,
-        lambda rows: project_heads(
-            rows, w_query, key_weight, value_weight, q_gain, k_gain, cosine, sine
+        lambda *pieces: project_heads(
+            places, pieces, w_query, key_weight, value_weight, q_gain, k_gain, cosine, sine
         ),
-        whole_a,
+        *pieces_a,
     )
     attended = order.step(
         11.0, lambda query, key, value: attend(lengths, query, key, value), query, key, value
     )
+    whole_ffn = jnp.concatenate(gather_ffn.pieces(), axis=0)
     branch_out = order.step(1.5, lambda rows: matmul(rows, w_out, 1, 0), attended)
     settle_mixed = Settle(order, branch_out)
     settle_mixed.cross()
-    whole_ffn = gather_ffn.land()
     grad_act = order.step(2.0, lambda rows: matmul(rows, w_down, 1, 1), whole_ffn)
     mixed = resid + settle_mixed.land()
 
     order.clock += 2.0
-    whole_m = Spread(order, rms_norm(mixed, mlp_gain).astype(jnp.bfloat16)).land()
+    gather_m = Spread(order, rms_norm(mixed, mlp_gain).astype(jnp.bfloat16))
 
     def hidden(rows, grad_act):
         gate_proj = dot(rows, w_gate, 1, 0)
@@ -512,7 +610,24 @@
             grad_up.astype(jnp.bfloat16),
         )
 
-    activated, grad_gate, grad_up = order.step(7.5, hidden, whole_m, grad_act)
+    near_m = jnp.concatenate([gather_m.values, gather_m.near.received], axis=0)
+    half = near_m.shape[0]
+    near_hidden = order.step(4.0, hidden, near_m, grad_act[:half])
+    far_m = jnp.concatenate(gather_m.pieces()[2:], axis=0)
+    far_hidden = order.step(4.0, hidden, far_m, grad_act[half:])
+    whole_m = jnp.concatenate([near_m, far_m], axis=0)
+    activated, grad_gate, grad_up = [
+        jnp.concatenate(both, axis=0) for both in zip(near_hidden, far_hidden)
+    ]
+    quarter = half // 2
+    near_far = [
+        jnp.concatenate([near[quarter:], far[quarter:]], axis=0)
+        for near, far in zip(near_hidden, far_hidden)
+    ]
+    mine_across = [
+        jnp.concatenate([near[:quarter], far[:quarter]], axis=0)
+        for near, far in zip(near_hidden, far_hidden)
+    ]
     grad_w_down = DpSum(
         order, order.step(2.0, lambda a, b: matmul(a, b, 0, 0), activated, whole_ffn), 0
     )
@@ -521,21 +636,26 @@
         lambda a, b: (dot(a, w_gate, 1, 1) + dot(b, w_up, 1, 1)).astype(jnp.bfloat16),
         grad_gate, grad_up,
     )
-    settle_m = Settle(order, grad_normed_m)
+    settle_m = SettlePieces(
+        order, 2.0,
+        lambda grads: (dot(grads[1], w_gate, 1, 1) + dot(grads[2], w_up, 1, 1)).astype(jnp.bfloat16),
+        near_far, mine_across,
+    )
     settle_m.cross()
     grad_w_gate = DpSum(
         order, order.step(2.0, lambda a, b: matmul(a, b, 0, 0), whole_m, grad_gate), 0
     )
     up_grad = order.step(2.0, lambda a, b: matmul(a, b, 0, 0), whole_m, grad_up)
-    layer_branch = order.step(2.0, lambda rows: matmul(rows, w_down, 1, 0), activated)
     _, mlp_norm_back = jax.vjp(rms_norm, mixed, mlp_gain)
     grad_mixed_norm, grad_mlp_gain = mlp_norm_back(settle_m.land())
     grad_mixed = grad_out + grad_mixed_norm
     order.clock += 2.0
     gather_branch = Spread(order, grad_mixed.astype(jnp.bfloat16))
     grad_w_up = DpSum(order, up_grad, 1)
-    settle_out = Settle(order, layer_branch)
-    grad_branch = gather_branch.land()
+    settle_out = SettlePieces(
+        order, 1.5, lambda rows: matmul(rows[0], w_down, 1, 0), near_far, mine_across
+    )
+    grad_branch = gather_branch.land(places)
 
     grad_attended = order.step(2.0, lambda rows: matmul(rows, w_out, 1, 1), grad_branch)
     settle_out.cross()
@@ -548,7 +668,7 @@
         out, head_q_gain, head_k_gain = order.step(
             12.5,
             lambda grad: attend_back(
-                head, lengths, query, key, value, grad, raw_q, raw_k,
+                head, lengths, query, key, value, attended, grad, raw_q, raw_k,
                 q_gain, k_gain, cosine, sine,
             ),
             grad_attended,

time: 390 us -> 360 us (0.923)
  starting transfers between devices: 73 us -> 48.6 us
  local copies, waits for them, and re-layouts: 29.4 us -> 17.2 us
  matrix products: 35.3 us -> 39.2 us
    ppermute x61, starting transfers between devices: 73 us -> 48.6 us  [swap(): return lax.ppermute(values, axis, [(i, i ^ 1 << bit) for i in range(size)])]
    convert_element_type x19 -> x21, other arithmetic: 8.9 us -> 21.7 us  [the longest x18 18.4 us: total(): return sum(parts[1:], parts[0]).astype(jnp.bfloat16)]
    select_n x29 -> x18, other arithmetic: 12.5 us -> 3.53 us  [ordered_pair(): jnp.where(is_first, mine, other)]
    unnamed x130 -> x110, local copies, waits for them, and re-layouts: 13.8 us -> 7.06 us
    concatenate x0 -> x13, other arithmetic: none -> 4.96 us  [the longest x1 1.62 us: body(): whole_ffn = jnp.concatenate(gather_ffn.pieces(), axis=0)]
    pallas_call x1 -> x2, Pallas kernels: 7.28 us -> 11.8 us  [the longest x1 8.84 us: project_heads(): pl.pallas_call(heads_kernel, grid_spec=pltpu.PrefetchScalarGridSpec(num_s...]
    dynamic_slice x18 -> x6, local copies, waits for them, and re-layouts: 6.83 us -> 2.78 us  [total(): lax.dynamic_slice_in_dim(values, first + start, self.rows, 0)]
    dot_general x16 -> x21, matrix products: 35.3 us -> 39.2 us  [dot(): lax.dot_general(left, right, (((left_dim,), (right_dim,)), ((), ())), pre...]
  transfers between devices with their start and end apart: 61 -> 61, of which waited for: 23 -> 27; matrix products, arithmetic and copies ran while one was open for 19% -> 25% of each run, Pallas kernels for 7% -> 12%
where the time goes in v3:
time: 360 us; the launch traced here: 355 us
  waiting for transfers between devices  148 us (41%)
  other arithmetic  57.6 us (16%)
  starting transfers between devices  48.6 us (14%)
  Pallas kernels  42 us (12%)
  matrix products  39.2 us (11%)
  local copies, waits for them, and re-layouts  17.2 us (5%)
    ppermute x61, waiting for transfers between devices, swap(): return lax.ppermute(values, axis, [(i, i ^ 1 << bit) for i in range(size)])  148 us
    ppermute x61, starting transfers between devices, swap(): return lax.ppermute(values, axis, [(i, i ^ 1 << bit) for i in range(size)])  48.6 us
    dot_general x21, matrix products, dot(): lax.dot_general(left, right, (((left_dim,), (right_dim,)), ((), ())), pre...  39.2 us
    pallas_call x2, Pallas kernels, attend_back(): pl.pallas_call(attend_back_kernel, grid_spec=pltpu.PrefetchScalarGridSpec...  22 us
    convert_element_type x18, other arithmetic, total(): return sum(parts[1:], parts[0]).astype(jnp.bfloat16)  18.4 us
    pallas_call x1, Pallas kernels, project_heads(): pl.pallas_call(heads_kernel, grid_spec=pltpu.PrefetchScalarGridSpec(num_s...  8.84 us
    pallas_call x1, Pallas kernels, attend(): pl.pallas_call(attend_kernel, grid_spec=pltpu.PrefetchScalarGridSpec(num_...  8.18 us
  transfers between devices with their start and end apart: 61, of which 27 were waited for; matrix products, arithmetic and copies ran while one was open for 25% of the time, Pallas kernels for 12%

profile of v3, /device:TPU:0, one launch (start us, length us, event | category | flops | bytes accessed | tf_op | source)
XLA Modules:
  0.0 355.3 jit_solution(12424986699070341966)
XLA Ops:
  3.3 3.0 collective-permute-start.1
  7.2 11.2 %collective-permute-done.1.across_ref = bf16[256,1024]{1,0:T(8,128)(2,1)} collective-permute-done((bf16[256,1024]{1,0:T(8,128)(2,1)S(1)}, bf16[256,1024]{1,0:T(8,128)(2,1)}, u32[]{:S(2)}, u32[]{:S(2)}) %collective-permute-start.1) | collective-permute-done | bytes 524320 | tf_op jit(solution)/shard_map/ppermute | solution.py:320
  18.3 1.7 collective-permute-start.3
  20.6 2.0 fusion.26
  24.7 8.8 %project_heads.1 = (bf16[1024,1024]{1,0:T(8,128)(2,1)}, f32[1024,512]{1,0:T(8,128)}, f32[1024,256]{1,0:T(8,128)}, bf16[1024,512]{1,0:T(8,128)(2,1)}, bf16[1024,2...) custom-call(s32[4]{0:T(128)} %xor_add_fusion.place_ref, bf16[256,1024]{1,0:T(8,128)(2,1)} %copy-done.12, ...), custom_call_target="tpu_custom_call" | custom-call | tf_op jit(solution)/shard_map/project_heads/pallas_call | solution.py:91
  33.6 8.2 %attend.1.attended_ref = bf16[1024,512]{1,0:T(8,128)(2,1)} custom-call(s32[1]{0:T(128)} %copy.27.length_ref, bf16[1024,512]{1,0:T(8,128)(2,1)} %get-tuple-element.199.query_ref, bf16[1024,256]{1,0:T(8,128)(2,1)} %get-tuple-element.200.key_ref, bf16[1024,256]{1,0:T(8,128)(2,1)} %get-tuple-element.201.value_ref), custom_call_target="tpu_custom_call" | custom-call | tf_op jit(solution)/shard_map/attend/pallas_call | solution.py:158
  41.8 2.5 convolution_convert_fusion
  47.4 3.5 collective-permute-done.6
  50.9 1.6 convert_add_fusion.1
  53.0 1.6 pad_maximum_fusion
  54.7 3.0 convolution_convert_fusion.4
  57.6 9.1 %collective-permute-done.5 = bf16[256,1024]{1,0:T(8,128)(2,1)S(1)} collective-permute-done((bf16[256,1024]{1,0:T(8,128)(2,1)S(1)}, bf16[256,1024]{1,0:T(8,128)(2,1)S(1)}, u32[]{:S(2)}, u32[]{:S(2)}) %collective-permute-start.5) | collective-permute-done | bytes 524320 | tf_op jit(solution)/shard_map/ppermute | solution.py:320
  72.6 1.8 add_convert_fusion.4
  74.4 9.8 %collective-permute-done.9 = bf16[256,1024]{1,0:T(8,128)(2,1)S(1)} collective-permute-done((bf16[256,1024]{1,0:T(8,128)(2,1)}, bf16[256,1024]{1,0:T(8,128)(2,1)S(1)}, u32[]{:S(2)}, u32[]{:S(2)}) %collective-permute-start.9) | collective-permute-done | bytes 524320 | tf_op jit(solution)/shard_map/ppermute | solution.py:320
  84.3 1.7 collective-permute-done.10
  87.1 1.8 add_convert_fusion.3
  93.4 2.0 convolution_convert_fusion.1
  95.5 1.6 collective-permute-start.13
  101.4 1.9 convolution_convert_fusion.3
  103.8 1.9 convolution_convert_fusion.2
  105.7 10.3 %collective-permute-done.13 = bf16[384,1024]{1,0:T(8,128)(2,1)S(1)} collective-permute-done((bf16[384,1024]{1,0:T(8,128)(2,1)S(1)}, bf16[384,1024]{1,0:T(8,128)(2,1)S(1)}, u32[]{:S(2)}, u32[]{:S(2)}) %collective-permute-start.13) | collective-permute-done | bytes 786464 | tf_op jit(solution)/shard_map/ppermute | solution.py:320
  116.1 1.6 collective-permute-start.18
  121.7 2.0 convolution_convert_fusion.6
  124.2 1.9 convolution_convert_fusion.5
  127.0 5.3 %collective-permute-done.17 = bf16[512,768]{1,0:T(8,128)(2,1)S(1)} collective-permute-done((bf16[512,768]{1,0:T(8,128)(2,1)S(1)}, bf16[512,768]{1,0:T(8,128)(2,1)S(1)}, u32[]{:S(2)}, u32[]{:S(2)}) %collective-permute-start.17) | collective-permute-done | bytes 786464 | tf_op jit(solution)/shard_map/ppermute | solution.py:320
  136.0 2.6 collective-permute-start.22
  140.6 3.0 join.1
  143.6 4.2 %convolution_convert_fusion.10.grad_ref = bf16[1024,512]{1,0:T(8,128)(2,1)} fusion(bf16[1024,1024]{1,0:T(8,128)(2,1)} %join.1, bf16[512,1024]{1,0:T(8,128)(2,1)} %param.23), kind=kOutput, calls=%fused_computation.45 | convolution fusion | flops 1074266112 | bytes 4194304 | tf_op jit(solution)/shard_map/dot_general | solution.py:46
  147.8 2.2 add_convert_fusion.5
  151.8 15.2 %collective-permute-done.21 = bf16[512,768]{1,0:T(8,128)(2,1)} collective-permute-done((bf16[512,768]{1,0:T(8,128)(2,1)}, bf16[512,768]{1,0:T(8,128)(2,1)}, u32[]{:S(2)}, u32[]{:S(2)}) %collective-permute-start.21) | collective-permute-done | bytes 786464 | tf_op jit(solution)/shard_map/ppermute | solution.py:320
  167.0 1.9 add_convert_fusion.7
  174.1 10.8 %attend_back.2 = (bf16[1024,512]{1,0:T(8,128)(2,1)}, f32[1,128]{1,0:T(1,128)}, f32[1,128]{1,0:T(1,128)}) custom-call(s32[1]{0:T(128)} %copy.27.length_ref, bf16[1024,512]{1,0:T(8,128)(2,1)} %get-tuple-element.199.query_ref, bf16[1024,256]{1,0:T(8,128)(2,1)} %get-tuple-element.200.key_ref, bf16[1024,256]{1,0:T(8,128)(2,1)} %get-tuple-element.201.value_ref, ...), custom_call_target="tpu_custom_call" | custom-call | tf_op jit(solution)/shard_map/attend_back/pallas_call | solution.py:242
  184.9 3.1 convolution_convert_fusion.8
  189.4 1.8 add_convert_fusion.16
  191.2 2.9 collective-permute-start.30
  194.3 1.7 add_convert_fusion.12
  196.1 1.9 add_convert_fusion.15
  199.5 11.2 %attend_back.3 = (bf16[1024,512]{1,0:T(8,128)(2,1)}, f32[1,128]{1,0:T(1,128)}, f32[1,128]{1,0:T(1,128)}) custom-call(s32[1]{0:T(128)} %copy.27.length_ref, bf16[1024,512]{1,0:T(8,128)(2,1)} %get-tuple-element.199.query_ref, bf16[1024,256]{1,0:T(8,128)(2,1)} %get-tuple-element.200.key_ref, bf16[1024,256]{1,0:T(8,128)(2,1)} %get-tuple-element.201.value_ref, ...), custom_call_target="tpu_custom_call" | custom-call | tf_op jit(solution)/shard_map/attend_back/pallas_call | solution.py:242
  210.7 3.2 convolution_convert_fusion.7
  214.1 2.1 collective-permute-start.26
  218.6 2.1 collective-permute-start.34
  223.4 4.2 %collective-permute-done.26 = bf16[128,1024]{1,0:T(8,128)(2,1)S(1)} collective-permute-done((bf16[128,1024]{1,0:T(8,128)(2,1)S(1)}, bf16[128,1024]{1,0:T(8,128)(2,1)S(1)}, u32[]{:S(2)}, u32[]{:S(2)}) %collective-permute-start.26) | collective-permute-done | bytes 262176 | tf_op jit(solution)/shard_map/ppermute | solution.py:320
  232.0 6.8 %collective-permute-done.35 = bf16[512,512]{1,0:T(8,128)(2,1)S(1)} collective-permute-done((bf16[512,512]{1,0:T(8,128)(2,1)S(1)}, bf16[512,512]{1,0:T(8,128)(2,1)S(1)}, u32[]{:S(2)}, u32[]{:S(2)}) %collective-permute-start.35) | collective-permute-done | bytes 524320 | tf_op jit(solution)/shard_map/ppermute | solution.py:320
  239.1 2.6 collective-permute-done.33
  243.1 6.3 %collective-permute-done.32 = bf16[64,1024]{1,0:T(8,128)(2,1)S(1)} collective-permute-done((bf16[64,1024]{1,0:T(8,128)(2,1)S(1)}, bf16[64,1024]{1,0:T(8,128)(2,1)S(1)}, u32[]{:S(2)}, u32[]{:S(2)}) %collective-permute-start.32) | collective-permute-done | bytes 131104 | tf_op jit(solution)/shard_map/ppermute | solution.py:320
  250.5 2.6 collective-permute-start.43
  253.4 2.1 fusion.37
  256.4 2.5 collective-permute-start.36
  259.0 13.8 %collective-permute-done.37 = bf16[256,512]{1,0:T(8,128)(2,1)S(1)} collective-permute-done((bf16[256,512]{1,0:T(8,128)(2,1)S(1)}, bf16[256,512]{1,0:T(8,128)(2,1)S(1)}, u32[]{:S(2)}, u32[]{:S(2)}) %collective-permute-start.37) | collective-permute-done | bytes 262176 | tf_op jit(solution)/shard_map/ppermute | solution.py:320
  273.2 2.4 collective-permute-done.42
  279.9 2.7 collective-permute-done.36
  283.2 2.5 add_select_fusion
  285.6 4.6 %collective-permute-done.47 = bf16[256,768]{1,0:T(8,128)(2,1)S(1)} collective-permute-done((bf16[256,768]{1,0:T(8,128)(2,1)S(1)}, bf16[256,768]{1,0:T(8,128)(2,1)S(1)}, u32[]{:S(2)}, u32[]{:S(2)}) %collective-permute-start.47) | collective-permute-done | bytes 393248 | tf_op jit(solution)/shard_map/ppermute | solution.py:320
  291.9 2.2 collective-permute-start.56
  295.2 6.7 %collective-permute-done.49 = bf16[128,1024]{1,0:T(8,128)(2,1)S(1)} collective-permute-done((bf16[128,1024]{1,0:T(8,128)(2,1)S(1)}, bf16[128,1024]{1,0:T(8,128)(2,1)S(1)}, u32[]{:S(2)}, u32[]{:S(2)}) %collective-permute-start.49) | collective-permute-done | bytes 262176 | tf_op jit(solution)/shard_map/ppermute | solution.py:320
  305.7 10.8 %collective-permute-done.51 = bf16[256,512]{1,0:T(8,128)(2,1)S(1)} collective-permute-done((bf16[256,512]{1,0:T(8,128)(2,1)S(1)}, bf16[256,512]{1,0:T(8,128)(2,1)S(1)}, u32[]{:S(2)}, u32[]{:S(2)}) %collective-permute-start.51) | collective-permute-done | bytes 262176 | tf_op jit(solution)/shard_map/ppermute | solution.py:320
  316.5 3.4 collective-permute-start.55
  320.3 6.9 %collective-permute-done.55 = bf16[256,512]{1,0:T(8,128)(2,1)S(1)} collective-permute-done((bf16[256,512]{1,0:T(8,128)(2,1)S(1)}, bf16[256,512]{1,0:T(8,128)(2,1)S(1)}, u32[]{:S(2)}, u32[]{:S(2)}) %collective-permute-start.55) | collective-permute-done | bytes 262176 | tf_op jit(solution)/shard_map/ppermute | solution.py:320
  327.7 6.9 %collective-permute-done.57 = f32[2304]{0:T(1024)S(1)} collective-permute-done((f32[2304]{0:T(1024)S(1)}, f32[2304]{0:T(1024)S(1)}, u32[]{:S(2)}, u32[]{:S(2)}) %collective-permute-start.57) | collective-permute-done | bytes 9248 | tf_op jit(solution)/shard_map/ppermute | solution.py:320
  334.7 1.9 fusion.36
  336.6 1.6 collective-permute-start.58
  342.9 2.1 fusion.35
  345.3 3.3 collective-permute-done.58
  353.4 1.6 pad_maximum_fusion.2
  (322 shorter events, 82.3 us)
Async XLA Ops:
  0.6 71.9 %copy-start = (bf16[1024,768]{1,0:T(8,128)(2,1)S(1)}, bf16[1024,768]{1,0:T(8,128)(2,1)}, u32[]{:S(2)}) copy-start(bf16[1024,768]{1,0:T(8,128)(2,1)} %param.24) | copy-start | bytes 4718596
  3.3 15.0 %collective-permute-start.1 = (bf16[256,1024]{1,0:T(8,128)(2,1)S(1)}, bf16[256,1024]{1,0:T(8,128)(2,1)}, u32[]{:S(2)}, u32[]{:S(2)}) collective-permute-start(bf16[256,1024]{1,0:T(8,128)(2,1)S(1)} %fusion.4.mine_ref), channel_id=1, source_target_pairs={{0,2},{1,3},{2,0},{3,1},{4,6},{5,7},{6,4},{7,5},{8,10},{9,11},{10,... | collective-permute-start | bytes 1572872 | tf_op jit(solution)/shard_map/ppermute | solution.py:320
  6.3 17.6 %collective-permute-start = (bf16[256,1024]{1,0:T(8,128)(2,1)S(1)}, bf16[256,1024]{1,0:T(8,128)(2,1)}, u32[]{:S(2)}, u32[]{:S(2)}) collective-permute-start(bf16[256,1024]{1,0:T(8,128)(2,1)S(1)} %fusion.4.mine_ref), channel_id=1, source_target_pairs={{0,1},{1,0},{2,3},{3,2},{4,5},{5,4},{6,7},{7,6},{8,9},{9,8},{10,11... | collective-permute-start | bytes 1572872 | tf_op jit(solution)/shard_map/ppermute | solution.py:320
  18.3 5.6 %collective-permute-start.2 = (bf16[256,1024]{1,0:T(8,128)(2,1)}, bf16[256,1024]{1,0:T(8,128)(2,1)S(1)}, u32[]{:S(2)}, u32[]{:S(2)}) collective-permute-start(bf16[256,1024]{1,0:T(8,128)(2,1)} %collective-permute-done.1.across_ref), channel_id=1, source_target_pairs={{0,1},{1,0},{2,3},{3,2},{4,5},{5,4},{6,7},{7,6},{8,9},{9,8},{10,11... | collective-permute-start | bytes 1572872 | tf_op jit(solution)/shard_map/ppermute | solution.py:320
  18.3 23.4 %collective-permute-start.3 = (bf16[256,1024]{1,0:T(8,128)(2,1)S(1)}, bf16[256,1024]{1,0:T(8,128)(2,1)}, u32[]{:S(2)}, u32[]{:S(2)}) collective-permute-start(bf16[256,1024]{1,0:T(8,128)(2,1)S(1)} %fusion.21), channel_id=1, source_target_pairs={{0,2},{1,3},{2,0},{3,1},{4,6},{5,7},{6,4},{7,5},{8,10},{9,11},{10,... | collective-permute-start | bytes 1572872 | tf_op jit(solution)/shard_map/ppermute | solution.py:320
  46.6 4.3 %collective-permute-start.4 = (bf16[2,1,256,1024]{3,2,1,0:T(8,128)(2,1)}, bf16[2,1,256,1024]{3,2,1,0:T(8,128)(2,1)S(1)}, u32[]{:S(2)}, u32[]{:S(2)}) collective-permute-start(bf16[2,1,256,1024]{3,2,1,0:T(8,128)(2,1)} %constant_dynamic-slice_fusion.7), channel_id=1, source_target_pairs={{0,1},{1,0},{2,3},{3,2},{4,5},{5,4},{6,7},{7,6},{8,9},{9,8},{10,11... | collective-permute-start | bytes 3145736 | tf_op jit(solution)/shard_map/ppermute | solution.py:320
  46.9 4.0 %collective-permute-start.6 = (bf16[256,1024]{1,0:T(8,128)(2,1)S(1)}, bf16[256,1024]{1,0:T(8,128)(2,1)}, u32[]{:S(2)}, u32[]{:S(2)}) collective-permute-start(bf16[256,1024]{1,0:T(8,128)(2,1)S(1)} %fusion.21), channel_id=1, source_target_pairs={{0,1},{1,0},{2,3},{3,2},{4,5},{5,4},{6,7},{7,6},{8,9},{9,8},{10,11... | collective-permute-start | bytes 1572872 | tf_op jit(solution)/shard_map/ppermute | solution.py:320
  47.1 5.9 %collective-permute-start.7 = (bf16[256,1024]{1,0:T(8,128)(2,1)}, bf16[256,1024]{1,0:T(8,128)(2,1)}, u32[]{:S(2)}, u32[]{:S(2)}) collective-permute-start(bf16[256,1024]{1,0:T(8,128)(2,1)} %collective-permute-done.3), channel_id=1, source_target_pairs={{0,1},{1,0},{2,3},{3,2},{4,5},{5,4},{6,7},{7,6},{8,9},{9,8},{10,11... | collective-permute-start | bytes 1572872 | tf_op jit(solution)/shard_map/ppermute | solution.py:320
  52.6 14.1 %collective-permute-start.5 = (bf16[256,1024]{1,0:T(8,128)(2,1)S(1)}, bf16[256,1024]{1,0:T(8,128)(2,1)S(1)}, u32[]{:S(2)}, u32[]{:S(2)}) collective-permute-start(bf16[256,1024]{1,0:T(8,128)(2,1)S(1)} %fusion.22), channel_id=1, source_target_pairs={{0,2},{1,3},{2,0},{3,1},{4,6},{5,7},{6,4},{7,5},{8,10},{9,11},{10,... | collective-permute-start | bytes 1572872 | tf_op jit(solution)/shard_map/ppermute | solution.py:320
  68.0 2.3 collective-permute-start.8
  69.5 14.6 %collective-permute-start.9 = (bf16[256,1024]{1,0:T(8,128)(2,1)}, bf16[256,1024]{1,0:T(8,128)(2,1)S(1)}, u32[]{:S(2)}, u32[]{:S(2)}) collective-permute-start(bf16[256,1024]{1,0:T(8,128)(2,1)} %multiply_convert_fusion.2), channel_id=1, source_target_pairs={{0,2},{1,3},{2,0},{3,1},{4,6},{5,7},{6,4},{7,5},{8,10},{9,11},{10,... | collective-permute-start | bytes 1572872 | tf_op jit(solution)/shard_map/ppermute | solution.py:320
  84.1 1.9 collective-permute-start.10
  91.5 9.1 %collective-permute-start.11 = (bf16[512,1024]{1,0:T(8,128)(2,1)S(1)}, bf16[512,1024]{1,0:T(8,128)(2,1)S(1)}, u32[]{:S(2)}, u32[]{:S(2)}) collective-permute-start(bf16[512,1024]{1,0:T(8,128)(2,1)S(1)} %add_convert_fusion.2), channel_id=1, source_target_pairs={{0,1},{1,0},{2,3},{3,2},{4,5},{5,4},{6,7},{7,6},{8,9},{9,8},{10,11... | collective-permute-start | bytes 3145736 | tf_op jit(solution)/shard_map/ppermute | solution.py:320
  95.4 30.8 %copy-start.23 = (bf16[768,1024]{1,0:T(8,128)(2,1)}, bf16[768,1024]{1,0:T(8,128)(2,1)S(1)}, u32[]{:S(2)}) copy-start(bf16[768,1024]{1,0:T(8,128)(2,1)S(1)} %convolution_convert_fusion.1) | copy-start | bytes 4718596
  95.5 20.4 %collective-permute-start.13 = (bf16[384,1024]{1,0:T(8,128)(2,1)S(1)}, bf16[384,1024]{1,0:T(8,128)(2,1)S(1)}, u32[]{:S(2)}, u32[]{:S(2)}) collective-permute-start(bf16[384,1024]{1,0:T(8,128)(2,1)S(1)} %constant_dynamic-slice_fusion.4), channel_id=1, source_target_pairs={{0,4},{4,0},{8,12},{12,8},{16,20},{20,16},{24,28},{28,24},{1,5},{5... | collective-permute-start | bytes 2359304 | tf_op jit(solution)/shard_map/ppermute | solution.py:320
  100.9 17.8 %collective-permute-start.12 = (bf16[256,1024]{1,0:T(8,128)(2,1)S(1)}, bf16[256,1024]{1,0:T(8,128)(2,1)S(1)}, u32[]{:S(2)}, u32[]{:S(2)}) collective-permute-start(bf16[256,1024]{1,0:T(8,128)(2,1)S(1)} %add_convert_fusion.6), channel_id=1, source_target_pairs={{0,2},{1,3},{2,0},{3,1},{4,6},{5,7},{6,4},{7,5},{8,10},{9,11},{10,... | collective-permute-start | bytes 1572872 | tf_op jit(solution)/shard_map/ppermute | solution.py:320
  103.3 29.0 %copy-start.22 = (bf16[1024,768]{1,0:T(8,128)(2,1)}, bf16[1024,768]{1,0:T(8,128)(2,1)S(1)}, u32[]{:S(2)}) copy-start(bf16[1024,768]{1,0:T(8,128)(2,1)S(1)} %convolution_convert_fusion.3) | copy-start | bytes 4718596
  103.4 28.9 %collective-permute-start.17 = (bf16[512,768]{1,0:T(8,128)(2,1)S(1)}, bf16[512,768]{1,0:T(8,128)(2,1)S(1)}, u32[]{:S(2)}, u32[]{:S(2)}) collective-permute-start(bf16[512,768]{1,0:T(8,128)(2,1)S(1)} %constant_dynamic-slice_fusion.6), channel_id=1, source_target_pairs={{0,4},{4,0},{8,12},{12,8},{16,20},{20,16},{24,28},{28,24},{1,5},{5... | collective-permute-start | bytes 2359304 | tf_op jit(solution)/shard_map/ppermute | solution.py:320
  116.1 10.1 %collective-permute-start.18 = (bf16[192,1024]{1,0:T(8,128)(2,1)S(1)}, bf16[192,1024]{1,0:T(8,128)(2,1)S(1)}, u32[]{:S(2)}, u32[]{:S(2)}) collective-permute-start(bf16[192,1024]{1,0:T(8,128)(2,1)S(1)} %add_convert_fusion.9), channel_id=1, source_target_pairs={{0,8},{4,12},{8,0},{12,4},{16,24},{20,28},{24,16},{28,20},{1,9},{5... | collective-permute-start | bytes 1179656 | tf_op jit(solution)/shard_map/ppermute | solution.py:320
  121.2 12.6 %collective-permute-start.16 = (bf16[256,1024]{1,0:T(8,128)(2,1)S(1)}, bf16[256,1024]{1,0:T(8,128)(2,1)S(1)}, u32[]{:S(2)}, u32[]{:S(2)}) collective-permute-start(bf16[256,1024]{1,0:T(8,128)(2,1)S(1)} %get-tuple-element.250.refs_0_), channel_id=1, source_target_pairs={{0,2},{1,3},{2,0},{3,1},{4,6},{5,7},{6,4},{7,5},{8,10},{9,11},{10,... | collective-permute-start | bytes 1572872 | tf_op jit(solution)/shard_map/ppermute | solution.py:320
  121.7 18.0 %collective-permute-start.15 = (bf16[256,1024]{1,0:T(8,128)(2,1)S(1)}, bf16[256,1024]{1,0:T(8,128)(2,1)S(1)}, u32[]{:S(2)}, u32[]{:S(2)}) collective-permute-start(bf16[256,1024]{1,0:T(8,128)(2,1)S(1)} %get-tuple-element.250.refs_0_), channel_id=1, source_target_pairs={{0,1},{1,0},{2,3},{3,2},{4,5},{5,4},{6,7},{7,6},{8,9},{9,8},{10,11... | collective-permute-start | bytes 1572872 | tf_op jit(solution)/shard_map/ppermute | solution.py:320
  123.7 24.2 %collective-permute-start.14 = (bf16[512,1024]{1,0:T(8,128)(2,1)}, bf16[512,1024]{1,0:T(8,128)(2,1)}, u32[]{:S(2)}, u32[]{:S(2)}) collective-permute-start(bf16[512,1024]{1,0:T(8,128)(2,1)} %convolution_convert_fusion.6), channel_id=1, source_target_pairs={{0,1},{1,0},{2,3},{3,2},{4,5},{5,4},{6,7},{7,6},{8,9},{9,8},{10,11... | collective-permute-start | bytes 3145736 | tf_op jit(solution)/shard_map/ppermute | solution.py:320
  133.8 6.8 %collective-permute-start.19 = (bf16[256,1024]{1,0:T(8,128)(2,1)S(1)}, bf16[256,1024]{1,0:T(8,128)(2,1)}, u32[]{:S(2)}, u32[]{:S(2)}) collective-permute-start(bf16[256,1024]{1,0:T(8,128)(2,1)S(1)} %collective-permute-done.16.refs_2_), channel_id=1, source_target_pairs={{0,1},{1,0},{2,3},{3,2},{4,5},{5,4},{6,7},{7,6},{8,9},{9,8},{10,11... | collective-permute-start | bytes 1572872 | tf_op jit(solution)/shard_map/ppermute | solution.py:320
  136.0 14.0 %collective-permute-start.22 = (bf16[96,1024]{1,0:T(8,128)(2,1)}, bf16[96,1024]{1,0:T(8,128)(2,1)}, u32[]{:S(2)}, u32[]{:S(2)}) collective-permute-start(bf16[96,1024]{1,0:T(8,128)(2,1)} %add_convert_fusion.18), channel_id=1, source_target_pairs={{0,16},{4,20},{8,24},{12,28},{16,0},{20,4},{24,8},{28,12},{1,17},{... | collective-permute-start | bytes 589832 | tf_op jit(solution)/shard_map/ppermute | solution.py:320
  138.6 28.5 %collective-permute-start.21 = (bf16[512,768]{1,0:T(8,128)(2,1)}, bf16[512,768]{1,0:T(8,128)(2,1)}, u32[]{:S(2)}, u32[]{:S(2)}) collective-permute-start(bf16[512,768]{1,0:T(8,128)(2,1)} %constant_dynamic-slice_fusion.5), channel_id=1, source_target_pairs={{0,8},{4,12},{8,0},{12,4},{16,24},{20,28},{24,16},{28,20},{1,9},{5... | collective-permute-start | bytes 2359304 | tf_op jit(solution)/shard_map/ppermute | solution.py:320
  139.7 49.3 %collective-permute-start.25 = (bf16[256,768]{1,0:T(8,128)(2,1)}, bf16[256,768]{1,0:T(8,128)(2,1)S(1)}, u32[]{:S(2)}, u32[]{:S(2)}) collective-permute-start(bf16[256,768]{1,0:T(8,128)(2,1)} %add_convert_fusion.8), channel_id=1, source_target_pairs={{0,8},{4,12},{8,0},{12,4},{16,24},{20,28},{24,16},{28,20},{1,9},{5... | collective-permute-start | bytes 1179656 | tf_op jit(solution)/shard_map/ppermute | solution.py:320
  151.4 39.8 %collective-permute-start.24 = (bf16[96,1024]{1,0:T(8,128)(2,1)S(1)}, bf16[96,1024]{1,0:T(8,128)(2,1)S(1)}, u32[]{:S(2)}, u32[]{:S(2)}) collective-permute-start(bf16[96,1024]{1,0:T(8,128)(2,1)S(1)} %add_convert_fusion.17), channel_id=1, source_target_pairs={{0,16},{4,20},{8,24},{12,28},{16,0},{20,4},{24,8},{28,12},{1,17},{... | collective-permute-start | bytes 589832 | tf_op jit(solution)/shard_map/ppermute | solution.py:320
  172.1 22.1 %collective-permute-start.23 = (bf16[256,1024]{1,0:T(8,128)(2,1)}, bf16[256,1024]{1,0:T(8,128)(2,1)}, u32[]{:S(2)}, u32[]{:S(2)}) collective-permute-start(bf16[256,1024]{1,0:T(8,128)(2,1)} %constant_dynamic-slice_fusion.2), channel_id=1, source_target_pairs={{0,4},{4,0},{8,12},{12,8},{16,20},{20,16},{24,28},{28,24},{1,5},{5... | collective-permute-start | bytes 1572872 | tf_op jit(solution)/shard_map/ppermute | solution.py:320
  173.6 22.4 %collective-permute-start.27 = (bf16[256,768]{1,0:T(8,128)(2,1)}, bf16[256,768]{1,0:T(8,128)(2,1)}, u32[]{:S(2)}, u32[]{:S(2)}) collective-permute-start(bf16[256,768]{1,0:T(8,128)(2,1)} %add_convert_fusion.7), channel_id=1, source_target_pairs={{0,16},{4,20},{8,24},{12,28},{16,0},{20,4},{24,8},{28,12},{1,17},{... | collective-permute-start | bytes 1179656 | tf_op jit(solution)/shard_map/ppermute | solution.py:320
  173.6 109.1 %collective-permute-start.20 = (bf16[256,1024]{1,0:T(8,128)(2,1)}, bf16[256,1024]{1,0:T(8,128)(2,1)}, u32[]{:S(2)}, u32[]{:S(2)}) collective-permute-start(bf16[256,1024]{1,0:T(8,128)(2,1)} %add_convert_fusion.5), channel_id=1, source_target_pairs={{0,2},{1,3},{2,0},{3,1},{4,6},{5,7},{6,4},{7,5},{8,10},{9,11},{10,... | collective-permute-start | bytes 1572872 | tf_op jit(solution)/shard_map/ppermute | solution.py:320
  188.9 25.1 %collective-permute-start.31 = (bf16[512,512]{1,0:T(8,128)(2,1)}, bf16[512,512]{1,0:T(8,128)(2,1)}, u32[]{:S(2)}, u32[]{:S(2)}) collective-permute-start(bf16[512,512]{1,0:T(8,128)(2,1)} %constant_dynamic-slice_fusion.1), channel_id=1, source_target_pairs={{0,4},{4,0},{8,12},{12,8},{16,20},{20,16},{24,28},{28,24},{1,5},{5... | collective-permute-start | bytes 1572872 | tf_op jit(solution)/shard_map/ppermute | solution.py:320
  191.2 25.9 %collective-permute-start.30 = (bf16[128,768]{1,0:T(8,128)(2,1)}, bf16[128,768]{1,0:T(8,128)(2,1)}, u32[]{:S(2)}, u32[]{:S(2)}) collective-permute-start(bf16[128,768]{1,0:T(8,128)(2,1)} %add_convert_fusion.16), channel_id=1, source_target_pairs={{0,16},{4,20},{8,24},{12,28},{16,0},{20,4},{24,8},{28,12},{1,17},{... | collective-permute-start | bytes 589832 | tf_op jit(solution)/shard_map/ppermute | solution.py:320
  194.3 24.3 %collective-permute-start.29 = (bf16[192,1024]{1,0:T(8,128)(2,1)S(1)}, bf16[192,1024]{1,0:T(8,128)(2,1)}, u32[]{:S(2)}, u32[]{:S(2)}) collective-permute-start(bf16[192,1024]{1,0:T(8,128)(2,1)S(1)} %pad_maximum_fusion.30), channel_id=1, source_target_pairs={{0,8},{4,12},{8,0},{12,4},{16,24},{20,28},{24,16},{28,20},{1,9},{5... | collective-permute-start | bytes 1179656 | tf_op jit(solution)/shard_map/ppermute | solution.py:320
  197.9 24.0 %collective-permute-start.28 = (bf16[128,768]{1,0:T(8,128)(2,1)}, bf16[128,768]{1,0:T(8,128)(2,1)}, u32[]{:S(2)}, u32[]{:S(2)}) collective-permute-start(bf16[128,768]{1,0:T(8,128)(2,1)} %add_convert_fusion.15), channel_id=1, source_target_pairs={{0,4},{4,0},{8,12},{12,8},{16,20},{20,16},{24,28},{28,24},{1,5},{5... | collective-permute-start | bytes 589832 | tf_op jit(solution)/shard_map/ppermute | solution.py:320
  214.1 13.5 %collective-permute-start.26 = (bf16[128,1024]{1,0:T(8,128)(2,1)S(1)}, bf16[128,1024]{1,0:T(8,128)(2,1)S(1)}, u32[]{:S(2)}, u32[]{:S(2)}) collective-permute-start(bf16[128,1024]{1,0:T(8,128)(2,1)S(1)} %copy-done.41), channel_id=1, source_target_pairs={{0,8},{4,12},{8,0},{12,4},{16,24},{20,28},{24,16},{28,20},{1,9},{5... | collective-permute-start | bytes 786440 | tf_op jit(solution)/shard_map/ppermute | solution.py:320
  217.2 21.7 %collective-permute-start.35 = (bf16[512,512]{1,0:T(8,128)(2,1)S(1)}, bf16[512,512]{1,0:T(8,128)(2,1)S(1)}, u32[]{:S(2)}, u32[]{:S(2)}) collective-permute-start(bf16[512,512]{1,0:T(8,128)(2,1)S(1)} %constant_dynamic-slice_fusion), channel_id=1, source_target_pairs={{0,8},{4,12},{8,0},{12,4},{16,24},{20,28},{24,16},{28,20},{1,9},{5... | collective-permute-start | bytes 1572872 | tf_op jit(solution)/shard_map/ppermute | solution.py:320
  218.6 20.4 %collective-permute-start.34 = (bf16[128,768]{1,0:T(8,128)(2,1)S(1)}, bf16[128,768]{1,0:T(8,128)(2,1)S(1)}, u32[]{:S(2)}, u32[]{:S(2)}) collective-permute-start(bf16[128,768]{1,0:T(8,128)(2,1)S(1)} %add_convert_fusion.14), channel_id=1, source_target_pairs={{0,16},{4,20},{8,24},{12,28},{16,0},{20,4},{24,8},{28,12},{1,17},{... | collective-permute-start | bytes 589832 | tf_op jit(solution)/shard_map/ppermute | solution.py:320
  221.9 19.7 %collective-permute-start.33 = (bf16[256,512]{1,0:T(8,128)(2,1)S(1)}, bf16[256,512]{1,0:T(8,128)(2,1)S(1)}, u32[]{:S(2)}, u32[]{:S(2)}) collective-permute-start(bf16[256,512]{1,0:T(8,128)(2,1)S(1)} %add_convert_fusion.11), channel_id=1, source_target_pairs={{0,8},{4,12},{8,0},{12,4},{16,24},{20,28},{24,16},{28,20},{1,9},{5... | collective-permute-start | bytes 786440 | tf_op jit(solution)/shard_map/ppermute | solution.py:320
  227.6 22.9 %collective-permute-start.40 = (bf16[384,1024]{1,0:T(8,128)(2,1)S(1)}, bf16[384,1024]{1,0:T(8,128)(2,1)S(1)}, u32[]{:S(2)}, u32[]{:S(2)}) collective-permute-start(bf16[384,1024]{1,0:T(8,128)(2,1)S(1)} %pad_maximum_fusion.22), channel_id=1, source_target_pairs={{0,4},{4,0},{8,12},{12,8},{16,20},{20,16},{24,28},{28,24},{1,5},{5... | collective-permute-start | bytes 2359304 | tf_op jit(solution)/shard_map/ppermute | solution.py:320
  238.9 10.6 %collective-permute-start.32 = (bf16[64,1024]{1,0:T(8,128)(2,1)S(1)}, bf16[64,1024]{1,0:T(8,128)(2,1)S(1)}, u32[]{:S(2)}, u32[]{:S(2)}) collective-permute-start(bf16[64,1024]{1,0:T(8,128)(2,1)S(1)} %add_convert_fusion.24), channel_id=1, source_target_pairs={{0,16},{4,20},{8,24},{12,28},{16,0},{20,4},{24,8},{28,12},{1,17},{... | collective-permute-start | bytes 393224 | tf_op jit(solution)/shard_map/ppermute | solution.py:320
  238.9 16.6 %collective-permute-start.39 = (bf16[2,1,256,1024]{3,2,1,0:T(8,128)(2,1)S(1)}, bf16[2,1,256,1024]{3,2,1,0:T(8,128)(2,1)S(1)}, u32[]{:S(2)}, u32[]{:S(2)}) collective-permute-start(bf16[2,1,256,1024]{3,2,1,0:T(8,128)(2,1)S(1)} %constant_dynamic-slice_fusion.3), channel_id=1, source_target_pairs={{0,1},{1,0},{2,3},{3,2},{4,5},{5,4},{6,7},{7,6},{8,9},{9,8},{10,11... | collective-permute-start | bytes 3145736 | tf_op jit(solution)/shard_map/ppermute | solution.py:320
  241.7 14.8 %collective-permute-start.38 = (bf16[128,768]{1,0:T(8,128)(2,1)S(1)}, bf16[128,768]{1,0:T(8,128)(2,1)S(1)}, u32[]{:S(2)}, u32[]{:S(2)}) collective-permute-start(bf16[128,768]{1,0:T(8,128)(2,1)S(1)} %add_convert_fusion.13), channel_id=1, source_target_pairs={{0,4},{4,0},{8,12},{12,8},{16,20},{20,16},{24,28},{28,24},{1,5},{5... | collective-permute-start | bytes 589832 | tf_op jit(solution)/shard_map/ppermute | solution.py:320
  249.5 23.3 %collective-permute-start.37 = (bf16[256,512]{1,0:T(8,128)(2,1)S(1)}, bf16[256,512]{1,0:T(8,128)(2,1)S(1)}, u32[]{:S(2)}, u32[]{:S(2)}) collective-permute-start(bf16[256,512]{1,0:T(8,128)(2,1)S(1)} %add_convert_fusion.10), channel_id=1, source_target_pairs={{0,16},{4,20},{8,24},{12,28},{16,0},{20,4},{24,8},{28,12},{1,17},{... | collective-permute-start | bytes 786440 | tf_op jit(solution)/shard_map/ppermute | solution.py:320
  250.5 22.4 %collective-permute-start.43 = (bf16[256,768]{1,0:T(8,128)(2,1)S(1)}, bf16[256,768]{1,0:T(8,128)(2,1)S(1)}, u32[]{:S(2)}, u32[]{:S(2)}) collective-permute-start(bf16[256,768]{1,0:T(8,128)(2,1)S(1)} %pad_maximum_fusion.31), channel_id=1, source_target_pairs={{0,8},{4,12},{8,0},{12,4},{16,24},{20,28},{24,16},{28,20},{1,9},{5... | collective-permute-start | bytes 1179656 | tf_op jit(solution)/shard_map/ppermute | solution.py:320
  255.5 20.1 %collective-permute-start.42 = (bf16[128,512]{1,0:T(8,128)(2,1)S(1)}, bf16[128,512]{1,0:T(8,128)(2,1)S(1)}, u32[]{:S(2)}, u32[]{:S(2)}) collective-permute-start(bf16[128,512]{1,0:T(8,128)(2,1)S(1)} %add_convert_fusion.23), channel_id=1, source_target_pairs={{0,16},{4,20},{8,24},{12,28},{16,0},{20,4},{24,8},{28,12},{1,17},{... | collective-permute-start | bytes 393224 | tf_op jit(solution)/shard_map/ppermute | solution.py:320
  256.4 26.2 %collective-permute-start.36 = (bf16[64,1024]{1,0:T(8,128)(2,1)S(1)}, bf16[64,1024]{1,0:T(8,128)(2,1)S(1)}, u32[]{:S(2)}, u32[]{:S(2)}) collective-permute-start(bf16[64,1024]{1,0:T(8,128)(2,1)S(1)} %add_convert_fusion.22), channel_id=1, source_target_pairs={{0,16},{4,20},{8,24},{12,28},{16,0},{20,4},{24,8},{28,12},{1,17},{... | collective-permute-start | bytes 393224 | tf_op jit(solution)/shard_map/ppermute | solution.py:320
  272.8 17.4 %collective-permute-start.47 = (bf16[256,768]{1,0:T(8,128)(2,1)S(1)}, bf16[256,768]{1,0:T(8,128)(2,1)S(1)}, u32[]{:S(2)}, u32[]{:S(2)}) collective-permute-start(bf16[256,768]{1,0:T(8,128)(2,1)S(1)} %pad_maximum_fusion.32), channel_id=1, source_target_pairs={{0,16},{4,20},{8,24},{12,28},{16,0},{20,4},{24,8},{28,12},{1,17},{... | collective-permute-start | bytes 1179656 | tf_op jit(solution)/shard_map/ppermute | solution.py:320
  272.9 5.6 %collective-permute-start.41 = (bf16[128,512]{1,0:T(8,128)(2,1)S(1)}, bf16[128,512]{1,0:T(8,128)(2,1)S(1)}, u32[]{:S(2)}, u32[]{:S(2)}) collective-permute-start(bf16[128,512]{1,0:T(8,128)(2,1)S(1)} %add_convert_fusion.21), channel_id=1, source_target_pairs={{0,4},{4,0},{8,12},{12,8},{16,20},{20,16},{24,28},{28,24},{1,5},{5... | collective-permute-start | bytes 393224 | tf_op jit(solution)/shard_map/ppermute | solution.py:320
  275.6 18.6 %collective-permute-start.44 = (bf16[256,1024]{1,0:T(8,128)(2,1)S(1)}, bf16[256,1024]{1,0:T(8,128)(2,1)S(1)}, u32[]{:S(2)}, u32[]{:S(2)}) collective-permute-start(bf16[256,1024]{1,0:T(8,128)(2,1)S(1)} %fusion.23), channel_id=1, source_target_pairs={{0,2},{1,3},{2,0},{3,1},{4,6},{5,7},{6,4},{7,5},{8,10},{9,11},{10,... | collective-permute-start | bytes 1572872 | tf_op jit(solution)/shard_map/ppermute | solution.py:320
  278.5 41.7 %collective-permute-start.48 = (bf16[512,768]{1,0:T(8,128)(2,1)S(1)}, bf16[512,768]{1,0:T(8,128)(2,1)S(1)}, u32[]{:S(2)}, u32[]{:S(2)}) collective-permute-start(bf16[512,768]{1,0:T(8,128)(2,1)S(1)} %pad_maximum_fusion.23), channel_id=1, source_target_pairs={{0,4},{4,0},{8,12},{12,8},{16,20},{20,16},{24,28},{28,24},{1,5},{5... | collective-permute-start | bytes 2359304 | tf_op jit(solution)/shard_map/ppermute | solution.py:320
  282.6 21.5 %collective-permute-start.53 = (bf16[128,512]{1,0:T(8,128)(2,1)S(1)}, bf16[128,512]{1,0:T(8,128)(2,1)S(1)}, u32[]{:S(2)}, u32[]{:S(2)}) collective-permute-start(bf16[128,512]{1,0:T(8,128)(2,1)S(1)} %add_convert_fusion.20), channel_id=1, source_target_pairs={{0,16},{4,20},{8,24},{12,28},{16,0},{20,4},{24,8},{28,12},{1,17},{... | collective-permute-start | bytes 393224 | tf_op jit(solution)/shard_map/ppermute | solution.py:320
  282.7 9.2 %collective-permute-start.46 = (bf16[128,512]{1,0:T(8,128)(2,1)S(1)}, bf16[128,512]{1,0:T(8,128)(2,1)S(1)}, u32[]{:S(2)}, u32[]{:S(2)}) collective-permute-start(bf16[128,512]{1,0:T(8,128)(2,1)S(1)} %add_convert_fusion.19), channel_id=1, source_target_pairs={{0,4},{4,0},{8,12},{12,8},{16,20},{20,16},{24,28},{28,24},{1,5},{5... | collective-permute-start | bytes 393224 | tf_op jit(solution)/shard_map/ppermute | solution.py:320
  290.2 11.7 %collective-permute-start.49 = (bf16[128,1024]{1,0:T(8,128)(2,1)S(1)}, bf16[128,1024]{1,0:T(8,128)(2,1)S(1)}, u32[]{:S(2)}, u32[]{:S(2)}) collective-permute-start(bf16[128,1024]{1,0:T(8,128)(2,1)S(1)} %pad_maximum_fusion.33), channel_id=1, source_target_pairs={{0,8},{4,12},{8,0},{12,4},{16,24},{20,28},{24,16},{28,20},{1,9},{5... | collective-permute-start | bytes 786440 | tf_op jit(solution)/shard_map/ppermute | solution.py:320
  291.9 50.2 %collective-permute-start.56 = (bf16[512,768]{1,0:T(8,128)(2,1)S(1)}, bf16[512,768]{1,0:T(8,128)(2,1)S(1)}, u32[]{:S(2)}, u32[]{:S(2)}) collective-permute-start(bf16[512,768]{1,0:T(8,128)(2,1)S(1)} %pad_maximum_fusion.24), channel_id=1, source_target_pairs={{0,8},{4,12},{8,0},{12,4},{16,24},{20,28},{24,16},{28,20},{1,9},{5... | collective-permute-start | bytes 2359304 | tf_op jit(solution)/shard_map/ppermute | solution.py:320
  294.2 22.3 %collective-permute-start.51 = (bf16[256,512]{1,0:T(8,128)(2,1)S(1)}, bf16[256,512]{1,0:T(8,128)(2,1)S(1)}, u32[]{:S(2)}, u32[]{:S(2)}) collective-permute-start(bf16[256,512]{1,0:T(8,128)(2,1)S(1)} %pad_maximum_fusion.34), channel_id=1, source_target_pairs={{0,16},{4,20},{8,24},{12,28},{16,0},{20,4},{24,8},{28,12},{1,17},{... | collective-permute-start | bytes 786440 | tf_op jit(solution)/shard_map/ppermute | solution.py:320
  301.9 1.5 collective-permute-start.45
  303.4 36.9 %collective-permute-start.52 = (bf16[256,1024]{1,0:T(8,128)(2,1)S(1)}, bf16[256,1024]{1,0:T(8,128)(2,1)S(1)}, u32[]{:S(2)}, u32[]{:S(2)}) collective-permute-start(bf16[256,1024]{1,0:T(8,128)(2,1)S(1)} %pad_maximum_fusion.27), channel_id=1, source_target_pairs={{0,4},{4,0},{8,12},{12,8},{16,20},{20,16},{24,28},{28,24},{1,5},{5... | collective-permute-start | bytes 1572872 | tf_op jit(solution)/shard_map/ppermute | solution.py:320
  304.1 16.0 %collective-permute-start.50 = (f32[2304]{0:T(1024)S(1)}, f32[2304]{0:T(1024)S(1)}, u32[]{:S(2)}, u32[]{:S(2)}) collective-permute-start(f32[2304]{0:T(1024)S(1)} %fusion.31), channel_id=1, source_target_pairs={{0,2},{1,3},{2,0},{3,1},{4,6},{5,7},{6,4},{7,5},{8,10},{9,11},{10,... | collective-permute-start | bytes 27656 | tf_op jit(solution)/shard_map/ppermute | solution.py:320
  316.5 10.6 %collective-permute-start.55 = (bf16[256,512]{1,0:T(8,128)(2,1)S(1)}, bf16[256,512]{1,0:T(8,128)(2,1)S(1)}, u32[]{:S(2)}, u32[]{:S(2)}) collective-permute-start(bf16[256,512]{1,0:T(8,128)(2,1)S(1)} %pad_maximum_fusion.35), channel_id=1, source_target_pairs={{0,8},{4,12},{8,0},{12,4},{16,24},{20,28},{24,16},{28,20},{1,9},{5... | collective-permute-start | bytes 786440 | tf_op jit(solution)/shard_map/ppermute | solution.py:320
  320.1 22.3 %collective-permute-start.59 = (bf16[512,512]{1,0:T(8,128)(2,1)S(1)}, bf16[512,512]{1,0:T(8,128)(2,1)S(1)}, u32[]{:S(2)}, u32[]{:S(2)}) collective-permute-start(bf16[512,512]{1,0:T(8,128)(2,1)S(1)} %pad_maximum_fusion.28), channel_id=1, source_target_pairs={{0,8},{4,12},{8,0},{12,4},{16,24},{20,28},{24,16},{28,20},{1,9},{5... | collective-permute-start | bytes 1572872 | tf_op jit(solution)/shard_map/ppermute | solution.py:320
  320.2 7.1 %collective-permute-start.54 = (f32[2304]{0:T(1024)S(1)}, f32[2304]{0:T(1024)S(1)}, u32[]{:S(2)}, u32[]{:S(2)}) collective-permute-start(f32[2304]{0:T(1024)S(1)} %add.585), channel_id=1, source_target_pairs={{0,4},{4,0},{8,12},{12,8},{16,20},{20,16},{24,28},{28,24},{1,5},{5... | collective-permute-start | bytes 27656 | tf_op jit(solution)/shard_map/ppermute | solution.py:320
  327.3 7.3 %collective-permute-start.57 = (f32[2304]{0:T(1024)S(1)}, f32[2304]{0:T(1024)S(1)}, u32[]{:S(2)}, u32[]{:S(2)}) collective-permute-start(f32[2304]{0:T(1024)S(1)} %add.586), channel_id=1, source_target_pairs={{0,8},{4,12},{8,0},{12,4},{16,24},{20,28},{24,16},{28,20},{1,9},{5... | collective-permute-start | bytes 27656 | tf_op jit(solution)/shard_map/ppermute | solution.py:320
  334.6 4.6 %collective-permute-start.60 = (f32[2304]{0:T(1024)S(1)}, f32[2304]{0:T(1024)S(1)}, u32[]{:S(2)}, u32[]{:S(2)}) collective-permute-start(f32[2304]{0:T(1024)S(1)} %add.587), channel_id=1, source_target_pairs={{0,16},{4,20},{8,24},{12,28},{16,0},{20,4},{24,8},{28,12},{1,17},{... | collective-permute-start | bytes 27656 | tf_op jit(solution)/shard_map/ppermute | solution.py:320
  336.6 12.0 %collective-permute-start.58 = (bf16[512,512]{1,0:T(8,128)(2,1)S(1)}, bf16[512,512]{1,0:T(8,128)(2,1)S(1)}, u32[]{:S(2)}, u32[]{:S(2)}) collective-permute-start(bf16[512,512]{1,0:T(8,128)(2,1)S(1)} %pad_maximum_fusion.29), channel_id=1, source_target_pairs={{0,4},{4,0},{8,12},{12,8},{16,20},{20,16},{24,28},{28,24},{1,5},{5... | collective-permute-start | bytes 1572872 | tf_op jit(solution)/shard_map/ppermute | solution.py:320
  (54 other events, 301.1 us)

commit v4 on v3

--- a/solution.py
+++ b/solution.py
@@ -369,14 +369,14 @@
         if axis == "tensor" and bit == 0:
             us = size / 400e3
         else:
-            us = 2 * size / 87e3 * (2 if axis == "dp" and bit > 1 else 1)
+            us = 2 * size / 75e3 * (2 if axis == "dp" and bit > 1 else 1)
         values = self.gate(values)
         received = swap(values, axis, bit)
         self.token = values
         self.clock += 1.6
         start = max(self.clock, self.free.get((axis, bit), 0.0))
         self.free[axis, bit] = start + us
-        return Flight(received, start + us + 1.0)
+        return Flight(received, start + us + 2.0)
 
     def fill(self, until):
         while True:
@@ -651,7 +651,7 @@
     grad_mixed = grad_out + grad_mixed_norm
     order.clock += 2.0
     gather_branch = Spread(order, grad_mixed.astype(jnp.bfloat16))
-    grad_w_up = DpSum(order, up_grad, 1)
+    grad_w_up = DpSum(order, up_grad, 0)
     settle_out = SettlePieces(
         order, 1.5, lambda rows: matmul(rows[0], w_down, 1, 0), near_far, mine_across
     )

time: 360 us -> 337 us (0.936)
  waiting for transfers between devices: 148 us -> 115 us
  starting transfers between devices: 48.6 us -> 54.2 us
    ppermute x61, waiting for transfers between devices: 148 us -> 115 us  [swap(): return lax.ppermute(values, axis, [(i, i ^ 1 << bit) for i in range(size)])]
    ppermute x61, starting transfers between devices: 48.6 us -> 54.2 us  [swap(): return lax.ppermute(values, axis, [(i, i ^ 1 << bit) for i in range(size)])]
    unnamed x110 -> x116, local copies, waits for them, and re-layouts: 7.06 us -> 9.71 us
  transfers between devices with their start and end apart: 61 -> 61, of which waited for: 27 -> 22; matrix products, arithmetic and copies ran while one was open for 25% -> 27% of each run, Pallas kernels for 12% -> 13%
where the time goes in v4:
time: 337 us; the launch traced here: 332 us
  waiting for transfers between devices  115 us (34%)
  other arithmetic  58.1 us (17%)
  starting transfers between devices  54.2 us (16%)
  Pallas kernels  42 us (12%)
  matrix products  39.2 us (12%)
  local copies, waits for them, and re-layouts  19.9 us (6%)
    ppermute x61, waiting for transfers between devices, swap(): return lax.ppermute(values, axis, [(i, i ^ 1 << bit) for i in range(size)])  115 us
    ppermute x61, starting transfers between devices, swap(): return lax.ppermute(values, axis, [(i, i ^ 1 << bit) for i in range(size)])  54.2 us
    dot_general x21, matrix products, dot(): lax.dot_general(left, right, (((left_dim,), (right_dim,)), ((), ())), pre...  39.2 us
    pallas_call x2, Pallas kernels, attend_back(): pl.pallas_call(attend_back_kernel, grid_spec=pltpu.PrefetchScalarGridSpec...  22 us
    convert_element_type x18, other arithmetic, total(): return sum(parts[1:], parts[0]).astype(jnp.bfloat16)  17.1 us
    unnamed x116, local copies, waits for them, and re-layouts  9.71 us
    pallas_call x1, Pallas kernels, project_heads(): pl.pallas_call(heads_kernel, grid_spec=pltpu.PrefetchScalarGridSpec(num_s...  8.84 us
    pallas_call x1, Pallas kernels, attend(): pl.pallas_call(attend_kernel, grid_spec=pltpu.PrefetchScalarGridSpec(num_...  8.18 us
  transfers between devices with their start and end apart: 61, of which 22 were waited for; matrix products, arithmetic and copies ran while one was open for 27% of the time, Pallas kernels for 13%

profile of v4, /device:TPU:0, one launch (start us, length us, event | category | flops | bytes accessed | tf_op | source)
XLA Modules:
  0.0 331.8 jit_solution(9117750726888992864)
XLA Ops:
  3.9 3.0 collective-permute-start.1
  7.7 11.2 %collective-permute-done.1.across_ref = bf16[256,1024]{1,0:T(8,128)(2,1)} collective-permute-done((bf16[256,1024]{1,0:T(8,128)(2,1)S(1)}, bf16[256,1024]{1,0:T(8,128)(2,1)}, u32[]{:S(2)}, u32[]{:S(2)}) %collective-permute-start.1) | collective-permute-done | bytes 524320 | tf_op jit(solution)/shard_map/ppermute | solution.py:320
  18.9 1.7 collective-permute-start.3
  21.2 2.0 fusion.26
  25.3 8.8 %project_heads.1 = (bf16[1024,1024]{1,0:T(8,128)(2,1)}, f32[1024,512]{1,0:T(8,128)}, f32[1024,256]{1,0:T(8,128)}, bf16[1024,512]{1,0:T(8,128)(2,1)}, bf16[1024,2...) custom-call(s32[4]{0:T(128)} %xor_add_fusion.place_ref, bf16[256,1024]{1,0:T(8,128)(2,1)} %copy-done.12, ...), custom_call_target="tpu_custom_call" | custom-call | tf_op jit(solution)/shard_map/project_heads/pallas_call | solution.py:91
  34.1 8.2 %attend.1.attended_ref = bf16[1024,512]{1,0:T(8,128)(2,1)} custom-call(s32[1]{0:T(128)} %copy.27.length_ref, bf16[1024,512]{1,0:T(8,128)(2,1)} %get-tuple-element.199.query_ref, bf16[1024,256]{1,0:T(8,128)(2,1)} %get-tuple-element.200.key_ref, bf16[1024,256]{1,0:T(8,128)(2,1)} %get-tuple-element.201.value_ref), custom_call_target="tpu_custom_call" | custom-call | tf_op jit(solution)/shard_map/attend/pallas_call | solution.py:158
  42.3 2.5 convolution_convert_fusion
  47.9 3.6 %collective-permute-done.6 = bf16[256,1024]{1,0:T(8,128)(2,1)} collective-permute-done((bf16[256,1024]{1,0:T(8,128)(2,1)S(1)}, bf16[256,1024]{1,0:T(8,128)(2,1)}, u32[]{:S(2)}, u32[]{:S(2)}) %collective-permute-start.6) | collective-permute-done | bytes 524320 | tf_op jit(solution)/shard_map/ppermute | solution.py:320
  51.5 1.6 convert_add_fusion.1
  53.5 1.7 pad_maximum_fusion
  55.2 3.0 convolution_convert_fusion.4
  58.2 9.1 %collective-permute-done.5 = bf16[256,1024]{1,0:T(8,128)(2,1)S(1)} collective-permute-done((bf16[256,1024]{1,0:T(8,128)(2,1)S(1)}, bf16[256,1024]{1,0:T(8,128)(2,1)S(1)}, u32[]{:S(2)}, u32[]{:S(2)}) %collective-permute-start.5) | collective-permute-done | bytes 524320 | tf_op jit(solution)/shard_map/ppermute | solution.py:320
  73.1 1.8 add_convert_fusion.4
  74.9 9.8 %collective-permute-done.9 = bf16[256,1024]{1,0:T(8,128)(2,1)S(1)} collective-permute-done((bf16[256,1024]{1,0:T(8,128)(2,1)}, bf16[256,1024]{1,0:T(8,128)(2,1)S(1)}, u32[]{:S(2)}, u32[]{:S(2)}) %collective-permute-start.9) | collective-permute-done | bytes 524320 | tf_op jit(solution)/shard_map/ppermute | solution.py:320
  84.9 1.7 collective-permute-done.10
  87.6 1.8 add_convert_fusion.3
  94.0 2.0 convolution_convert_fusion.1
  96.1 1.6 collective-permute-start.13
  102.0 1.9 convolution_convert_fusion.3
  104.3 1.9 convolution_convert_fusion.2
  106.2 10.3 %collective-permute-done.13 = bf16[384,1024]{1,0:T(8,128)(2,1)S(1)} collective-permute-done((bf16[384,1024]{1,0:T(8,128)(2,1)S(1)}, bf16[384,1024]{1,0:T(8,128)(2,1)S(1)}, u32[]{:S(2)}, u32[]{:S(2)}) %collective-permute-start.13) | collective-permute-done | bytes 786464 | tf_op jit(solution)/shard_map/ppermute | solution.py:320
  116.7 1.6 collective-permute-start.18
  122.3 2.0 convolution_convert_fusion.6
  124.8 2.0 convolution_convert_fusion.5
  127.5 5.3 %collective-permute-done.17 = bf16[512,768]{1,0:T(8,128)(2,1)S(1)} collective-permute-done((bf16[512,768]{1,0:T(8,128)(2,1)S(1)}, bf16[512,768]{1,0:T(8,128)(2,1)S(1)}, u32[]{:S(2)}, u32[]{:S(2)}) %collective-permute-start.17) | collective-permute-done | bytes 786464 | tf_op jit(solution)/shard_map/ppermute | solution.py:320
  136.5 2.6 collective-permute-start.22
  141.8 3.0 join.1
  144.7 4.2 %convolution_convert_fusion.10.grad_ref = bf16[1024,512]{1,0:T(8,128)(2,1)} fusion(bf16[1024,1024]{1,0:T(8,128)(2,1)} %join.1, bf16[512,1024]{1,0:T(8,128)(2,1)} %param.23), kind=kOutput, calls=%fused_computation.45 | convolution fusion | flops 1074266112 | bytes 4194304 | tf_op jit(solution)/shard_map/dot_general | solution.py:46
  149.0 2.2 add_convert_fusion.5
  153.0 2.5 collective-permute-done.21
  161.0 10.8 %attend_back.2 = (bf16[1024,512]{1,0:T(8,128)(2,1)}, f32[1,128]{1,0:T(1,128)}, f32[1,128]{1,0:T(1,128)}) custom-call(s32[1]{0:T(128)} %copy.27.length_ref, bf16[1024,512]{1,0:T(8,128)(2,1)} %get-tuple-element.199.query_ref, bf16[1024,256]{1,0:T(8,128)(2,1)} %get-tuple-element.200.key_ref, bf16[1024,256]{1,0:T(8,128)(2,1)} %get-tuple-element.201.value_ref, ...), custom_call_target="tpu_custom_call" | custom-call | tf_op jit(solution)/shard_map/attend_back/pallas_call | solution.py:242
  171.7 3.1 convolution_convert_fusion.8
  177.3 2.0 add_convert_fusion.7
  183.7 1.7 add_convert_fusion.12
  186.7 2.9 collective-permute-start.32
  189.6 11.2 %attend_back.3 = (bf16[1024,512]{1,0:T(8,128)(2,1)}, f32[1,128]{1,0:T(1,128)}, f32[1,128]{1,0:T(1,128)}) custom-call(s32[1]{0:T(128)} %copy.27.length_ref, bf16[1024,512]{1,0:T(8,128)(2,1)} %get-tuple-element.199.query_ref, bf16[1024,256]{1,0:T(8,128)(2,1)} %get-tuple-element.200.key_ref, bf16[1024,256]{1,0:T(8,128)(2,1)} %get-tuple-element.201.value_ref, ...), custom_call_target="tpu_custom_call" | custom-call | tf_op jit(solution)/shard_map/attend_back/pallas_call | solution.py:242
  200.8 3.2 convolution_convert_fusion.7
  205.5 1.6 collective-permute-start.36
  210.2 6.4 %collective-permute-done.30 = bf16[128,1024]{1,0:T(8,128)(2,1)S(1)} collective-permute-done((bf16[128,1024]{1,0:T(8,128)(2,1)}, bf16[128,1024]{1,0:T(8,128)(2,1)S(1)}, u32[]{:S(2)}, u32[]{:S(2)}) %collective-permute-start.30) | collective-permute-done | bytes 262176 | tf_op jit(solution)/shard_map/ppermute | solution.py:320
  223.6 5.4 %collective-permute-done.35 = bf16[512,512]{1,0:T(8,128)(2,1)S(1)} collective-permute-done((bf16[512,512]{1,0:T(8,128)(2,1)S(1)}, bf16[512,512]{1,0:T(8,128)(2,1)S(1)}, u32[]{:S(2)}, u32[]{:S(2)}) %collective-permute-start.35) | collective-permute-done | bytes 524320 | tf_op jit(solution)/shard_map/ppermute | solution.py:320
  229.1 6.5 %collective-permute-done.34 = bf16[64,1024]{1,0:T(8,128)(2,1)S(1)} collective-permute-done((bf16[64,1024]{1,0:T(8,128)(2,1)S(1)}, bf16[64,1024]{1,0:T(8,128)(2,1)S(1)}, u32[]{:S(2)}, u32[]{:S(2)}) %collective-permute-start.34) | collective-permute-done | bytes 131104 | tf_op jit(solution)/shard_map/ppermute | solution.py:320
  235.6 1.8 collective-permute-start.39
  238.3 3.4 %collective-permute-start.40 = (bf16[128,768]{1,0:T(8,128)(2,1)S(1)}, bf16[128,768]{1,0:T(8,128)(2,1)S(1)}, u32[]{:S(2)}, u32[]{:S(2)}) collective-permute-start(bf16[128,768]{1,0:T(8,128)(2,1)S(1)} %add_convert_fusion.13), channel_id=1, source_target_pairs={{0,16},{4,20},{8,24},{12,28},{16,0},{20,4},{24,8},{28,12},{1,17},{... | collective-permute-start | bytes 589832 | tf_op jit(solution)/shard_map/ppermute | solution.py:320
  242.5 2.6 collective-permute-done.29
  247.9 10.5 %collective-permute-done.40 = bf16[128,768]{1,0:T(8,128)(2,1)S(1)} collective-permute-done((bf16[128,768]{1,0:T(8,128)(2,1)S(1)}, bf16[128,768]{1,0:T(8,128)(2,1)S(1)}, u32[]{:S(2)}, u32[]{:S(2)}) %collective-permute-start.40) | collective-permute-done | bytes 196640 | tf_op jit(solution)/shard_map/ppermute | solution.py:320
  258.5 1.5 collective-permute-start.37
  260.6 2.1 fusion.37
  262.7 2.4 add_select_fusion
  265.1 2.5 collective-permute-done.37
  268.5 2.9 collective-permute-done.43
  275.4 1.5 collective-permute-start.45
  277.9 2.0 collective-permute-start.47
  280.2 3.6 %collective-permute-done.49 = bf16[128,1024]{1,0:T(8,128)(2,1)S(1)} collective-permute-done((bf16[128,1024]{1,0:T(8,128)(2,1)S(1)}, bf16[128,1024]{1,0:T(8,128)(2,1)S(1)}, u32[]{:S(2)}, u32[]{:S(2)}) %collective-permute-start.49) | collective-permute-done | bytes 262176 | tf_op jit(solution)/shard_map/ppermute | solution.py:320
  284.8 1.6 collective-permute-done.47
  286.5 1.6 collective-permute-start.51
  288.1 6.4 %collective-permute-done.52 = bf16[128,512]{1,0:T(8,128)(2,1)S(1)} collective-permute-done((bf16[128,512]{1,0:T(8,128)(2,1)S(1)}, bf16[128,512]{1,0:T(8,128)(2,1)S(1)}, u32[]{:S(2)}, u32[]{:S(2)}) %collective-permute-start.52) | collective-permute-done | bytes 131104 | tf_op jit(solution)/shard_map/ppermute | solution.py:320
  294.6 2.5 collective-permute-start.57
  297.1 1.9 fusion.36
  300.7 8.1 %collective-permute-done.57 = bf16[256,512]{1,0:T(8,128)(2,1)S(1)} collective-permute-done((bf16[256,512]{1,0:T(8,128)(2,1)S(1)}, bf16[256,512]{1,0:T(8,128)(2,1)S(1)}, u32[]{:S(2)}, u32[]{:S(2)}) %collective-permute-start.57) | collective-permute-done | bytes 262176 | tf_op jit(solution)/shard_map/ppermute | solution.py:320
  309.9 3.8 %collective-permute-start.60 = (bf16[512,512]{1,0:T(8,128)(2,1)S(1)}, bf16[512,512]{1,0:T(8,128)(2,1)S(1)}, u32[]{:S(2)}, u32[]{:S(2)}) collective-permute-start(bf16[512,512]{1,0:T(8,128)(2,1)S(1)} %pad_maximum_fusion.29), channel_id=1, source_target_pairs={{0,8},{4,12},{8,0},{12,4},{16,24},{20,28},{24,16},{28,20},{1,9},{5... | collective-permute-start | bytes 1572872 | tf_op jit(solution)/shard_map/ppermute | solution.py:320
  315.1 1.6 fusion.34
  317.0 1.9 fusion.35
  318.9 4.5 %collective-permute-done.58 = bf16[512,512]{1,0:T(8,128)(2,1)S(1)} collective-permute-done((bf16[512,512]{1,0:T(8,128)(2,1)S(1)}, bf16[512,512]{1,0:T(8,128)(2,1)S(1)}, u32[]{:S(2)}, u32[]{:S(2)}) %collective-permute-start.58) | collective-permute-done | bytes 524320 | tf_op jit(solution)/shard_map/ppermute | solution.py:320
  329.9 1.6 pad_maximum_fusion.2
  (328 shorter events, 87.3 us)
Async XLA Ops:
  0.6 72.4 %copy-start = (bf16[1024,768]{1,0:T(8,128)(2,1)S(1)}, bf16[1024,768]{1,0:T(8,128)(2,1)}, u32[]{:S(2)}) copy-start(bf16[1024,768]{1,0:T(8,128)(2,1)} %param.24) | copy-start | bytes 4718596
  3.9 15.0 %collective-permute-start.1 = (bf16[256,1024]{1,0:T(8,128)(2,1)S(1)}, bf16[256,1024]{1,0:T(8,128)(2,1)}, u32[]{:S(2)}, u32[]{:S(2)}) collective-permute-start(bf16[256,1024]{1,0:T(8,128)(2,1)S(1)} %fusion.4.mine_ref), channel_id=1, source_target_pairs={{0,2},{1,3},{2,0},{3,1},{4,6},{5,7},{6,4},{7,5},{8,10},{9,11},{10,... | collective-permute-start | bytes 1572872 | tf_op jit(solution)/shard_map/ppermute | solution.py:320
  6.9 17.6 %collective-permute-start = (bf16[256,1024]{1,0:T(8,128)(2,1)S(1)}, bf16[256,1024]{1,0:T(8,128)(2,1)}, u32[]{:S(2)}, u32[]{:S(2)}) collective-permute-start(bf16[256,1024]{1,0:T(8,128)(2,1)S(1)} %fusion.4.mine_ref), channel_id=1, source_target_pairs={{0,1},{1,0},{2,3},{3,2},{4,5},{5,4},{6,7},{7,6},{8,9},{9,8},{10,11... | collective-permute-start | bytes 1572872 | tf_op jit(solution)/shard_map/ppermute | solution.py:320
  18.9 5.6 %collective-permute-start.2 = (bf16[256,1024]{1,0:T(8,128)(2,1)}, bf16[256,1024]{1,0:T(8,128)(2,1)S(1)}, u32[]{:S(2)}, u32[]{:S(2)}) collective-permute-start(bf16[256,1024]{1,0:T(8,128)(2,1)} %collective-permute-done.1.across_ref), channel_id=1, source_target_pairs={{0,1},{1,0},{2,3},{3,2},{4,5},{5,4},{6,7},{7,6},{8,9},{9,8},{10,11... | collective-permute-start | bytes 1572872 | tf_op jit(solution)/shard_map/ppermute | solution.py:320
  18.9 23.4 %collective-permute-start.3 = (bf16[256,1024]{1,0:T(8,128)(2,1)S(1)}, bf16[256,1024]{1,0:T(8,128)(2,1)}, u32[]{:S(2)}, u32[]{:S(2)}) collective-permute-start(bf16[256,1024]{1,0:T(8,128)(2,1)S(1)} %fusion.21), channel_id=1, source_target_pairs={{0,2},{1,3},{2,0},{3,1},{4,6},{5,7},{6,4},{7,5},{8,10},{9,11},{10,... | collective-permute-start | bytes 1572872 | tf_op jit(solution)/shard_map/ppermute | solution.py:320
  47.2 4.3 %collective-permute-start.4 = (bf16[2,1,256,1024]{3,2,1,0:T(8,128)(2,1)}, bf16[2,1,256,1024]{3,2,1,0:T(8,128)(2,1)S(1)}, u32[]{:S(2)}, u32[]{:S(2)}) collective-permute-start(bf16[2,1,256,1024]{3,2,1,0:T(8,128)(2,1)} %constant_dynamic-slice_fusion.7), channel_id=1, source_target_pairs={{0,1},{1,0},{2,3},{3,2},{4,5},{5,4},{6,7},{7,6},{8,9},{9,8},{10,11... | collective-permute-start | bytes 3145736 | tf_op jit(solution)/shard_map/ppermute | solution.py:320
  47.4 4.1 %collective-permute-start.6 = (bf16[256,1024]{1,0:T(8,128)(2,1)S(1)}, bf16[256,1024]{1,0:T(8,128)(2,1)}, u32[]{:S(2)}, u32[]{:S(2)}) collective-permute-start(bf16[256,1024]{1,0:T(8,128)(2,1)S(1)} %fusion.21), channel_id=1, source_target_pairs={{0,1},{1,0},{2,3},{3,2},{4,5},{5,4},{6,7},{7,6},{8,9},{9,8},{10,11... | collective-permute-start | bytes 1572872 | tf_op jit(solution)/shard_map/ppermute | solution.py:320
  47.7 5.8 %collective-permute-start.7 = (bf16[256,1024]{1,0:T(8,128)(2,1)}, bf16[256,1024]{1,0:T(8,128)(2,1)}, u32[]{:S(2)}, u32[]{:S(2)}) collective-permute-start(bf16[256,1024]{1,0:T(8,128)(2,1)} %collective-permute-done.3), channel_id=1, source_target_pairs={{0,1},{1,0},{2,3},{3,2},{4,5},{5,4},{6,7},{7,6},{8,9},{9,8},{10,11... | collective-permute-start | bytes 1572872 | tf_op jit(solution)/shard_map/ppermute | solution.py:320
  53.2 14.1 %collective-permute-start.5 = (bf16[256,1024]{1,0:T(8,128)(2,1)S(1)}, bf16[256,1024]{1,0:T(8,128)(2,1)S(1)}, u32[]{:S(2)}, u32[]{:S(2)}) collective-permute-start(bf16[256,1024]{1,0:T(8,128)(2,1)S(1)} %fusion.22), channel_id=1, source_target_pairs={{0,2},{1,3},{2,0},{3,1},{4,6},{5,7},{6,4},{7,5},{8,10},{9,11},{10,... | collective-permute-start | bytes 1572872 | tf_op jit(solution)/shard_map/ppermute | solution.py:320
  68.6 2.3 collective-permute-start.8
  70.1 14.6 %collective-permute-start.9 = (bf16[256,1024]{1,0:T(8,128)(2,1)}, bf16[256,1024]{1,0:T(8,128)(2,1)S(1)}, u32[]{:S(2)}, u32[]{:S(2)}) collective-permute-start(bf16[256,1024]{1,0:T(8,128)(2,1)} %multiply_convert_fusion.2), channel_id=1, source_target_pairs={{0,2},{1,3},{2,0},{3,1},{4,6},{5,7},{6,4},{7,5},{8,10},{9,11},{10,... | collective-permute-start | bytes 1572872 | tf_op jit(solution)/shard_map/ppermute | solution.py:320
  84.7 1.9 collective-permute-start.10
  92.1 9.1 %collective-permute-start.11 = (bf16[512,1024]{1,0:T(8,128)(2,1)S(1)}, bf16[512,1024]{1,0:T(8,128)(2,1)S(1)}, u32[]{:S(2)}, u32[]{:S(2)}) collective-permute-start(bf16[512,1024]{1,0:T(8,128)(2,1)S(1)} %add_convert_fusion.2), channel_id=1, source_target_pairs={{0,1},{1,0},{2,3},{3,2},{4,5},{5,4},{6,7},{7,6},{8,9},{9,8},{10,11... | collective-permute-start | bytes 3145736 | tf_op jit(solution)/shard_map/ppermute | solution.py:320
  96.0 30.7 %copy-start.22 = (bf16[768,1024]{1,0:T(8,128)(2,1)}, bf16[768,1024]{1,0:T(8,128)(2,1)S(1)}, u32[]{:S(2)}) copy-start(bf16[768,1024]{1,0:T(8,128)(2,1)S(1)} %convolution_convert_fusion.1) | copy-start | bytes 4718596
  96.1 20.4 %collective-permute-start.13 = (bf16[384,1024]{1,0:T(8,128)(2,1)S(1)}, bf16[384,1024]{1,0:T(8,128)(2,1)S(1)}, u32[]{:S(2)}, u32[]{:S(2)}) collective-permute-start(bf16[384,1024]{1,0:T(8,128)(2,1)S(1)} %constant_dynamic-slice_fusion.4), channel_id=1, source_target_pairs={{0,4},{4,0},{8,12},{12,8},{16,20},{20,16},{24,28},{28,24},{1,5},{5... | collective-permute-start | bytes 2359304 | tf_op jit(solution)/shard_map/ppermute | solution.py:320
  101.4 17.8 %collective-permute-start.12 = (bf16[256,1024]{1,0:T(8,128)(2,1)S(1)}, bf16[256,1024]{1,0:T(8,128)(2,1)S(1)}, u32[]{:S(2)}, u32[]{:S(2)}) collective-permute-start(bf16[256,1024]{1,0:T(8,128)(2,1)S(1)} %add_convert_fusion.6), channel_id=1, source_target_pairs={{0,2},{1,3},{2,0},{3,1},{4,6},{5,7},{6,4},{7,5},{8,10},{9,11},{10,... | collective-permute-start | bytes 1572872 | tf_op jit(solution)/shard_map/ppermute | solution.py:320
  103.9 28.9 %copy-start.21 = (bf16[1024,768]{1,0:T(8,128)(2,1)}, bf16[1024,768]{1,0:T(8,128)(2,1)S(1)}, u32[]{:S(2)}) copy-start(bf16[1024,768]{1,0:T(8,128)(2,1)S(1)} %convolution_convert_fusion.3) | copy-start | bytes 4718596
  104.0 28.8 %collective-permute-start.17 = (bf16[512,768]{1,0:T(8,128)(2,1)S(1)}, bf16[512,768]{1,0:T(8,128)(2,1)S(1)}, u32[]{:S(2)}, u32[]{:S(2)}) collective-permute-start(bf16[512,768]{1,0:T(8,128)(2,1)S(1)} %constant_dynamic-slice_fusion.6), channel_id=1, source_target_pairs={{0,4},{4,0},{8,12},{12,8},{16,20},{20,16},{24,28},{28,24},{1,5},{5... | collective-permute-start | bytes 2359304 | tf_op jit(solution)/shard_map/ppermute | solution.py:320
  116.7 10.1 %collective-permute-start.18 = (bf16[192,1024]{1,0:T(8,128)(2,1)S(1)}, bf16[192,1024]{1,0:T(8,128)(2,1)S(1)}, u32[]{:S(2)}, u32[]{:S(2)}) collective-permute-start(bf16[192,1024]{1,0:T(8,128)(2,1)S(1)} %add_convert_fusion.9), channel_id=1, source_target_pairs={{0,8},{4,12},{8,0},{12,4},{16,24},{20,28},{24,16},{28,20},{1,9},{5... | collective-permute-start | bytes 1179656 | tf_op jit(solution)/shard_map/ppermute | solution.py:320
  121.8 12.6 %collective-permute-start.16 = (bf16[256,1024]{1,0:T(8,128)(2,1)S(1)}, bf16[256,1024]{1,0:T(8,128)(2,1)S(1)}, u32[]{:S(2)}, u32[]{:S(2)}) collective-permute-start(bf16[256,1024]{1,0:T(8,128)(2,1)S(1)} %get-tuple-element.250.refs_0_), channel_id=1, source_target_pairs={{0,2},{1,3},{2,0},{3,1},{4,6},{5,7},{6,4},{7,5},{8,10},{9,11},{10,... | collective-permute-start | bytes 1572872 | tf_op jit(solution)/shard_map/ppermute | solution.py:320
  122.3 18.4 %collective-permute-start.15 = (bf16[256,1024]{1,0:T(8,128)(2,1)S(1)}, bf16[256,1024]{1,0:T(8,128)(2,1)S(1)}, u32[]{:S(2)}, u32[]{:S(2)}) collective-permute-start(bf16[256,1024]{1,0:T(8,128)(2,1)S(1)} %get-tuple-element.250.refs_0_), channel_id=1, source_target_pairs={{0,1},{1,0},{2,3},{3,2},{4,5},{5,4},{6,7},{7,6},{8,9},{9,8},{10,11... | collective-permute-start | bytes 1572872 | tf_op jit(solution)/shard_map/ppermute | solution.py:320
  124.3 24.7 %collective-permute-start.14 = (bf16[512,1024]{1,0:T(8,128)(2,1)}, bf16[512,1024]{1,0:T(8,128)(2,1)}, u32[]{:S(2)}, u32[]{:S(2)}) collective-permute-start(bf16[512,1024]{1,0:T(8,128)(2,1)} %convolution_convert_fusion.6), channel_id=1, source_target_pairs={{0,1},{1,0},{2,3},{3,2},{4,5},{5,4},{6,7},{7,6},{8,9},{9,8},{10,11... | collective-permute-start | bytes 3145736 | tf_op jit(solution)/shard_map/ppermute | solution.py:320
  134.3 7.4 %collective-permute-start.19 = (bf16[256,1024]{1,0:T(8,128)(2,1)S(1)}, bf16[256,1024]{1,0:T(8,128)(2,1)}, u32[]{:S(2)}, u32[]{:S(2)}) collective-permute-start(bf16[256,1024]{1,0:T(8,128)(2,1)S(1)} %collective-permute-done.16.refs_2_), channel_id=1, source_target_pairs={{0,1},{1,0},{2,3},{3,2},{4,5},{5,4},{6,7},{7,6},{8,9},{9,8},{10,11... | collective-permute-start | bytes 1572872 | tf_op jit(solution)/shard_map/ppermute | solution.py:320
  136.5 14.6 %collective-permute-start.22 = (bf16[96,1024]{1,0:T(8,128)(2,1)}, bf16[96,1024]{1,0:T(8,128)(2,1)}, u32[]{:S(2)}, u32[]{:S(2)}) collective-permute-start(bf16[96,1024]{1,0:T(8,128)(2,1)} %add_convert_fusion.18), channel_id=1, source_target_pairs={{0,16},{4,20},{8,24},{12,28},{16,0},{20,4},{24,8},{28,12},{1,17},{... | collective-permute-start | bytes 589832 | tf_op jit(solution)/shard_map/ppermute | solution.py:320
  139.1 36.6 %collective-permute-start.24 = (bf16[512,768]{1,0:T(8,128)(2,1)}, bf16[512,768]{1,0:T(8,128)(2,1)}, u32[]{:S(2)}, u32[]{:S(2)}) collective-permute-start(bf16[512,768]{1,0:T(8,128)(2,1)} %constant_dynamic-slice_fusion.5), channel_id=1, source_target_pairs={{0,4},{4,0},{8,12},{12,8},{16,20},{20,16},{24,28},{28,24},{1,5},{5... | collective-permute-start | bytes 2359304 | tf_op jit(solution)/shard_map/ppermute | solution.py:320
  140.7 14.8 %collective-permute-start.21 = (bf16[256,768]{1,0:T(8,128)(2,1)}, bf16[256,768]{1,0:T(8,128)(2,1)}, u32[]{:S(2)}, u32[]{:S(2)}) collective-permute-start(bf16[256,768]{1,0:T(8,128)(2,1)} %add_convert_fusion.8), channel_id=1, source_target_pairs={{0,8},{4,12},{8,0},{12,4},{16,24},{20,28},{24,16},{28,20},{1,9},{5... | collective-permute-start | bytes 1179656 | tf_op jit(solution)/shard_map/ppermute | solution.py:320
  152.6 26.7 %collective-permute-start.28 = (bf16[96,1024]{1,0:T(8,128)(2,1)S(1)}, bf16[96,1024]{1,0:T(8,128)(2,1)S(1)}, u32[]{:S(2)}, u32[]{:S(2)}) collective-permute-start(bf16[96,1024]{1,0:T(8,128)(2,1)S(1)} %add_convert_fusion.17), channel_id=1, source_target_pairs={{0,16},{4,20},{8,24},{12,28},{16,0},{20,4},{24,8},{28,12},{1,17},{... | collective-permute-start | bytes 589832 | tf_op jit(solution)/shard_map/ppermute | solution.py:320
  159.8 23.4 %collective-permute-start.27 = (bf16[256,1024]{1,0:T(8,128)(2,1)}, bf16[256,1024]{1,0:T(8,128)(2,1)}, u32[]{:S(2)}, u32[]{:S(2)}) collective-permute-start(bf16[256,1024]{1,0:T(8,128)(2,1)} %constant_dynamic-slice_fusion.3), channel_id=1, source_target_pairs={{0,4},{4,0},{8,12},{12,8},{16,20},{20,16},{24,28},{28,24},{1,5},{5... | collective-permute-start | bytes 1572872 | tf_op jit(solution)/shard_map/ppermute | solution.py:320
  160.3 25.1 %collective-permute-start.26 = (bf16[128,768]{1,0:T(8,128)(2,1)S(1)}, bf16[128,768]{1,0:T(8,128)(2,1)}, u32[]{:S(2)}, u32[]{:S(2)}) collective-permute-start(bf16[128,768]{1,0:T(8,128)(2,1)S(1)} %add_convert_fusion.16), channel_id=1, source_target_pairs={{0,16},{4,20},{8,24},{12,28},{16,0},{20,4},{24,8},{28,12},{1,17},{... | collective-permute-start | bytes 589832 | tf_op jit(solution)/shard_map/ppermute | solution.py:320
  160.4 86.0 %collective-permute-start.20 = (bf16[256,1024]{1,0:T(8,128)(2,1)}, bf16[256,1024]{1,0:T(8,128)(2,1)}, u32[]{:S(2)}, u32[]{:S(2)}) collective-permute-start(bf16[256,1024]{1,0:T(8,128)(2,1)} %add_convert_fusion.5), channel_id=1, source_target_pairs={{0,2},{1,3},{2,0},{3,1},{4,6},{5,7},{6,4},{7,5},{8,10},{9,11},{10,... | collective-permute-start | bytes 1572872 | tf_op jit(solution)/shard_map/ppermute | solution.py:320
  175.8 29.7 %collective-permute-start.23 = (bf16[512,512]{1,0:T(8,128)(2,1)}, bf16[512,512]{1,0:T(8,128)(2,1)}, u32[]{:S(2)}, u32[]{:S(2)}) collective-permute-start(bf16[512,512]{1,0:T(8,128)(2,1)} %constant_dynamic-slice_fusion.2), channel_id=1, source_target_pairs={{0,4},{4,0},{8,12},{12,8},{16,20},{20,16},{24,28},{28,24},{1,5},{5... | collective-permute-start | bytes 1572872 | tf_op jit(solution)/shard_map/ppermute | solution.py:320
  179.9 24.1 %collective-permute-start.25 = (bf16[256,768]{1,0:T(8,128)(2,1)}, bf16[256,768]{1,0:T(8,128)(2,1)}, u32[]{:S(2)}, u32[]{:S(2)}) collective-permute-start(bf16[256,768]{1,0:T(8,128)(2,1)} %add_convert_fusion.7), channel_id=1, source_target_pairs={{0,8},{4,12},{8,0},{12,4},{16,24},{20,28},{24,16},{28,20},{1,9},{5... | collective-permute-start | bytes 1179656 | tf_op jit(solution)/shard_map/ppermute | solution.py:320
  183.2 25.6 %collective-permute-start.31 = (bf16[192,1024]{1,0:T(8,128)(2,1)}, bf16[192,1024]{1,0:T(8,128)(2,1)}, u32[]{:S(2)}, u32[]{:S(2)}) collective-permute-start(bf16[192,1024]{1,0:T(8,128)(2,1)} %pad_maximum_fusion.30), channel_id=1, source_target_pairs={{0,8},{4,12},{8,0},{12,4},{16,24},{20,28},{24,16},{28,20},{1,9},{5... | collective-permute-start | bytes 1179656 | tf_op jit(solution)/shard_map/ppermute | solution.py:320
  186.7 21.4 %collective-permute-start.32 = (bf16[128,768]{1,0:T(8,128)(2,1)S(1)}, bf16[128,768]{1,0:T(8,128)(2,1)S(1)}, u32[]{:S(2)}, u32[]{:S(2)}) collective-permute-start(bf16[128,768]{1,0:T(8,128)(2,1)S(1)} %add_convert_fusion.15), channel_id=1, source_target_pairs={{0,16},{4,20},{8,24},{12,28},{16,0},{20,4},{24,8},{28,12},{1,17},{... | collective-permute-start | bytes 589832 | tf_op jit(solution)/shard_map/ppermute | solution.py:320
  204.1 12.5 %collective-permute-start.30 = (bf16[128,1024]{1,0:T(8,128)(2,1)}, bf16[128,1024]{1,0:T(8,128)(2,1)S(1)}, u32[]{:S(2)}, u32[]{:S(2)}) collective-permute-start(bf16[128,1024]{1,0:T(8,128)(2,1)} %add_convert_fusion.12), channel_id=1, source_target_pairs={{0,8},{4,12},{8,0},{12,4},{16,24},{20,28},{24,16},{28,20},{1,9},{5... | collective-permute-start | bytes 786440 | tf_op jit(solution)/shard_map/ppermute | solution.py:320
  205.5 15.6 %collective-permute-start.36 = (bf16[128,768]{1,0:T(8,128)(2,1)S(1)}, bf16[128,768]{1,0:T(8,128)(2,1)S(1)}, u32[]{:S(2)}, u32[]{:S(2)}) collective-permute-start(bf16[128,768]{1,0:T(8,128)(2,1)S(1)} %add_convert_fusion.14), channel_id=1, source_target_pairs={{0,16},{4,20},{8,24},{12,28},{16,0},{20,4},{24,8},{28,12},{1,17},{... | collective-permute-start | bytes 589832 | tf_op jit(solution)/shard_map/ppermute | solution.py:320
  208.1 20.9 %collective-permute-start.35 = (bf16[512,512]{1,0:T(8,128)(2,1)S(1)}, bf16[512,512]{1,0:T(8,128)(2,1)S(1)}, u32[]{:S(2)}, u32[]{:S(2)}) collective-permute-start(bf16[512,512]{1,0:T(8,128)(2,1)S(1)} %constant_dynamic-slice_fusion.1), channel_id=1, source_target_pairs={{0,8},{4,12},{8,0},{12,4},{16,24},{20,28},{24,16},{28,20},{1,9},{5... | collective-permute-start | bytes 1572872 | tf_op jit(solution)/shard_map/ppermute | solution.py:320
  220.5 21.4 %collective-permute-start.33 = (bf16[2,1,256,1024]{3,2,1,0:T(8,128)(2,1)S(1)}, bf16[2,1,256,1024]{3,2,1,0:T(8,128)(2,1)S(1)}, u32[]{:S(2)}, u32[]{:S(2)}) collective-permute-start(bf16[2,1,256,1024]{3,2,1,0:T(8,128)(2,1)S(1)} %constant_dynamic-slice_fusion), channel_id=1, source_target_pairs={{0,1},{1,0},{2,3},{3,2},{4,5},{5,4},{6,7},{7,6},{8,9},{9,8},{10,11... | collective-permute-start | bytes 3145736 | tf_op jit(solution)/shard_map/ppermute | solution.py:320
  221.1 17.2 %collective-permute-start.38 = (bf16[256,768]{1,0:T(8,128)(2,1)S(1)}, bf16[256,768]{1,0:T(8,128)(2,1)S(1)}, u32[]{:S(2)}, u32[]{:S(2)}) collective-permute-start(bf16[256,768]{1,0:T(8,128)(2,1)S(1)} %pad_maximum_fusion.31), channel_id=1, source_target_pairs={{0,8},{4,12},{8,0},{12,4},{16,24},{20,28},{24,16},{28,20},{1,9},{5... | collective-permute-start | bytes 1179656 | tf_op jit(solution)/shard_map/ppermute | solution.py:320
  221.1 14.4 %collective-permute-start.34 = (bf16[64,1024]{1,0:T(8,128)(2,1)S(1)}, bf16[64,1024]{1,0:T(8,128)(2,1)S(1)}, u32[]{:S(2)}, u32[]{:S(2)}) collective-permute-start(bf16[64,1024]{1,0:T(8,128)(2,1)S(1)} %add_convert_fusion.24), channel_id=1, source_target_pairs={{0,16},{4,20},{8,24},{12,28},{16,0},{20,4},{24,8},{28,12},{1,17},{... | collective-permute-start | bytes 393224 | tf_op jit(solution)/shard_map/ppermute | solution.py:320
  229.0 16.1 %collective-permute-start.29 = (bf16[256,512]{1,0:T(8,128)(2,1)S(1)}, bf16[256,512]{1,0:T(8,128)(2,1)S(1)}, u32[]{:S(2)}, u32[]{:S(2)}) collective-permute-start(bf16[256,512]{1,0:T(8,128)(2,1)S(1)} %add_convert_fusion.11), channel_id=1, source_target_pairs={{0,8},{4,12},{8,0},{12,4},{16,24},{20,28},{24,16},{28,20},{1,9},{5... | collective-permute-start | bytes 786440 | tf_op jit(solution)/shard_map/ppermute | solution.py:320
  235.6 24.5 %collective-permute-start.39 = (bf16[384,1024]{1,0:T(8,128)(2,1)S(1)}, bf16[384,1024]{1,0:T(8,128)(2,1)S(1)}, u32[]{:S(2)}, u32[]{:S(2)}) collective-permute-start(bf16[384,1024]{1,0:T(8,128)(2,1)S(1)} %pad_maximum_fusion.22), channel_id=1, source_target_pairs={{0,4},{4,0},{8,12},{12,8},{16,20},{20,16},{24,28},{28,24},{1,5},{5... | collective-permute-start | bytes 2359304 | tf_op jit(solution)/shard_map/ppermute | solution.py:320
  238.3 20.2 %collective-permute-start.40 = (bf16[128,768]{1,0:T(8,128)(2,1)S(1)}, bf16[128,768]{1,0:T(8,128)(2,1)S(1)}, u32[]{:S(2)}, u32[]{:S(2)}) collective-permute-start(bf16[128,768]{1,0:T(8,128)(2,1)S(1)} %add_convert_fusion.13), channel_id=1, source_target_pairs={{0,16},{4,20},{8,24},{12,28},{16,0},{20,4},{24,8},{28,12},{1,17},{... | collective-permute-start | bytes 589832 | tf_op jit(solution)/shard_map/ppermute | solution.py:320
  242.0 26.4 %collective-permute-start.44 = (bf16[256,512]{1,0:T(8,128)(2,1)S(1)}, bf16[256,512]{1,0:T(8,128)(2,1)S(1)}, u32[]{:S(2)}, u32[]{:S(2)}) collective-permute-start(bf16[256,512]{1,0:T(8,128)(2,1)S(1)} %add_convert_fusion.10), channel_id=1, source_target_pairs={{0,16},{4,20},{8,24},{12,28},{16,0},{20,4},{24,8},{28,12},{1,17},{... | collective-permute-start | bytes 786440 | tf_op jit(solution)/shard_map/ppermute | solution.py:320
  245.2 27.5 %collective-permute-start.42 = (bf16[64,1024]{1,0:T(8,128)(2,1)S(1)}, bf16[64,1024]{1,0:T(8,128)(2,1)S(1)}, u32[]{:S(2)}, u32[]{:S(2)}) collective-permute-start(bf16[64,1024]{1,0:T(8,128)(2,1)S(1)} %add_convert_fusion.23), channel_id=1, source_target_pairs={{0,16},{4,20},{8,24},{12,28},{16,0},{20,4},{24,8},{28,12},{1,17},{... | collective-permute-start | bytes 393224 | tf_op jit(solution)/shard_map/ppermute | solution.py:320
  246.5 31.5 %collective-permute-start.50 = (bf16[512,768]{1,0:T(8,128)(2,1)S(1)}, bf16[512,768]{1,0:T(8,128)(2,1)S(1)}, u32[]{:S(2)}, u32[]{:S(2)}) collective-permute-start(bf16[512,768]{1,0:T(8,128)(2,1)S(1)} %pad_maximum_fusion.23), channel_id=1, source_target_pairs={{0,4},{4,0},{8,12},{12,8},{16,20},{20,16},{24,28},{28,24},{1,5},{5... | collective-permute-start | bytes 2359304 | tf_op jit(solution)/shard_map/ppermute | solution.py:320
  258.5 9.2 %collective-permute-start.37 = (bf16[256,1024]{1,0:T(8,128)(2,1)S(1)}, bf16[256,1024]{1,0:T(8,128)(2,1)S(1)}, u32[]{:S(2)}, u32[]{:S(2)}) collective-permute-start(bf16[256,1024]{1,0:T(8,128)(2,1)S(1)} %fusion.23), channel_id=1, source_target_pairs={{0,2},{1,3},{2,0},{3,1},{4,6},{5,7},{6,4},{7,5},{8,10},{9,11},{10,... | collective-permute-start | bytes 1572872 | tf_op jit(solution)/shard_map/ppermute | solution.py:320
  260.1 11.3 %collective-permute-start.43 = (bf16[256,768]{1,0:T(8,128)(2,1)S(1)}, bf16[256,768]{1,0:T(8,128)(2,1)S(1)}, u32[]{:S(2)}, u32[]{:S(2)}) collective-permute-start(bf16[256,768]{1,0:T(8,128)(2,1)S(1)} %pad_maximum_fusion.32), channel_id=1, source_target_pairs={{0,8},{4,12},{8,0},{12,4},{16,24},{20,28},{24,16},{28,20},{1,9},{5... | collective-permute-start | bytes 1179656 | tf_op jit(solution)/shard_map/ppermute | solution.py:320
  267.7 7.8 %collective-permute-start.46 = (bf16[128,512]{1,0:T(8,128)(2,1)S(1)}, bf16[128,512]{1,0:T(8,128)(2,1)S(1)}, u32[]{:S(2)}, u32[]{:S(2)}) collective-permute-start(bf16[128,512]{1,0:T(8,128)(2,1)S(1)} %add_convert_fusion.22), channel_id=1, source_target_pairs={{0,16},{4,20},{8,24},{12,28},{16,0},{20,4},{24,8},{28,12},{1,17},{... | collective-permute-start | bytes 393224 | tf_op jit(solution)/shard_map/ppermute | solution.py:320
  268.4 6.9 %collective-permute-start.41 = (f32[2304]{0:T(1024)S(1)}, f32[2304]{0:T(1024)S(1)}, u32[]{:S(2)}, u32[]{:S(2)}) collective-permute-start(f32[2304]{0:T(1024)S(1)} %pad_maximum_fusion.36), channel_id=1, source_target_pairs={{0,1},{1,0},{2,3},{3,2},{4,5},{5,4},{6,7},{7,6},{8,9},{9,8},{10,11... | collective-permute-start | bytes 27656 | tf_op jit(solution)/shard_map/ppermute | solution.py:320
  271.4 12.6 %collective-permute-start.48 = (bf16[128,512]{1,0:T(8,128)(2,1)S(1)}, bf16[128,512]{1,0:T(8,128)(2,1)S(1)}, u32[]{:S(2)}, u32[]{:S(2)}) collective-permute-start(bf16[128,512]{1,0:T(8,128)(2,1)S(1)} %add_convert_fusion.21), channel_id=1, source_target_pairs={{0,4},{4,0},{8,12},{12,8},{16,20},{20,16},{24,28},{28,24},{1,5},{5... | collective-permute-start | bytes 393224 | tf_op jit(solution)/shard_map/ppermute | solution.py:320
  272.6 44.1 %collective-permute-start.54 = (bf16[512,768]{1,0:T(8,128)(2,1)S(1)}, bf16[512,768]{1,0:T(8,128)(2,1)S(1)}, u32[]{:S(2)}, u32[]{:S(2)}) collective-permute-start(bf16[512,768]{1,0:T(8,128)(2,1)S(1)} %pad_maximum_fusion.24), channel_id=1, source_target_pairs={{0,4},{4,0},{8,12},{12,8},{16,20},{20,16},{24,28},{28,24},{1,5},{5... | collective-permute-start | bytes 2359304 | tf_op jit(solution)/shard_map/ppermute | solution.py:320
  275.3 8.5 %collective-permute-start.49 = (bf16[128,1024]{1,0:T(8,128)(2,1)S(1)}, bf16[128,1024]{1,0:T(8,128)(2,1)S(1)}, u32[]{:S(2)}, u32[]{:S(2)}) collective-permute-start(bf16[128,1024]{1,0:T(8,128)(2,1)S(1)} %pad_maximum_fusion.33), channel_id=1, source_target_pairs={{0,8},{4,12},{8,0},{12,4},{16,24},{20,28},{24,16},{28,20},{1,9},{5... | collective-permute-start | bytes 786440 | tf_op jit(solution)/shard_map/ppermute | solution.py:320
  275.4 11.0 %collective-permute-start.45 = (f32[2304]{0:T(1024)S(1)}, f32[2304]{0:T(1024)S(1)}, u32[]{:S(2)}, u32[]{:S(2)}) collective-permute-start(f32[2304]{0:T(1024)S(1)} %fusion.31), channel_id=1, source_target_pairs={{0,2},{1,3},{2,0},{3,1},{4,6},{5,7},{6,4},{7,5},{8,10},{9,11},{10,... | collective-permute-start | bytes 27656 | tf_op jit(solution)/shard_map/ppermute | solution.py:320
  277.9 8.4 %collective-permute-start.47 = (bf16[128,512]{1,0:T(8,128)(2,1)S(1)}, bf16[128,512]{1,0:T(8,128)(2,1)S(1)}, u32[]{:S(2)}, u32[]{:S(2)}) collective-permute-start(bf16[128,512]{1,0:T(8,128)(2,1)S(1)} %add_convert_fusion.20), channel_id=1, source_target_pairs={{0,16},{4,20},{8,24},{12,28},{16,0},{20,4},{24,8},{28,12},{1,17},{... | collective-permute-start | bytes 393224 | tf_op jit(solution)/shard_map/ppermute | solution.py:320
  284.1 10.4 %collective-permute-start.52 = (bf16[128,512]{1,0:T(8,128)(2,1)S(1)}, bf16[128,512]{1,0:T(8,128)(2,1)S(1)}, u32[]{:S(2)}, u32[]{:S(2)}) collective-permute-start(bf16[128,512]{1,0:T(8,128)(2,1)S(1)} %add_convert_fusion.19), channel_id=1, source_target_pairs={{0,4},{4,0},{8,12},{12,8},{16,20},{20,16},{24,28},{28,24},{1,5},{5... | collective-permute-start | bytes 393224 | tf_op jit(solution)/shard_map/ppermute | solution.py:320
  286.4 14.2 %collective-permute-start.55 = (bf16[256,512]{1,0:T(8,128)(2,1)S(1)}, bf16[256,512]{1,0:T(8,128)(2,1)S(1)}, u32[]{:S(2)}, u32[]{:S(2)}) collective-permute-start(bf16[256,512]{1,0:T(8,128)(2,1)S(1)} %pad_maximum_fusion.34), channel_id=1, source_target_pairs={{0,8},{4,12},{8,0},{12,4},{16,24},{20,28},{24,16},{28,20},{1,9},{5... | collective-permute-start | bytes 786440 | tf_op jit(solution)/shard_map/ppermute | solution.py:320
  286.5 13.3 %collective-permute-start.51 = (f32[2304]{0:T(1024)S(1)}, f32[2304]{0:T(1024)S(1)}, u32[]{:S(2)}, u32[]{:S(2)}) collective-permute-start(f32[2304]{0:T(1024)S(1)} %add.585), channel_id=1, source_target_pairs={{0,4},{4,0},{8,12},{12,8},{16,20},{20,16},{24,28},{28,24},{1,5},{5... | collective-permute-start | bytes 27656 | tf_op jit(solution)/shard_map/ppermute | solution.py:320
  294.6 14.2 %collective-permute-start.57 = (bf16[256,512]{1,0:T(8,128)(2,1)S(1)}, bf16[256,512]{1,0:T(8,128)(2,1)S(1)}, u32[]{:S(2)}, u32[]{:S(2)}) collective-permute-start(bf16[256,512]{1,0:T(8,128)(2,1)S(1)} %pad_maximum_fusion.35), channel_id=1, source_target_pairs={{0,16},{4,20},{8,24},{12,28},{16,0},{20,4},{24,8},{28,12},{1,17},{... | collective-permute-start | bytes 786440 | tf_op jit(solution)/shard_map/ppermute | solution.py:320
  299.0 15.8 %collective-permute-start.53 = (bf16[256,1024]{1,0:T(8,128)(2,1)S(1)}, bf16[256,1024]{1,0:T(8,128)(2,1)S(1)}, u32[]{:S(2)}, u32[]{:S(2)}) collective-permute-start(bf16[256,1024]{1,0:T(8,128)(2,1)S(1)} %pad_maximum_fusion.27), channel_id=1, source_target_pairs={{0,4},{4,0},{8,12},{12,8},{16,20},{20,16},{24,28},{28,24},{1,5},{5... | collective-permute-start | bytes 1572872 | tf_op jit(solution)/shard_map/ppermute | solution.py:320
  299.8 9.1 %collective-permute-start.56 = (f32[2304]{0:T(1024)S(1)}, f32[2304]{0:T(1024)S(1)}, u32[]{:S(2)}, u32[]{:S(2)}) collective-permute-start(f32[2304]{0:T(1024)S(1)} %add.586), channel_id=1, source_target_pairs={{0,8},{4,12},{8,0},{12,4},{16,24},{20,28},{24,16},{28,20},{1,9},{5... | collective-permute-start | bytes 27656 | tf_op jit(solution)/shard_map/ppermute | solution.py:320
  308.9 4.8 %collective-permute-start.59 = (f32[2304]{0:T(1024)S(1)}, f32[2304]{0:T(1024)S(1)}, u32[]{:S(2)}, u32[]{:S(2)}) collective-permute-start(f32[2304]{0:T(1024)S(1)} %add.587), channel_id=1, source_target_pairs={{0,16},{4,20},{8,24},{12,28},{16,0},{20,4},{24,8},{28,12},{1,17},{... | collective-permute-start | bytes 27656 | tf_op jit(solution)/shard_map/ppermute | solution.py:320
  309.1 14.3 %collective-permute-start.58 = (bf16[512,512]{1,0:T(8,128)(2,1)S(1)}, bf16[512,512]{1,0:T(8,128)(2,1)S(1)}, u32[]{:S(2)}, u32[]{:S(2)}) collective-permute-start(bf16[512,512]{1,0:T(8,128)(2,1)S(1)} %pad_maximum_fusion.28), channel_id=1, source_target_pairs={{0,4},{4,0},{8,12},{12,8},{16,20},{20,16},{24,28},{28,24},{1,5},{5... | collective-permute-start | bytes 1572872 | tf_op jit(solution)/shard_map/ppermute | solution.py:320
  309.9 15.3 %collective-permute-start.60 = (bf16[512,512]{1,0:T(8,128)(2,1)S(1)}, bf16[512,512]{1,0:T(8,128)(2,1)S(1)}, u32[]{:S(2)}, u32[]{:S(2)}) collective-permute-start(bf16[512,512]{1,0:T(8,128)(2,1)S(1)} %pad_maximum_fusion.29), channel_id=1, source_target_pairs={{0,8},{4,12},{8,0},{12,4},{16,24},{20,28},{24,16},{28,20},{1,9},{5... | collective-permute-start | bytes 1572872 | tf_op jit(solution)/shard_map/ppermute | solution.py:320
  (57 other events, 266.8 us)
